TPU v7x, 32 devices: a whole 2x2x4 slice. The times are simulated.
32 devices in a mesh: seq: 2 (over core), batch: 16 (over z, y, x).
Axes of the slice: x: 2, y: 2, z: 4, core: 2. Of those that a mesh axis runs over, the one named last changes fastest.
Arguments:
- first_layer_input: bfloat16 [48, 512, 768], P('batch', 'seq'), may hold values from -6 to 6
- output_gradient: bfloat16 [48, 512, 768], P('batch', 'seq'), may hold values from -6 to 6
- sentence_pair_index: int32 [48, 512], P('batch', 'seq'), may hold values from 0 to 15, never falling along the last dimension, each value on 1 to 96 neighbouring positions
- sequence_live_length: int32 [48], P('batch'), may hold values from 256 to 512, as said below
- optimizer_step_count: int32 [2, 2, 2], replicated, may hold values from 1 to 4
- query_key_value_weight: bfloat16 [2, 768, 2304], replicated, may hold values from -0.21875 to 0.21875
- attention_output_weight: bfloat16 [2, 768, 768], replicated, may hold values from -0.4375 to 0.4375
- feedforward_up_weight: bfloat16 [2, 768, 3072], replicated, may hold values from -0.21875 to 0.21875
- feedforward_down_weight: bfloat16 [2, 3072, 768], replicated, may hold values from -0.109375 to 0.109375
- layer_bias_gain_rows: bfloat16 [2, 8, 768], replicated, may hold values from -1.5 to 1.5, as said below
- feedforward_up_bias: bfloat16 [2, 3072], replicated, may hold values from -3 to 3
- adapter_down_factors: float32 [2, 2, 8, 768], replicated, may hold values from -0.21875 to 0.21875
- adapter_up_factors: float32 [2, 2, 768, 8], replicated, may hold values from -1 to 1
- first_moment_down: float32 [2, 2, 8, 768], replicated, may hold values from -0.046875 to 0.046875
- second_moment_down: float32 [2, 2, 8, 768], replicated, may hold values from 8.138021e-07 to 2.0345053e-05
- first_moment_up: float32 [2, 2, 768, 8], replicated, may hold values from -0.046875 to 0.046875
- second_moment_up: float32 [2, 2, 768, 8], replicated, may hold values from 8.138021e-07 to 2.0345053e-05
Outputs:
- hidden_out: bfloat16 [48, 512, 768], P('batch', 'seq')
- grad_in: float32 [48, 512, 768], P('batch', 'seq')
- updated_down_factors: float32 [2, 2, 8, 768], replicated
- updated_up_factors: float32 [2, 2, 768, 8], replicated
- updated_first_moment_down: float32 [2, 2, 8, 768], replicated
- updated_second_moment_down: float32 [2, 2, 8, 768], replicated
- updated_first_moment_up: float32 [2, 2, 768, 8], replicated
- updated_second_moment_up: float32 [2, 2, 768, 8], replicated
Inputs may be any that keep to these rules, and one draw needn't show every extreme that they name: `sentence_pair_index`: ids never fall along a sequence; each sentence pair covers at most 96 positions. `sequence_live_length`: every sequence has 256 live positions or more, and some sequence has all 512. `layer_bias_gain_rows`: rows 4 and 6 lie between 0.55 and 1.45.
All inputs are finite; a program needn't handle non-finite values.
Results may differ from a plain program's by a relative error of at most 0.04.
Values may be sent and summed in bfloat16 or wider, within the bound.
No kernel may reach another device: no remote copies, remote signals or barrier semaphores. Data moves between devices by JAX's collectives and lax.ppermute only.
A program may use at most 256 MiB of HBM per device.

v0:
```python
import math

import jax
import jax.numpy as jnp
from jax import lax
from jax.sharding import PartitionSpec as P

HEADS = 12
ENCODER_LAYERS = 2


MASKED = -1000000000.0


def matmul(left_side, right_side):
    return jnp.dot(left_side, right_side, preferred_element_type=jnp.float32)


def normalize_keep(values, gain_row, shift_row):
    center = values - jnp.mean(values, axis=-1, keepdims=True)
    spread = jnp.mean(center * center, axis=-1, keepdims=True)
    inverse = lax.rsqrt(spread + 1e-05)
    scaled = center * inverse
    return (scaled * gain_row + shift_row, scaled, inverse)


def normalize_back(gradient, scaled, inverse, gain_row):
    inner = gradient * gain_row
    return inverse * (
        inner
        - jnp.mean(inner, axis=-1, keepdims=True)
        - scaled * jnp.mean(inner * scaled, axis=-1, keepdims=True)
    )


def head_scores(query_heads, key_heads, allowed, scaling):
    raw = (
        jnp.einsum("sqhe,skhe->shqk", query_heads, key_heads, preferred_element_type=jnp.float32)
        * scaling
    )
    return jnp.where(allowed, raw, MASKED)


def gelu_exact(values):
    return jax.nn.gelu(values, approximate=False)


def adamw_step_update(weight, gradient, moment, velocity, bias_correction, learn_rate, decay_rate):
    moment = 0.5 * moment + 0.5 * gradient
    velocity = 0.5 * velocity + 0.5 * gradient * gradient
    step_size = moment / bias_correction / (jnp.sqrt(velocity / bias_correction) + 1e-08)
    return (weight - learn_rate * (step_size + decay_rate * weight), moment, velocity)


def shards(
    first_layer_input,
    output_gradient,
    sentence_pair_index,
    sequence_live_length,
    optimizer_step_count,
    query_key_value_weight,
    attention_output_weight,
    feedforward_up_weight,
    feedforward_down_weight,
    layer_bias_gain_rows,
    feedforward_up_bias,
    adapter_down_factors,
    adapter_up_factors,
    first_moment_down,
    second_moment_down,
    first_moment_up,
    second_moment_up,
):
    sequences, local_len, model_width = first_layer_input.shape
    halves = lax.axis_size("seq")
    seq_width = local_len * halves
    head_width = model_width // HEADS
    scaling = 1.0 / math.sqrt(head_width)
    offset = lax.axis_index("seq") * local_len
    own_places = offset + jnp.arange(local_len, dtype=jnp.int32)
    all_places = jnp.arange(seq_width, dtype=jnp.int32)
    doc_keys = lax.all_gather(sentence_pair_index, "seq", axis=1, tiled=True)
    key_span = all_places.shape[0]
    live_keys = (all_places[None, :] >= 0) & (all_places[None, :] < sequence_live_length[:, None])
    same_doc = sentence_pair_index[:, :, None] == doc_keys[:, None, :]
    itself = own_places[:, None] == all_places[None, :]
    allowed = (same_doc & (live_keys[:, None, :] | itself[None]))[:, None]
    live_rows = (own_places[None, :] < sequence_live_length[:, None]).astype(jnp.float32)[
        :, :, None
    ]
    vectors = layer_bias_gain_rows.astype(jnp.float32)
    bias_up = feedforward_up_bias.astype(jnp.float32)

    def split_heads(values, rows):
        return values.reshape(sequences, rows, HEADS, head_width)

    def join_heads(values, rows):
        return values.reshape(sequences, rows, model_width)

    current = first_layer_input.astype(jnp.float32)
    stored = []
    for layer_number in range(ENCODER_LAYERS):
        vec_now = vectors[layer_number]
        down_adapter_path = adapter_down_factors[layer_number].astype(jnp.bfloat16)
        up_adapter_path = adapter_up_factors[layer_number].astype(jnp.bfloat16)
        layer_in = current.astype(jnp.bfloat16)
        joined = matmul(layer_in, query_key_value_weight[layer_number])
        inner_query = matmul(layer_in, down_adapter_path[0].T).astype(jnp.bfloat16)
        inner_value = matmul(layer_in, down_adapter_path[1].T).astype(jnp.bfloat16)
        queries = (
            joined[..., :model_width] + vec_now[0] + 2.0 * matmul(inner_query, up_adapter_path[0].T)
        ).astype(jnp.bfloat16)
        key_rows = joined[..., model_width : 2 * model_width].astype(jnp.bfloat16)
        values = (
            joined[..., 2 * model_width :]
            + vec_now[1]
            + 2.0 * matmul(inner_value, up_adapter_path[1].T)
        ).astype(jnp.bfloat16)
        keys_all, values_all = (
            lax.all_gather(key_rows, "seq", axis=1, tiled=True),
            lax.all_gather(values, "seq", axis=1, tiled=True),
        )
        key_heads = split_heads(keys_all, key_span)
        value_heads = split_heads(values_all, key_span)
        scores = head_scores(split_heads(queries, local_len), key_heads, allowed, scaling)
        row_max = jnp.max(scores, axis=-1, keepdims=True)
        shifted = jnp.exp(scores - row_max)
        row_sum = jnp.sum(shifted, axis=-1, keepdims=True)
        probs_low = (shifted / row_sum).astype(jnp.bfloat16)
        log_total = row_max + jnp.log(row_sum)
        mixture = jnp.einsum(
            "shqk,skhe->sqhe", probs_low, value_heads, preferred_element_type=jnp.float32
        )
        mixture = join_heads(mixture, local_len).astype(jnp.bfloat16)
        attended = matmul(mixture, attention_output_weight[layer_number]) + vec_now[2] + current
        normed_one, one_scaled, one_inverse = normalize_keep(attended, vec_now[4], vec_now[5])
        gate_in = (
            matmul(normed_one.astype(jnp.bfloat16), feedforward_up_weight[layer_number])
            + bias_up[layer_number]
        )
        active = gelu_exact(gate_in).astype(jnp.bfloat16)
        summed_two = matmul(active, feedforward_down_weight[layer_number]) + vec_now[3] + normed_one
        current, two_scaled, two_inverse = normalize_keep(summed_two, vec_now[6], vec_now[7])
        stored.append(
            (
                layer_in,
                inner_query,
                inner_value,
                queries,
                key_heads,
                value_heads,
                log_total,
                one_scaled,
                one_inverse,
                gate_in,
                two_scaled,
                two_inverse,
            )
        )
    gradient = output_gradient.astype(jnp.float32) * live_rows
    layer_grads_a = [None] * ENCODER_LAYERS
    layer_grads_b = [None] * ENCODER_LAYERS
    for layer_number in reversed(range(ENCODER_LAYERS)):
        (
            layer_in,
            inner_query,
            inner_value,
            queries,
            key_heads,
            value_heads,
            log_total,
            one_scaled,
            one_inverse,
            gate_in,
            two_scaled,
            two_inverse,
        ) = stored[layer_number]
        vec_now = vectors[layer_number]
        down_adapter_path = adapter_down_factors[layer_number].astype(jnp.bfloat16)
        up_adapter_path = adapter_up_factors[layer_number].astype(jnp.bfloat16)
        d_two = normalize_back(gradient, two_scaled, two_inverse, vec_now[6])
        d_active = matmul(d_two.astype(jnp.bfloat16), feedforward_down_weight[layer_number].T)
        d_gate = jax.vjp(gelu_exact, gate_in)[1](d_active)[0].astype(jnp.bfloat16)
        d_one = d_two + matmul(d_gate, feedforward_up_weight[layer_number].T)
        d_att = normalize_back(d_one, one_scaled, one_inverse, vec_now[4])
        d_mix = matmul(d_att.astype(jnp.bfloat16), attention_output_weight[layer_number].T).astype(
            jnp.bfloat16
        )
        query_heads = split_heads(queries, local_len)
        d_out_heads = split_heads(d_mix, local_len)
        scores = head_scores(query_heads, key_heads, allowed, scaling)
        probs = jnp.exp(scores - log_total)
        d_probs = jnp.einsum(
            "sqhe,skhe->shqk", d_out_heads, value_heads, preferred_element_type=jnp.float32
        )
        delta = jnp.sum(d_probs * probs, axis=-1, keepdims=True)
        d_scores = (probs * (d_probs - delta)).astype(jnp.bfloat16)
        d_queries = (
            jnp.einsum("shqk,skhe->sqhe", d_scores, key_heads, preferred_element_type=jnp.float32)
            * scaling
        )
        key_terms = (
            jnp.einsum("shqk,sqhe->skhe", d_scores, query_heads, preferred_element_type=jnp.float32)
            * scaling
        )
        value_terms = jnp.einsum(
            "shqk,sqhe->skhe",
            probs.astype(jnp.bfloat16),
            d_out_heads,
            preferred_element_type=jnp.float32,
        )
        d_keys, d_values = (
            lax.psum_scatter(
                join_heads(key_terms, seq_width).astype(jnp.bfloat16),
                "seq",
                scatter_dimension=1,
                tiled=True,
            ).astype(jnp.float32),
            lax.psum_scatter(
                join_heads(value_terms, seq_width).astype(jnp.bfloat16),
                "seq",
                scatter_dimension=1,
                tiled=True,
            ).astype(jnp.float32),
        )
        d_queries = join_heads(d_queries, local_len).astype(jnp.bfloat16)
        d_keys = d_keys.astype(jnp.bfloat16)
        d_values = d_values.astype(jnp.bfloat16)
        d_inner_query = (2.0 * matmul(d_queries, up_adapter_path[0])).astype(jnp.bfloat16)
        d_inner_value = (2.0 * matmul(d_values, up_adapter_path[1])).astype(jnp.bfloat16)
        grad_query_up = 2.0 * jnp.einsum(
            "spd,spr->dr", d_queries, inner_query, preferred_element_type=jnp.float32
        )
        grad_value_up = 2.0 * jnp.einsum(
            "spd,spr->dr", d_values, inner_value, preferred_element_type=jnp.float32
        )
        grad_query_down = jnp.einsum(
            "spr,spd->rd", d_inner_query, layer_in, preferred_element_type=jnp.float32
        )
        grad_value_down = jnp.einsum(
            "spr,spd->rd", d_inner_value, layer_in, preferred_element_type=jnp.float32
        )
        d_joined = jnp.concatenate([d_queries, d_keys, d_values], axis=-1)
        gradient = (
            d_att
            + matmul(d_joined, query_key_value_weight[layer_number].T)
            + matmul(d_inner_query, down_adapter_path[0])
            + matmul(d_inner_value, down_adapter_path[1])
        )
        layer_a = jnp.stack([grad_query_down, grad_value_down])
        layer_b = jnp.stack([grad_query_up, grad_value_up])
        layer_grads_a[layer_number] = layer_a
        layer_grads_b[layer_number] = layer_b
    down_gradient_total = jnp.stack(layer_grads_a)
    up_gradient_total = jnp.stack(layer_grads_b)
    down_gradient_total, up_gradient_total = lax.psum(
        (down_gradient_total, up_gradient_total), ("seq", "batch")
    )
    token_slot_count = sequences * seq_width * lax.axis_size("batch")
    corrections = 1.0 - jnp.power(0.5, optimizer_step_count.astype(jnp.float32))
    correction_down = corrections[:, :, 0][:, :, None, None]
    correction_up = corrections[:, :, 1][:, :, None, None]
    updated_down_factors, updated_first_moment_down, updated_second_moment_down = adamw_step_update(
        adapter_down_factors,
        down_gradient_total / token_slot_count,
        first_moment_down,
        second_moment_down,
        correction_down,
        0.03125,
        0.1,
    )
    updated_up_factors, updated_first_moment_up, updated_second_moment_up = adamw_step_update(
        adapter_up_factors,
        up_gradient_total / token_slot_count,
        first_moment_up,
        second_moment_up,
        correction_up,
        0.5,
        0.0,
    )
    return (
        current.astype(jnp.bfloat16),
        gradient,
        updated_down_factors,
        updated_up_factors,
        updated_first_moment_down,
        updated_second_moment_down,
        updated_first_moment_up,
        updated_second_moment_up,
    )


def solution(mesh):
    return jax.shard_map(
        shards,
        mesh=mesh,
        in_specs=(
            P("batch", "seq", None),
            P("batch", "seq", None),
            P("batch", "seq"),
            P("batch"),
            P(),
            P(),
            P(),
            P(),
            P(),
            P(),
            P(),
            P(),
            P(),
            P(),
            P(),
            P(),
            P(),
        ),
        out_specs=(P("batch", "seq", None), P("batch", "seq", None), P(), P(), P(), P(), P(), P()),
        check_vma=False,
    )
```

profile of v0, /device:TPU:0, one launch (start us, length us, event | category | flops | bytes accessed | tf_op | source)
XLA Modules:
  0.0 549.7 jit_solution(9053407577279403554)
XLA Ops:
  33.2 5.6 %fusion.184 = (f32[3,12,256]{2,1,0:T(8,128)S(1)}, f32[3,12,256,512]{3,2,1,0:T(8,128)S(1)}) fusion(bf16[3,256,12,64]{1,3,2,0:T(8,128)(2,1)} %bitcast.286, bf16[3,512,12,64]{1,3,2,0:T(8,128)(2,1)S(1)} %bitcast.276, pred[3,256,512]{2,1,0:T(8,128)(4,1)} %or_and_fusion), kind=kOutput, calls=%fused_computation.308 | convolution fusion | flops 618126336 | bytes 22843392 | tf_op jit(solution)/shard_map/sqhe,skhe->shqk/dot_general | solution.py:38
  38.9 7.3 %copy-done = f32[3,12,256,512]{3,2,1,0:T(8,128)} copy-done((f32[3,12,256,512]{3,2,1,0:T(8,128)}, f32[3,12,256,512]{3,2,1,0:T(8,128)S(1)}, u32[]{:S(2)}) %copy-start) | copy-done | bytes 18874392
  54.3 10.2 %fusion.111 = bf16[3,12,64,256]{3,2,1,0:T(8,128)(2,1)S(1)} fusion(bf16[3,512,12,64]{1,3,2,0:T(8,128)(2,1)S(1)} %bitcast.294, f32[3,12,256,512]{3,2,1,0:T(8,128)} %copy-done, f32[3,12,256]{2,1,0:T(8,128)} %fusion, f32[3,12,256]{2,1,0:T(8,128)} %copy-done.37), kind=kOutput, calls=%fused_computation.170 | convolution fusion | flops 618725376 | bytes 22487040 | tf_op jit(solution)/shard_map/shqk,skhe->sqhe/dot_general | solution.py:131
  66.5 9.1 %fusion.87 = (u8[256,3072]{1,0:T(8,128)(4,1)S(1)}, u8[256,3072]{1,0:T(8,128)(4,1)S(1)}, f32[3,256,3072]{2,1,0:T(8,128)S(1)}) fusion(f32[3072]{0:T(1024)S(1)} %bitcast.302, bf16[2,768,3072]{2,1,0:T(8,128)(2,1)} %param.24, f32[3,256,768]{2,1,0:T(8,128)S(1)} %get-tuple-element.52, f32[768]{0:T(1024)S(1)} %copy-done.106, f32[768]{0:T(1024)S(1)} %get-tuple-element.32, ...), kind=kOutput, calls=%fused_computation.157 | convolution fusion | flops 3658285056 | bytes 18112512 | tf_op jit(solution)/shard_map/dot_general | solution.py:16
  75.7 21.9 %fusion.4 = f32[3,256,3072]{2,1,0:T(8,128)} fusion(f32[3,256,3072]{2,1,0:T(8,128)S(1)} %get-tuple-element.53, f32[3072]{0:T(1024)S(1)} %bitcast.303, u8[256,3072]{1,0:T(8,128)(4,1)S(1)} %get-tuple-element.11, u8[256,3072]{1,0:T(8,128)(4,1)S(1)} %get-tuple-element.10), kind=kLoop, calls=%fused_computation.18 | loop fusion | flops 160432128 | bytes 20459520 | tf_op jit(solution)/shard_map/erfc | solution.py:45
  97.6 9.5 %fusion.186 = (f32[3,256]{1,0:T(4,128)S(1)}, f32[3,256,768]{2,1,0:T(8,128)S(1)}) fusion(f32[768]{0:T(1024)S(1)} %copy-done.106, f32[768]{0:T(1024)S(1)} %get-tuple-element.32, f32[3,256]{1,0:T(4,128)S(1)} %add_rsqrt_fusion.3, f32[3,256,768]{2,1,0:T(8,128)S(1)} %get-tuple-element.52, f32[3,256]{1,0:T(4,128)S(1)} %broadcast_multiply_fusion.11, ...), kind=kOutput, calls=%fused_computation.310 | convolution fusion | flops 3637443840 | bytes 28342272 | tf_op jit(solution)/shard_map/dot_general | solution.py:16
  108.6 5.3 fusion.63
  151.3 9.9 %fusion.110 = bf16[3,12,64,256]{3,2,1,0:T(8,128)(2,1)S(1)} fusion(bf16[3,512,12,64]{1,3,2,0:T(8,128)(2,1)} %bitcast.296, f32[3,12,256,512]{3,2,1,0:T(8,128)} %copy-done.1, f32[3,12,256]{2,1,0:T(8,128)} %copy-done.48, f32[3,12,256]{2,1,0:T(8,128)} %copy-done.39), kind=kOutput, calls=%fused_computation.169 | convolution fusion | flops 618725376 | bytes 22487040 | tf_op jit(solution)/shard_map/shqk,skhe->sqhe/dot_general | solution.py:131
  163.6 9.1 %fusion.88 = (u8[256,3072]{1,0:T(8,128)(4,1)S(1)}, u8[256,3072]{1,0:T(8,128)(4,1)S(1)}, f32[3,256,3072]{2,1,0:T(8,128)S(1)}) fusion(f32[3072]{0:T(1024)S(1)} %bitcast.306, bf16[2,768,3072]{2,1,0:T(8,128)(2,1)} %param.24, f32[3,256,768]{2,1,0:T(8,128)S(1)} %get-tuple-element.59, f32[768]{0:T(1024)S(1)} %copy-done.103, f32[768]{0:T(1024)S(1)} %copy-done.101, ...), kind=kOutput, calls=%fused_computation.158 | convolution fusion | flops 3658285056 | bytes 18112512 | tf_op jit(solution)/shard_map/dot_general | solution.py:16
  172.7 21.9 %fusion.5 = f32[3,256,3072]{2,1,0:T(8,128)} fusion(f32[3,256,3072]{2,1,0:T(8,128)S(1)} %get-tuple-element.60, f32[3072]{0:T(1024)S(1)} %bitcast.307, u8[256,3072]{1,0:T(8,128)(4,1)S(1)} %get-tuple-element.9, u8[256,3072]{1,0:T(8,128)(4,1)S(1)} %get-tuple-element.8), kind=kLoop, calls=%fused_computation.19 | loop fusion | flops 160432128 | bytes 20459520 | tf_op jit(solution)/shard_map/erfc | solution.py:45
  194.6 9.5 %fusion.189 = (f32[3,256]{1,0:T(4,128)S(1)}, f32[3,256,768]{2,1,0:T(8,128)S(1)}) fusion(f32[768]{0:T(1024)S(1)} %copy-done.103, f32[768]{0:T(1024)S(1)} %copy-done.101, f32[3,256]{1,0:T(4,128)S(1)} %add_rsqrt_fusion.1, f32[3,256,768]{2,1,0:T(8,128)S(1)} %get-tuple-element.59, f32[3,256]{1,0:T(4,128)S(1)} %broadcast_multiply_fusion.9, ...), kind=kOutput, calls=%fused_computation.313 | convolution fusion | flops 3637443840 | bytes 28342272 | tf_op jit(solution)/shard_map/dot_general | solution.py:16
  209.0 20.9 %fusion.182 = (f32[3,256]{1,0:T(4,128)}, f32[3,256]{1,0:T(4,128)}, f32[3,256,768]{2,1,0:T(8,128)}) fusion(f32[3,256]{1,0:T(4,128)} %copy-done.83, f32[3,256,768]{2,1,0:T(8,128)} %copy-done.24, f32[3,256]{1,0:T(4,128)} %copy-done.72, f32[768]{0:T(1024)} %get-tuple-element.24, bf16[2,768,3072]{2,1,0:T(8,128)(2,1)} %param.24, f32[3,256,3072]{2,1,0:T(8,128)} %fusion.5, ...), kind=kOutput, calls=%fused_computation.306 | convolution fusion | flops 7298480128 | bytes 40187904 | tf_op jit(solution)/shard_map/dot_general | solution.py:16
  238.9 10.4 %fusion.92 = bf16[3,12,64,512]{3,2,1,0:T(8,128)(2,1)} fusion(bf16[3,256,12,64]{1,3,2,0:T(8,128)(2,1)} %bitcast.290, f32[3,12,256,512]{3,2,1,0:T(8,128)} %copy-done.1, f32[3,12,256]{2,1,0:T(8,128)} %log_add_fusion.1), kind=kOutput, calls=%fused_computation.166 | convolution fusion | flops 614596608 | bytes 22450176 | tf_op jit(solution)/shard_map/shqk,sqhe->skhe/dot_general | solution.py:206
  253.6 14.7 %multiply_reduce_fusion.1 = (f32[3,12,256]{2,1,0:T(8,128)S(1)}, f32[3,12,256,512]{3,2,1,0:T(8,128)}) fusion(f32[3,12,256,512]{3,2,1,0:T(8,128)} %copy-done.1, f32[3,12,256]{2,1,0:T(8,128)} %log_add_fusion.1, bf16[3,256,12,64]{1,3,2,0:T(8,128)(2,1)} %bitcast.291, bf16[3,512,12,64]{1,3,2,0:T(8,128)(2,1)} %bitcast.297), kind=kOutput, calls=%fused_computation.4 | convolution fusion | flops 618126336 | bytes 41361408 | tf_op jit(solution)/shard_map/sqhe,skhe->shqk/dot_general | solution.py:193
  268.3 12.9 %multiply_convert_fusion.1 = bf16[3,12,256,512]{3,2,1,0:T(8,128)(2,1)S(1)} fusion(f32[3,12,256,512]{3,2,1,0:T(8,128)} %get-tuple-element.65, f32[3,12,256,512]{3,2,1,0:T(8,128)} %copy-done.1, f32[3,12,256]{2,1,0:T(8,128)S(1)} %get-tuple-element.64, f32[3,12,256]{2,1,0:T(8,128)S(1)} %copy-done.33), kind=kLoop, calls=%fused_computation.3 | loop fusion | flops 18874368 | bytes 47259648 | tf_op jit(solution)/shard_map/convert_element_type | solution.py:197
  291.3 6.7 %multiply_convert_fusion.9 = bf16[3,12,64,256]{3,2,1,0:T(8,128)(2,1)S(1)} fusion(bf16[3,512,12,64]{1,3,2,0:T(8,128)(2,1)S(1)} %bitcast.279, bf16[3,12,256,512]{3,2,1,0:T(8,128)(2,1)} %copy-done.3), kind=kOutput, calls=%fused_computation.135 | convolution fusion | flops 605159424 | bytes 12976128 | tf_op jit(solution)/shard_map/shqk,skhe->sqhe/dot_general | solution.py:199
  304.8 5.9 %fusion.50 = f32[3,256,768]{2,1,0:T(8,128)S(1)} fusion(bf16[3,256,768]{2,1,0:T(8,128)(2,1)} %reduce-scatter.7.cloned.1.call-done, bf16[3,256,768]{2,1,0:T(8,128)(2,1)} %reduce-scatter.5.cloned.1.call-done, bf16[3,256,768]{2,1,0:T(8,128)(2,1)} %copy.64, bf16[2,768,2304]{2,1,0:T(8,128)(2,1)} %param.22), kind=kOutput, calls=%fused_computation.91 | convolution fusion | flops 2728525824 | bytes 9437184 | tf_op jit(solution)/shard_map/dot_general | solution.py:16
  314.6 18.7 %fusion.180 = (f32[3,256]{1,0:T(4,128)S(1)}, f32[3,256]{1,0:T(4,128)S(1)}, f32[3,256,768]{2,1,0:T(8,128)}) fusion(f32[3,256]{1,0:T(4,128)S(1)} %copy-done.77, f32[3,256,768]{2,1,0:T(8,128)} %copy-done.18, f32[3,256]{1,0:T(4,128)S(1)} %copy-done.66, f32[768]{0:T(1024)S(1)} %copy-done.100, bf16[2,768,3072]{2,1,0:T(8,128)(2,1)} %param.24, ...), kind=kOutput, calls=%fused_computation.304 | convolution fusion | flops 7294941184 | bytes 42530816 | tf_op jit(solution)/shard_map/dot_general | solution.py:16
  338.1 8.1 %fusion.95 = bf16[3,12,64,512]{3,2,1,0:T(8,128)(2,1)S(1)} fusion(bf16[3,256,12,64]{1,3,2,0:T(8,128)(2,1)S(1)} %bitcast.292, f32[3,12,256,512]{3,2,1,0:T(8,128)} %copy-done, f32[3,12,256]{2,1,0:T(8,128)} %log_add_fusion), kind=kOutput, calls=%fused_computation.167 | convolution fusion | flops 614596608 | bytes 22450176 | tf_op jit(solution)/shard_map/shqk,sqhe->skhe/dot_general | solution.py:206
  350.3 18.0 %multiply_reduce_fusion = (f32[3,12,256]{2,1,0:T(8,128)S(1)}, f32[3,12,256,512]{3,2,1,0:T(8,128)}) fusion(f32[3,12,256,512]{3,2,1,0:T(8,128)} %copy-done, f32[3,12,256]{2,1,0:T(8,128)} %log_add_fusion, bf16[3,256,12,64]{1,3,2,0:T(8,128)(2,1)S(1)} %bitcast.293, bf16[3,512,12,64]{1,3,2,0:T(8,128)(2,1)S(1)} %bitcast.295), kind=kOutput, calls=%fused_computation.1 | convolution fusion | flops 618126336 | bytes 41361408 | tf_op jit(solution)/shard_map/sqhe,skhe->shqk/dot_general | solution.py:193
  368.3 13.0 %multiply_convert_fusion = bf16[3,12,256,512]{3,2,1,0:T(8,128)(2,1)S(1)} fusion(f32[3,12,256,512]{3,2,1,0:T(8,128)} %get-tuple-element.69, f32[3,12,256,512]{3,2,1,0:T(8,128)} %copy-done, f32[3,12,256]{2,1,0:T(8,128)S(1)} %get-tuple-element.68, f32[3,12,256]{2,1,0:T(8,128)S(1)} %copy-done.34), kind=kLoop, calls=%fused_computation | loop fusion | flops 18874368 | bytes 47259648 | tf_op jit(solution)/shard_map/convert_element_type | solution.py:197
  393.1 8.5 %multiply_convert_fusion.8 = bf16[3,12,64,256]{3,2,1,0:T(8,128)(2,1)} fusion(bf16[3,512,12,64]{1,3,2,0:T(8,128)(2,1)S(1)} %bitcast.277, bf16[3,12,256,512]{3,2,1,0:T(8,128)(2,1)} %copy-done.2), kind=kOutput, calls=%fused_computation.128 | convolution fusion | flops 605159424 | bytes 12976128 | tf_op jit(solution)/shard_map/shqk,skhe->sqhe/dot_general | solution.py:199
  415.0 5.9 %fusion.56 = f32[3,256,768]{2,1,0:T(8,128)S(1)} fusion(bf16[3,256,768]{2,1,0:T(8,128)(2,1)} %reduce-scatter.11.cloned.1.call-done, bf16[3,256,768]{2,1,0:T(8,128)(2,1)} %reduce-scatter.9.cloned.1.call-done, bf16[3,256,768]{2,1,0:T(8,128)(2,1)} %copy.69, bf16[2,768,2304]{2,1,0:T(8,128)(2,1)} %param.22), kind=kOutput, calls=%fused_computation.97 | convolution fusion | flops 2728525824 | bytes 9437184 | tf_op jit(solution)/shard_map/dot_general | solution.py:16
  424.3 115.3 %all-reduce.3.cloned.1.call-done = (f32[2,2,8,768]{3,2,1,0:T(8,128)}, f32[2,2,768,8]{2,3,1,0:T(8,128)}) async-done(((f32[2,2,8,768]{3,2,1,0:T(8,128)}, f32[2,2,768,8]{2,3,1,0:T(8,128)}), (f32[2,2,8,768]{3,2,1,0:T(8,128)}, f32[2,2,768,8]{2,3,1,0:T(8,128)})) %all-reduce.3.cloned.1.call-update) | async-done | bytes 196624 | tf_op jit(solution)/shard_map/psum | solution.py:256
  (343 shorter events, 155.8 us)
Async XLA Ops:
  7.2 23.2 %all-gather.7.cloned.1.call-start = ((), (), s32[]{:S(2)}) async-start(), calls=%async_computation.5 | async-start | bytes 3538944 | tf_op jit(solution)/shard_map/all_gather | solution.py:120
  16.6 34.8 %all-gather.5.cloned.1.call-start = ((), (), s32[]{:S(2)}) async-start(), calls=%async_computation.4 | async-start | bytes 3538944 | tf_op jit(solution)/shard_map/all_gather | solution.py:121
  17.4 80.1 %copy-start.99 = (f32[768]{0:T(1024)}, f32[768]{0:T(1024)S(1)}, u32[]{:S(2)}) copy-start(f32[768]{0:T(1024)S(1)} %get-tuple-element.32) | copy-start | bytes 9220
  21.1 109.4 %all-gather.11.cloned.1.call-start = ((), (), s32[]{:S(2)}) async-start(), calls=%async_computation.7 | async-start | bytes 3538944 | tf_op jit(solution)/shard_map/all_gather | solution.py:120
  29.3 68.3 %copy-start.62 = (f32[1,3072]{1,0:T(1,128)}, f32[1,3072]{1,0:T(1,128)S(1)}, u32[]{:S(2)}) copy-start(f32[1,3072]{1,0:T(1,128)S(1)} %get-tuple-element.48) | copy-start | bytes 36868
  65.8 31.7 %copy-start.18 = (f32[3,256,768]{2,1,0:T(8,128)}, f32[3,256,768]{2,1,0:T(8,128)S(1)}, u32[]{:S(2)}) copy-start(f32[3,256,768]{2,1,0:T(8,128)S(1)} %get-tuple-element.52) | copy-start | bytes 7077892
  65.9 31.7 %copy-start.65 = (f32[3,256]{1,0:T(4,128)}, f32[3,256]{1,0:T(4,128)S(1)}, u32[]{:S(2)}) copy-start(f32[3,256]{1,0:T(4,128)S(1)} %broadcast_multiply_fusion.11) | copy-start | bytes 9220
  107.6 53.6 %copy-start.70 = (f32[3,256]{1,0:T(4,128)}, f32[3,256]{1,0:T(4,128)S(1)}, u32[]{:S(2)}) copy-start(f32[3,256]{1,0:T(4,128)S(1)} %add_rsqrt_fusion.2) | copy-start | bytes 9220
  118.0 28.9 %all-gather.9.cloned.1.call-start = ((), (), s32[]{:S(2)}) async-start(), calls=%async_computation.6 | async-start | bytes 3538944 | tf_op jit(solution)/shard_map/all_gather | solution.py:121
  123.1 179.9 %reduce-scatter.7.cloned.1.call-start = ((), (), s32[]{:S(2)}) async-start(), calls=%async_computation.9 | async-start | bytes 3538944 | tf_op jit(solution)/shard_map/reduce_scatter | solution.py:219
  162.8 31.8 %copy-start.24 = (f32[3,256,768]{2,1,0:T(8,128)}, f32[3,256,768]{2,1,0:T(8,128)S(1)}, u32[]{:S(2)}) copy-start(f32[3,256,768]{2,1,0:T(8,128)S(1)} %get-tuple-element.59) | copy-start | bytes 7077892
  162.9 31.7 %copy-start.72 = (f32[3,256]{1,0:T(4,128)}, f32[3,256]{1,0:T(4,128)S(1)}, u32[]{:S(2)}) copy-start(f32[3,256]{1,0:T(4,128)S(1)} %broadcast_multiply_fusion.9) | copy-start | bytes 9220
  253.5 51.2 %reduce-scatter.5.cloned.1.call-start = ((), (), s32[]{:S(2)}) async-start(), calls=%async_computation.8 | async-start | bytes 3538944 | tf_op jit(solution)/shard_map/reduce_scatter | solution.py:213
  289.8 121.4 %reduce-scatter.11.cloned.1.call-start = ((), (), s32[]{:S(2)}) async-start(), calls=%async_computation.11 | async-start | bytes 3538944 | tf_op jit(solution)/shard_map/reduce_scatter | solution.py:219
  348.7 66.3 %reduce-scatter.9.cloned.1.call-start = ((), (), s32[]{:S(2)}) async-start(), calls=%async_computation.10 | async-start | bytes 3538944 | tf_op jit(solution)/shard_map/reduce_scatter | solution.py:213
  387.5 152.1 %all-reduce.3.cloned.1.call-start = ((), (), s32[]{:S(2)}) async-start(), calls=%async_computation.12 | async-start | bytes 393216 | tf_op jit(solution)/shard_map/psum | solution.py:256
  421.0 118.6 %copy-start.44 = (f32[2,2,8,768]{3,2,1,0:T(8,128)S(1)}, f32[2,2,8,768]{3,2,1,0:T(8,128)}, u32[]{:S(2)}) copy-start(f32[2,2,8,768]{3,2,1,0:T(8,128)} %param.28) | copy-start | bytes 294916
  421.0 118.6 %copy-start.56 = (f32[2,2,8,768]{3,2,1,0:T(8,128)S(1)}, f32[2,2,8,768]{3,2,1,0:T(8,128)}, u32[]{:S(2)}) copy-start(f32[2,2,8,768]{3,2,1,0:T(8,128)} %param.31) | copy-start | bytes 294916
  421.0 118.6 %copy-start.57 = (f32[2,2,8,768]{3,2,1,0:T(8,128)S(1)}, f32[2,2,8,768]{3,2,1,0:T(8,128)}, u32[]{:S(2)}) copy-start(f32[2,2,8,768]{3,2,1,0:T(8,128)} %param.30) | copy-start | bytes 294916
  421.0 118.6 %copy-start.96 = (f32[2,2]{1,0:T(2,128)S(1)}, f32[2,2]{1,0:T(2,128)}, u32[]{:S(2)}) copy-start(f32[2,2]{1,0:T(2,128)} %get-tuple-element.37) | copy-start | bytes 52
  421.1 120.2 %copy-start.46 = (f32[2,2,768,8]{2,3,1,0:T(8,128)S(1)}, f32[2,2,768,8]{2,3,1,0:T(8,128)}, u32[]{:S(2)}) copy-start(f32[2,2,768,8]{2,3,1,0:T(8,128)} %param.29) | copy-start | bytes 294916
  421.1 120.2 %copy-start.58 = (f32[2,2,768,8]{2,3,1,0:T(8,128)S(1)}, f32[2,2,768,8]{2,3,1,0:T(8,128)}, u32[]{:S(2)}) copy-start(f32[2,2,768,8]{2,3,1,0:T(8,128)} %param.33) | copy-start | bytes 294916
  421.1 120.2 %copy-start.59 = (f32[2,2,768,8]{2,3,1,0:T(8,128)S(1)}, f32[2,2,768,8]{2,3,1,0:T(8,128)}, u32[]{:S(2)}) copy-start(f32[2,2,768,8]{2,3,1,0:T(8,128)} %param.32) | copy-start | bytes 294916
  421.1 120.2 %copy-start.95 = (f32[2,2]{1,0:T(2,128)S(1)}, f32[2,2]{1,0:T(2,128)}, u32[]{:S(2)}) copy-start(f32[2,2]{1,0:T(2,128)} %get-tuple-element.36) | copy-start | bytes 52
  (97 other events, 576.5 us)
Sparse Core Ops, SparseCore 0:
  16.7 13.6 all-gather.6
  32.5 12.1 all-gather.4
  118.2 12.3 all-gather.10
  132.5 12.1 all-gather.8
  253.6 11.0 reduce-scatter.6
  290.0 10.9 reduce-scatter.4
  348.8 10.9 reduce-scatter.10
  387.6 10.9 reduce-scatter.8
  415.1 124.4 all-reduce.2
where the time goes:
time: 559 us; the launch traced here: 550 us
  matrix products  250 us (45%)
  waiting for transfers between devices  120 us (21%)
  other arithmetic  95.3 us (17%)
  local copies, waits for them, and re-layouts  66.4 us (12%)
  between operations  15.5 us (3%)
    dot_general x30, matrix products, matmul(): return jnp.dot(left_side, right_side, preferred_element_type=jnp.float32)  141 us
    psum x1, waiting for transfers between devices, shards(): lax.psum((down_gradient_total, up_gradient_total), ('seq', 'batch'))  115 us
    another operation x2, other arithmetic, gelu_exact(): return jax.nn.gelu(values, approximate=False)  43.8 us
    dot_general x2, matrix products, shards(): jnp.einsum('sqhe,skhe->shqk', d_out_heads, value_heads, preferred_element...  32.7 us
    convert_element_type x2, other arithmetic, shards(): d_scores = (probs * (d_probs - delta)).astype(jnp.bfloat16)  25.9 us
    unnamed x224, local copies, waits for them, and re-layouts  25.9 us
    dot_general x2, matrix products, shards(): jnp.einsum('shqk,skhe->sqhe', probs_low, value_heads, preferred_element_t...  20.1 us
    dot_general x2, matrix products, shards(): jnp.einsum('shqk,sqhe->skhe', probs.astype(jnp.bfloat16), d_out_heads, pr...  18.4 us
  transfers between devices with their start and end apart: 9, of which 3 were waited for; matrix products, arithmetic and copies ran while one was open for 30% of the time, Pallas kernels for 0%

commit v1 on v0

v1 whole, which is shorter than its diff:
```python
import jax
import jax.numpy as jnp
from jax import lax
from jax.experimental import pallas as pl
from jax.experimental.pallas import tpu as pltpu
from jax.sharding import PartitionSpec as P

HEADS = 12
ENCODER_LAYERS = 2
HALO = 96
BLOCK = 128
SUB = 64
WINDOW = 256
QUAD = 256
MASKED = -1000000000.0
F32 = jnp.float32
BF16 = jnp.bfloat16


def dot_nn(a, b):
    return lax.dot_general(a, b, (((1,), (0,)), ((), ())), preferred_element_type=F32)


def dot_nt(a, b):
    return lax.dot_general(a, b, (((1,), (1,)), ((), ())), preferred_element_type=F32)


def dot_tn(a, b):
    return lax.dot_general(a, b, (((0,), (0,)), ((), ())), preferred_element_type=F32)


def rows_at(start, size, multiple):
    return pl.ds(pl.multiple_of(start, multiple), size)


def loop(count, body):
    def step(i, carry):
        body(i)
        return carry

    lax.fori_loop(0, count, step, 0)


def column_of(row):
    n = row.shape[1]
    eye = lax.broadcasted_iota(jnp.int32, (n, n), 0) == lax.broadcasted_iota(jnp.int32, (n, n), 1)
    return jnp.sum(jnp.where(eye, row, 0.0), axis=1, keepdims=True)


def head_lanes():
    return lax.broadcasted_iota(jnp.int32, (SUB, QUAD), 1) // 64


def spread_heads(tile, lanes):
    zero = jnp.zeros_like(tile)
    return jnp.concatenate([jnp.where(lanes == h, tile, zero) for h in range(4)], axis=0)


def gather_heads(wide, lanes):
    out = wide[:SUB]
    for h in range(1, 4):
        out = jnp.where(lanes == h, wide[h * SUB:(h + 1) * SUB], out)
    return out


def pipelined(units):
    units = list(units)
    live = []
    while units or live:
        if units:
            live.append(units.pop(0))
        for unit in list(live):
            if next(unit, None) is None:
                live.remove(unit)


class Side:
    def __init__(self, near, length, ids_refs, live_of=None):
        self.near, self.length = near, length
        self.side = lax.axis_index("seq")
        self.row0 = BLOCK * ((1 - self.side) if near else self.side)
        self.query_ids, self.key_ids = ids_refs

    def queries(self, s, sub):
        return rows_at(s * self.length + self.row0 + sub * SUB, SUB, SUB)

    def keys(self, s, sub):
        if self.near:
            return rows_at(s * (WINDOW + SUB) + sub * SUB, WINDOW, SUB)
        return rows_at(s * self.length, WINDOW, WINDOW)

    def diagonal(self, shape, sub, query_dim):
        query = lax.broadcasted_iota(jnp.int32, shape, query_dim)
        key = lax.broadcasted_iota(jnp.int32, shape, 1 - query_dim)
        if self.near:
            return query + HALO == key
        return query + (self.row0 + sub * SUB) == key

    def forward_bias(self, s):
        query = column_of(self.query_ids[pl.ds(s, 1), :])
        key = self.key_ids[pl.ds(s, 1), :]
        out = []
        for sub in range(2):
            keys = key[:, sub * SUB:sub * SUB + WINDOW] if self.near else key
            seen = query[sub * SUB:(sub + 1) * SUB] == keys
            seen = seen | self.diagonal((SUB, WINDOW), sub, 0)
            out.append(jnp.where(seen, 0.0, MASKED))
        return out

    def backward_bias(self, s):
        query = self.query_ids[pl.ds(s, 1), :]
        key = self.key_ids[pl.ds(s, 1), :]
        column = jnp.concatenate(
            [column_of(key[:, i:i + SUB]) for i in range(0, key.shape[1], SUB)], axis=0)
        out = []
        for sub in range(2):
            keys = column[sub * SUB:sub * SUB + WINDOW] if self.near else column
            seen = keys == query[:, sub * SUB:(sub + 1) * SUB]
            seen = seen | self.diagonal((WINDOW, SUB), sub, 1)
            out.append(jnp.where(seen, 0.0, MASKED))
        return out


def attention_forward(where, s, q_ref, k_ref, v_ref, out_ref, out_rows):
    lanes = head_lanes()
    biases = where.forward_bias(s)

    def unit(quad, sub):
        cols = slice(QUAD * quad, QUAD * quad + QUAD)
        keys = where.keys(s, sub)
        q4 = spread_heads(q_ref[where.queries(s, sub), cols], lanes)
        scores = dot_nt(q4, k_ref[keys, cols])
        yield True
        scores = scores + jnp.concatenate([biases[sub]] * 4, axis=0)
        top = jnp.max(scores, axis=1, keepdims=True)
        share = jnp.exp(scores - top)
        total = jnp.sum(share, axis=1, keepdims=True)
        share = share.astype(BF16)
        yield True
        mixed = dot_nn(share, v_ref[keys, cols])
        yield True
        out_ref[out_rows(s, sub), cols] = gather_heads(mixed * (1.0 / total), lanes).astype(BF16)

    width = q_ref.shape[1]
    pipelined(unit(quad, sub) for quad in range(width // QUAD) for sub in range(2))


def attention_backward(where, s, q_ref, k_ref, v_ref, dmix_ref, dmix_rows, dq_ref, dq_rows, done):
    lanes = head_lanes()
    biases = where.backward_bias(s)

    def unit(quad, sub, kept):
        cols = slice(QUAD * quad, QUAD * quad + QUAD)
        keys = where.keys(s, sub)
        q4 = spread_heads(q_ref[where.queries(s, sub), cols], lanes)
        d4 = spread_heads(dmix_ref[dmix_rows(s, sub), cols], lanes)
        key, value = k_ref[keys, cols], v_ref[keys, cols]
        scores = dot_nt(key, q4)
        d_share = dot_nt(value, d4)
        yield True
        scores = scores + jnp.concatenate([biases[sub]] * 4, axis=1)
        top = jnp.max(scores, axis=0, keepdims=True)
        share = jnp.exp(scores - top)
        share = share * (1.0 / jnp.sum(share, axis=0, keepdims=True))
        delta = jnp.sum(share * d_share, axis=0, keepdims=True)
        d_scores = (share * (d_share - delta)).astype(BF16)
        kept.append((share.astype(BF16), d_scores, q4, d4))
        yield True
        d_query = gather_heads(dot_tn(d_scores, key), lanes) * 0.125
        dq_ref[dq_rows(s, sub), cols] = d_query.astype(BF16)
        if sub == 1:
            done(s, cols, kept)

    width = q_ref.shape[1]

    def units():
        for quad in range(width // QUAD):
            kept = []
            for sub in range(2):
                yield unit(quad, sub, kept)

    pipelined(units())


def near_terms(kept, which, other):
    first = dot_nn(kept[0][which], kept[0][other])
    second = dot_nn(kept[1][which], kept[1][other])
    return first[:SUB], first[SUB:] + second[:WINDOW - SUB], second[WINDOW - SUB:]


def near_keys_start(sequences, length, k_ref, v_ref, halo_ref, nk_ref, nv_ref, sems):
    side = lax.axis_index("seq")
    wide, own = WINDOW + SUB, WINDOW + SUB - HALO
    copies = []
    for s in range(sequences):
        for i, (src, dst) in enumerate(((k_ref, nk_ref), (v_ref, nv_ref))):
            for j, (part, first, last, size) in enumerate((
                (src, s * length + (length - own) * (1 - side), s * wide + HALO * side, own),
                (halo_ref.at[i], s * HALO, s * wide + own * (1 - side), HALO),
            )):
                copies.append(pltpu.make_async_copy(
                    part.at[rows_at(first, size, 32)], dst.at[rows_at(last, size, 32)],
                    sems.at[s * 4 + i * 2 + j]))
    for copy in copies:
        copy.start()
    return copies


def norm_forward(values, gain, shift):
    center = values - jnp.mean(values, axis=1, keepdims=True)
    spread = jnp.mean(center * center, axis=1, keepdims=True)
    inverse = lax.rsqrt(spread + 1e-05)
    scaled = center * inverse
    return scaled * gain + shift, scaled, inverse


def norm_backward(gradient, scaled, inverse, gain):
    inner = gradient * gain
    return inverse * (
        inner
        - jnp.mean(inner, axis=1, keepdims=True)
        - scaled * jnp.mean(inner * scaled, axis=1, keepdims=True)
    )


def low_rank(a_ref, b_ref):
    down = jnp.concatenate([a_ref[0], a_ref[1]], axis=0).astype(BF16)
    zero = jnp.zeros_like(b_ref[0])
    up_q = jnp.concatenate([b_ref[0], zero], axis=0).astype(BF16)
    up_v = jnp.concatenate([zero, b_ref[1]], axis=0).astype(BF16)
    return down, up_q, up_v


def project_in(sequences, length, x_ref, w_ref, a_ref, b_ref, vec_ref, q_ref, k_ref, v_ref, u_ref,
               send_ref):
    side = lax.axis_index("seq")
    width = x_ref.shape[1]
    down, up_q, up_v = low_rank(a_ref, b_ref)
    vec = vec_ref[...].astype(F32)

    def one(s):
        rows = rows_at(s * length, length, length)
        x = x_ref[rows, :]
        inner = dot_nt(x, down).astype(BF16)
        u_ref[rows, :] = inner
        q = dot_nn(x, w_ref[:, :width]) + vec[0:1] + 2.0 * dot_nn(inner, up_q)
        q_ref[rows, :] = q.astype(BF16) * jnp.asarray(0.125, BF16)
        k_ref[rows, :] = dot_nn(x, w_ref[:, width:2 * width]).astype(BF16)
        v = dot_nn(x, w_ref[:, 2 * width:]) + vec[1:2] + 2.0 * dot_nn(inner, up_v)
        v_ref[rows, :] = v.astype(BF16)
        taken = rows_at(s * length + (1 - side) * (length - HALO), HALO, 32)
        given = rows_at(s * HALO, HALO, 32)
        send_ref[0, given, :] = k_ref[taken, :]
        send_ref[1, given, :] = v_ref[taken, :]

    loop(sequences, one)


def layer_rest(sequences, length, mix_ref, h_ref, wo_ref, wu_ref, wd_ref, waits, vec_ref, bu_ref,
               one_ref, low_ref, act_ref, n1_ref, r1_ref, dg_ref, n2_ref, r2_ref, h_outs, sent):
    hidden = wu_ref.shape[1]
    waits[0]()
    vec = vec_ref[...].astype(F32)

    def mixed(s):
        rows = rows_at(s * length, length, length)
        attended = dot_nn(mix_ref[rows, :], wo_ref[...]) + vec[2:3] + h_ref[rows, :].astype(F32)
        one, scaled, inverse = norm_forward(attended, vec[4:5], vec[5:6])
        n1_ref[rows, :] = scaled.astype(n1_ref.dtype)
        r1_ref[rows, :] = jnp.broadcast_to(inverse, (length, 128))
        one_ref[rows, :] = one
        low_ref[rows, :] = one.astype(BF16)

    loop(sequences, mixed)
    sent(0)
    waits[1]()
    tile = 512

    def up(j):
        cols = rows_at(j * tile, tile, tile)
        bias = bu_ref[:, cols].astype(F32)
        weights = wu_ref[:, cols]

        def unit(s):
            rows = slice(s * length, (s + 1) * length)
            gate = dot_nn(low_ref[rows, :], weights)
            yield True
            gate = gate + bias
            below = 0.5 * lax.erf(gate * 0.7071067811865476) + 0.5
            act_ref[rows, cols] = (gate * below).astype(BF16)
            density = jnp.exp2(gate * gate * -0.7213475204444817) * 0.3989422804014327
            dg_ref[rows, cols] = (below + gate * density).astype(BF16)

        pipelined(unit(s) for s in range(sequences))

    loop(hidden // tile, up)
    sent(1)
    waits[2]()

    def down(s):
        rows = rows_at(s * length, length, length)
        summed = dot_nn(act_ref[rows, :], wd_ref[...]) + vec[3:4] + one_ref[rows, :]
        out, scaled, inverse = norm_forward(summed, vec[6:7], vec[7:8])
        n2_ref[rows, :] = scaled.astype(n2_ref.dtype)
        r2_ref[rows, :] = jnp.broadcast_to(inverse, (length, 128))
        for h_out in h_outs:
            h_out[rows, :] = out.astype(h_out.dtype)

    loop(sequences, down)
    sent(2)


def layer_rest_back(sequences, length, gradient, waits, n1_ref, r1_ref, dg_ref, n2_ref, r2_ref,
                    wo_ref, wu_ref, wd_ref, vec_ref, two_ref, low_ref, gate_ref, datt_ref):
    hidden = wu_ref.shape[1]
    waits[0]()
    vec = vec_ref[...].astype(F32)

    def second(s):
        rows = rows_at(s * length, length, length)
        two = norm_backward(
            gradient(s, rows), n2_ref[rows, :].astype(F32), r2_ref[rows, 0:1], vec[6:7])
        two_ref[rows, :] = two
        low_ref[rows, :] = two.astype(BF16)

    loop(sequences, second)
    waits[1]()
    tile = 512

    def down(j):
        cols = rows_at(j * tile, tile, tile)
        weights = wd_ref[cols, :]

        def unit(s):
            rows = slice(s * length, (s + 1) * length)
            gate = dot_nt(low_ref[rows, :], weights)
            yield True
            gate_ref[rows, cols] = (gate * dg_ref[rows, cols].astype(F32)).astype(BF16)

        pipelined(unit(s) for s in range(sequences))

    loop(hidden // tile, down)
    waits[2]()
    waits[3]()

    def up(s):
        rows = rows_at(s * length, length, length)
        one = dot_nt(gate_ref[rows, :], wu_ref[...]) + two_ref[rows, :]
        att = norm_backward(one, n1_ref[rows, :].astype(F32), r1_ref[rows, 0:1], vec[4:5])
        datt_ref[rows, :] = att
        low_ref[rows, :] = dot_nt(att.astype(BF16), wo_ref[...]).astype(BF16)

    loop(sequences, up)


def near_backward(sequences, length, ids_refs, q_ref, nk_ref, nv_ref, dmix_ref, dfar_ref, dq_ref,
                  dnk_ref, dnv_ref, dhalo_ref):
    near = Side(True, length, ids_refs)
    side, wide = near.side, WINDOW + SUB

    def done(s, cols, kept):
        for out, which, other in ((dnv_ref, 0, 3), (dnk_ref, 1, 2)):
            first, both, second = near_terms(kept, which, other)
            out[rows_at(s * wide, SUB, SUB), cols] = first
            out[rows_at(s * wide + SUB, WINDOW - SUB, SUB), cols] = both
            out[rows_at(s * wide + WINDOW, SUB, SUB), cols] = second

    def one(s):
        dfar_ref[rows_at(s * BLOCK, BLOCK, BLOCK), :] = dmix_ref[
            rows_at(s * length + side * BLOCK, BLOCK, BLOCK), :]
        attention_backward(
            near, s, q_ref, nk_ref, nv_ref, dmix_ref, near.queries, dq_ref,
            lambda s, sub: rows_at(s * BLOCK + sub * SUB, SUB, SUB), done)
        halo = rows_at(s * wide + (wide - HALO) * (1 - side), HALO, 32)
        dhalo_ref[0, rows_at(s * HALO, HALO, 32), :] = dnk_ref[halo, :].astype(BF16)
        dhalo_ref[1, rows_at(s * HALO, HALO, 32), :] = dnv_ref[halo, :].astype(BF16)

    loop(sequences, one)


def adapter_back(sequences, length, dq_ref, dk_ref, dv_ref, dhalo_ref, u_ref, x_ref, a_ref,
                 b_ref, dkb_ref, dvb_ref, du_ref, grad_ref):
    side = lax.axis_index("seq")
    rank = a_ref.shape[1]
    _, up_q, up_v = low_rank(a_ref, b_ref)

    def one(s):
        rows = rows_at(s * length, length, length)
        taken = rows_at(s * length + (1 - side) * (length - HALO), HALO, 32)
        hrows = rows_at(s * HALO, HALO, 32)
        dk_ref[taken, :] = dk_ref[taken, :] + dhalo_ref[0, hrows, :].astype(F32)
        dv_ref[taken, :] = dv_ref[taken, :] + dhalo_ref[1, hrows, :].astype(F32)
        dkb_ref[rows, :] = dk_ref[rows, :].astype(BF16)
        dv16 = dv_ref[rows, :].astype(BF16)
        dvb_ref[rows, :] = dv16
        du_ref[rows, :] = (2.0 * (dot_nt(dq_ref[rows, :], up_q) + dot_nt(dv16, up_v))).astype(BF16)

    loop(sequences, one)
    u = u_ref[...]
    grad_ref[0:2 * rank, :] = dot_tn(du_ref[...], x_ref[...])
    up_q, up_v = dot_tn(u, dq_ref[...]), dot_tn(u, dvb_ref[...])
    grad_ref[2 * rank:3 * rank, :] = 2.0 * up_q[:rank]
    grad_ref[3 * rank:, :] = 2.0 * up_v[rank:]


def project_back(rows, own_rows, datt_ref, dq_ref, dk_ref, dv_ref, du_ref, w_ref, down):
    width = dq_ref.shape[1]
    out = datt_ref[rows, :] + dot_nn(du_ref[rows, :], down)
    out = out + dot_nt(dq_ref[rows, :], w_ref[:, :width])
    out = out + dot_nt(dk_ref[rows, :], w_ref[:, width:2 * width])
    return out + dot_nt(dv_ref[rows, :], w_ref[:, 2 * width:])


HBM, VMEM, SMEM = pltpu.HBM, pltpu.VMEM, pltpu.SMEM


def call(kernel, name, args, outs, scratch, flops, nbytes, limit, aliases=None):
    scratch = [pltpu.SemaphoreType.DMA((s,)) if isinstance(s, int) else pltpu.VMEM(*s)
               for s in scratch]
    return pl.pallas_call(
        kernel,
        name=name,
        out_shape=tuple(space(shape, dtype) for space, shape, dtype in outs),
        in_specs=[pl.BlockSpec(memory_space=space) for space, _ in args],
        out_specs=tuple(pl.BlockSpec(memory_space=space) for space, _, _ in outs),
        scratch_shapes=scratch,
        input_output_aliases=aliases or {},
        compiler_params=pltpu.CompilerParams(vmem_limit_bytes=limit * 1024 * 1024),
        cost_estimate=pl.CostEstimate(flops=flops, bytes_accessed=nbytes, transcendentals=0),
    )(*[array if space == SMEM else pltpu.with_memory_space_constraint(array, space)
        for space, array in args])


def sds(shape, dtype):
    return jax.ShapeDtypeStruct(shape, dtype)


def copies_of(pairs, sems):
    return [pltpu.make_async_copy(src, dst, sems.at[i]) for i, (src, dst) in enumerate(pairs)]


def start_all(copies):
    for copy in copies:
        copy.start()
    return copies


def wait_for(copies, *which):
    def wait():
        for i in which:
            copies[i].wait()

    return wait


def first_call(layer, sequences, length, x, w, a, b, vec):
    tokens, width = x.shape
    rank = a.shape[2]

    def kernel(x_hbm, w_hbm, a_hbm, b_hbm, vec_hbm, q_ref, k_ref, v_ref, send_ref, u_out, x_ref,
               w_ref, a_ref, b_ref, vec_ref, u_ref, sems, outs):
        copies = start_all(copies_of(
            [(a_hbm.at[layer], a_ref), (b_hbm.at[layer], b_ref), (vec_hbm.at[layer], vec_ref),
             (x_hbm, x_ref), (w_hbm.at[layer], w_ref)], sems))
        wait_for(copies, 0, 1, 2, 3, 4)()
        project_in(sequences, length, x_ref, w_ref, a_ref, b_ref, vec_ref, q_ref, k_ref, v_ref,
                   u_ref, send_ref)
        store = pltpu.make_async_copy(u_ref, u_out, outs.at[0])
        store.start()
        store.wait()

    act, small = (VMEM, (tokens, width), BF16), ((tokens, 2 * rank), BF16)
    return call(
        kernel, "project_in", [(HBM, x), (HBM, w), (HBM, a), (HBM, b), (HBM, vec)],
        [act, act, act, (VMEM, (2, sequences * HALO, width), BF16), (HBM,) + small],
        [((tokens, width), BF16), ((width, 3 * width), BF16), ((2, rank, width), F32),
         ((2, rank, width), F32), ((8, width), BF16), small, 5, 1],
        2 * tokens * width * width * 3, 12000000, 10)


def far_call(sequences, length, q, k, v, ids):
    tokens, width = q.shape

    def kernel(q_ref, k_ref, v_ref, qid_ref, kid_ref, out_ref):
        far = Side(False, length, (qid_ref, kid_ref))
        loop(sequences, lambda s: attention_forward(
            far, s, q_ref, k_ref, v_ref, out_ref,
            lambda s, sub: rows_at(s * BLOCK + sub * SUB, SUB, SUB)))

    return call(
        kernel, "attention_far",
        [(VMEM, q), (VMEM, k), (VMEM, v), (VMEM, ids[2]), (VMEM, ids[3])],
        [(VMEM, (sequences * BLOCK, width), BF16)], [], 2000000000, 6000000, 6)[0]


def near_forward(sequences, length, ids_refs, far_ref, q_ref, k_ref, v_ref, halo_ref, nk_ref,
                 nv_ref, mix_ref, sems):
    copies = near_keys_start(sequences, length, k_ref, v_ref, halo_ref, nk_ref, nv_ref, sems)
    near = Side(True, length, ids_refs)
    for copy in copies:
        copy.wait()

    def one(s):
        mix_ref[rows_at(s * length + near.side * BLOCK, BLOCK, BLOCK), :] = far_ref[
            rows_at(s * BLOCK, BLOCK, BLOCK), :]
        attention_forward(near, s, q_ref, nk_ref, nv_ref, mix_ref, near.queries)

    loop(sequences, one)


def middle_call(layer, sequences, length, ids, far, q, k, v, halo, h, w, a, b, wo, wu, wd, vec,
                bias_up):
    tokens, width = q.shape
    hidden, rank = wu.shape[2], a.shape[2]

    def kernel(qid_ref, kid_ref, far_ref, q_ref, k_ref, v_ref, halo_ref, h_hbm, w_hbm, a_hbm,
               b_hbm, wo_hbm, wu_hbm, wd_hbm, vec_hbm, bu_hbm,
               q2_ref, k2_ref, v2_ref, send_ref,
               u_out, x_out, h_out, n1_out, r1_out, dg_out, n2_out, r2_out, q_out, k_out, v_out,
               nk_out, nv_out,
               h_ref, w_ref, wo_ref, wu_ref, wd_ref, vec_ref, bu_ref, vec2_ref, a_ref, b_ref,
               u_ref, mix_ref, one_ref, low_ref, act_ref,
               n1_ref, r1_ref, dg_ref, n2_ref, r2_ref, nk_ref, nv_ref, ins, outs, sems):
        loads = start_all(copies_of(
            [(h_hbm, h_ref), (vec_hbm.at[layer], vec_ref), (wo_hbm.at[layer], wo_ref),
             (bu_hbm.at[layer], bu_ref), (wu_hbm.at[layer], wu_ref), (wd_hbm.at[layer], wd_ref),
             (w_hbm.at[layer + 1], w_ref), (a_hbm.at[layer + 1], a_ref),
             (b_hbm.at[layer + 1], b_ref), (vec_hbm.at[layer + 1], vec2_ref)], ins))
        stores = copies_of(
            [(q_ref, q_out), (k_ref, k_out), (v_ref, v_out), (nk_ref, nk_out), (nv_ref, nv_out),
             (n1_ref, n1_out), (r1_ref, r1_out), (dg_ref, dg_out), (n2_ref, n2_out),
             (r2_ref, r2_out), (one_ref, h_out), (low_ref, x_out), (u_ref, u_out)], outs)
        near_forward(sequences, length, (qid_ref, kid_ref), far_ref, q_ref, k_ref, v_ref,
                     halo_ref, nk_ref, nv_ref, mix_ref, sems)
        layer_rest(sequences, length, mix_ref, h_ref, wo_ref, wu_ref, wd_ref,
                   [wait_for(loads, 0, 1, 2), wait_for(loads, 3, 4), wait_for(loads, 5)], vec_ref,
                   bu_ref, one_ref, low_ref, act_ref, n1_ref, r1_ref, dg_ref, n2_ref, r2_ref,
                   (one_ref, low_ref),
                   lambda i: start_all((stores[:7], stores[7:8], stores[8:12])[i]))
        wait_for(loads, 6, 7, 8, 9)()
        project_in(sequences, length, low_ref, w_ref, a_ref, b_ref, vec2_ref, q2_ref, k2_ref,
                   v2_ref, u_ref, send_ref)
        stores[12].start()
        for copy in stores:
            copy.wait()

    act, stat = ((tokens, width), BF16), ((tokens, 128), F32)
    wide, deep = ((tokens, width), F32), ((tokens, hidden), BF16)
    near, small = ((sequences * (WINDOW + SUB), width), BF16), ((tokens, 2 * rank), BF16)
    factors = ((2, rank, width), F32)
    return call(
        kernel, "middle",
        [(VMEM, ids[0]), (VMEM, ids[1]), (VMEM, far), (VMEM, q), (VMEM, k), (VMEM, v),
         (VMEM, halo)]
        + [(HBM, item) for item in (h, w, a, b, wo, wu, wd, vec, bias_up)],
        [(VMEM,) + act, (VMEM,) + act, (VMEM,) + act, (VMEM, (2, sequences * HALO, width), BF16)]
        + [(HBM,) + item for item in (small, act, wide, act, stat, deep, act, stat, act, act, act,
                                      near, near)],
        [(h.shape, h.dtype), ((width, 3 * width), BF16), ((width, width), BF16),
         ((width, hidden), BF16), ((hidden, width), BF16), ((8, width), BF16),
         ((1, hidden), BF16), ((8, width), BF16), factors, factors, small, act, wide, act, deep,
         act, stat, deep, act, stat, near, near, 10, 13, 4 * sequences],
        2 * tokens * width * (2 * hidden + 4 * width), 24000000, 42)


def turn_call(layer, sequences, length, ids, live, far, q, k, v, halo, h, gradient, wo, wu, wd,
              vec, bias_up):
    tokens, width = q.shape
    hidden = wu.shape[2]

    def kernel(qid_ref, kid_ref, live_ref, far_ref, q_ref, k_ref, v_ref, halo_ref, h_hbm, g_hbm,
               wo_hbm, wu_hbm, wd_hbm, vec_hbm, bu_hbm,
               datt_ref, dfar_ref, dq_ref, dnk_ref, dnv_ref, dhalo_ref, hidden_out,
               h_ref, g_ref, wo_ref, wu_ref, wd_ref, vec_ref, bu_ref, mix_ref, one_ref, low_ref,
               act_ref, n1_ref, r1_ref, dg_ref, n2_ref, r2_ref, nk_ref, nv_ref, ins, outs, sems):
        loads = start_all(copies_of(
            [(h_hbm, h_ref), (vec_hbm.at[layer], vec_ref), (wo_hbm.at[layer], wo_ref),
             (bu_hbm.at[layer], bu_ref), (wu_hbm.at[layer], wu_ref), (wd_hbm.at[layer], wd_ref),
             (g_hbm, g_ref)], ins))
        store = pltpu.make_async_copy(mix_ref, hidden_out, outs.at[0])
        near_forward(sequences, length, (qid_ref, kid_ref), far_ref, q_ref, k_ref, v_ref,
                     halo_ref, nk_ref, nv_ref, mix_ref, sems)
        side = lax.axis_index("seq")
        layer_rest(sequences, length, mix_ref, h_ref, wo_ref, wu_ref, wd_ref,
                   [wait_for(loads, 0, 1, 2), wait_for(loads, 3, 4), wait_for(loads, 5)], vec_ref,
                   bu_ref, one_ref, low_ref, act_ref, n1_ref, r1_ref, dg_ref, n2_ref, r2_ref,
                   (mix_ref,), lambda i: None)
        store.start()

        def given(s, rows):
            places = lax.broadcasted_iota(jnp.int32, (length, 1), 0) + side * length
            return jnp.where(places < live_ref[s], g_ref[rows, :].astype(F32), 0.0)

        nothing = wait_for(loads)
        layer_rest_back(sequences, length, given,
                        [wait_for(loads, 6), nothing, nothing, nothing], n1_ref,
                        r1_ref, dg_ref, n2_ref, r2_ref, wo_ref, wu_ref, wd_ref, vec_ref, one_ref,
                        low_ref, act_ref, datt_ref)
        near_backward(sequences, length, (qid_ref, kid_ref), q_ref, nk_ref, nv_ref, low_ref,
                      dfar_ref, dq_ref, dnk_ref, dnv_ref, dhalo_ref)
        store.wait()

    act, stat = ((tokens, width), BF16), ((tokens, 128), F32)
    wide, deep = ((tokens, width), F32), ((tokens, hidden), BF16)
    near_rows = sequences * (WINDOW + SUB)
    near, block = ((near_rows, width), BF16), ((sequences * BLOCK, width), BF16)
    return call(
        kernel, "turn",
        [(VMEM, ids[0]), (VMEM, ids[1]), (SMEM, live), (VMEM, far), (VMEM, q), (VMEM, k),
         (VMEM, v), (VMEM, halo)]
        + [(HBM, item) for item in (h, gradient, wo, wu, wd, vec, bias_up)],
        [(VMEM,) + wide, (VMEM,) + block, (VMEM,) + block, (VMEM, (near_rows, width), F32),
         (VMEM, (near_rows, width), F32), (VMEM, (2, sequences * HALO, width), BF16),
         (HBM,) + act],
        [(h.shape, h.dtype), act, ((width, width), BF16), ((width, hidden), BF16),
         ((hidden, width), BF16), ((8, width), BF16), ((1, hidden), BF16), act, wide, act, deep,
         act, stat, deep, act, stat, near, near, 7, 1, 4 * sequences],
        4 * tokens * width * (2 * hidden + width), 24000000, 40)


def back_far_call(sequences, length, ids, q, k, v, dfar, dq_near, dnk, dnv):
    tokens, width = q.shape

    def kernel(qid_ref, kid_ref, q_ref, k_ref, v_ref, dfar_ref, dqn_ref, dnk_ref, dnv_ref, dq_ref,
               dk_ref, dv_ref):
        far = Side(False, length, (qid_ref, kid_ref))
        side, wide, own = far.side, WINDOW + SUB, WINDOW + SUB - HALO

        def done(s, cols, kept):
            for out, which, other in ((dv_ref, 0, 3), (dk_ref, 1, 2)):
                left = jnp.concatenate([kept[0][which], kept[1][which]], axis=1)
                right = jnp.concatenate([kept[0][other], kept[1][other]], axis=0)
                out[far.keys(s, 0), cols] = dot_nn(left, right)

        def one(s):
            attention_backward(
                far, s, q_ref, k_ref, v_ref, dfar_ref,
                lambda s, sub: rows_at(s * BLOCK + sub * SUB, SUB, SUB), dq_ref, far.queries, done)
            dq_ref[rows_at(s * length + (1 - side) * BLOCK, BLOCK, BLOCK), :] = dqn_ref[
                rows_at(s * BLOCK, BLOCK, BLOCK), :]
            mine = rows_at(s * length + (length - own) * (1 - side), own, 32)
            theirs = rows_at(s * wide + HALO * side, own, 32)
            dk_ref[mine, :] = dk_ref[mine, :] + dnk_ref[theirs, :]
            dv_ref[mine, :] = dv_ref[mine, :] + dnv_ref[theirs, :]

        loop(sequences, one)

    wide = (VMEM, (tokens, width), F32)
    return call(
        kernel, "back_far",
        [(VMEM, item) for item in (ids[2], ids[3], q, k, v, dfar, dq_near, dnk, dnv)],
        [(VMEM, (tokens, width), BF16), wide, wide], [], 4000000000, 16000000, 6)


def back_call(layer, sequences, length, ids, dq, dk, dv, dhalo, datt, u, x, saved, w, a, b, wo, wu,
              wd, vec):
    tokens, width = dq.shape
    hidden, rank = wu.shape[2], a.shape[2]

    def kernel(qid_ref, kid_ref, dq_ref, dk_ref, dv_ref, dhalo_ref, datt_ref, u_hbm, x_hbm,
               n1_hbm, r1_hbm, dg_hbm, n2_hbm, r2_hbm, q_hbm, k_hbm, v_hbm, nk_hbm, nv_hbm, w_hbm,
               a_hbm, b_hbm, wo_hbm, wu_hbm, wd_hbm, vec_hbm,
               datt_out, dfar_ref, dqn_ref, dnk_ref, dnv_ref, dhalo_out, q_ref, k_ref, v_ref,
               grad_out,
               u_ref, x_ref, n1_ref, r1_ref, dg_ref, n2_ref, r2_ref, nk_ref, nv_ref, w_ref,
               a_ref, b_ref, wo_ref, wu_ref, wd_ref, vec_ref, dkb_ref, dvb_ref, du_ref, grad_ref,
               two_ref, low_ref, ins, outs):
        loads = start_all(copies_of(
            [(a_hbm.at[layer + 1], a_ref), (b_hbm.at[layer + 1], b_ref), (u_hbm, u_ref),
             (x_hbm, x_ref), (w_hbm.at[layer + 1], w_ref), (vec_hbm.at[layer], vec_ref),
             (n2_hbm, n2_ref), (r2_hbm, r2_ref), (wd_hbm.at[layer], wd_ref), (dg_hbm, dg_ref),
             (wu_hbm.at[layer], wu_ref), (n1_hbm, n1_ref), (r1_hbm, r1_ref),
             (wo_hbm.at[layer], wo_ref), (q_hbm, q_ref), (nk_hbm, nk_ref), (nv_hbm, nv_ref),
             (k_hbm, k_ref), (v_hbm, v_ref)], ins))
        wait_for(loads, 0, 1, 2, 3)()
        adapter_back(sequences, length, dq_ref, dk_ref, dv_ref, dhalo_ref, u_ref, x_ref,
                     a_ref, b_ref, dkb_ref, dvb_ref, du_ref, grad_ref)
        store = pltpu.make_async_copy(grad_ref, grad_out, outs.at[0])
        store.start()
        down, _, _ = low_rank(a_ref, b_ref)

        def given(s, rows):
            return project_back(rows, rows, datt_ref, dq_ref, dkb_ref, dvb_ref, du_ref, w_ref,
                                down)

        layer_rest_back(sequences, length, given,
                        [wait_for(loads, 4, 5, 6, 7), wait_for(loads, 8, 9), wait_for(loads, 10),
                         wait_for(loads, 11, 12, 13)], n1_ref, r1_ref, dg_ref, n2_ref, r2_ref,
                        wo_ref, wu_ref, wd_ref, vec_ref, two_ref, low_ref, dg_ref, datt_out)
        wait_for(loads, 14, 15, 16)()
        near_backward(sequences, length, (qid_ref, kid_ref), q_ref, nk_ref, nv_ref, low_ref,
                      dfar_ref, dqn_ref, dnk_ref, dnv_ref, dhalo_out)
        wait_for(loads, 17, 18)()
        store.wait()

    act, stat = ((tokens, width), BF16), ((tokens, 128), F32)
    wide, deep = ((tokens, width), F32), ((tokens, hidden), BF16)
    near_rows = sequences * (WINDOW + SUB)
    near, block = ((near_rows, width), BF16), ((sequences * BLOCK, width), BF16)
    small, factors = ((tokens, 2 * rank), BF16), ((2, rank, width), F32)
    grad = ((4 * rank, width), F32)
    return call(
        kernel, "back",
        [(VMEM, item) for item in (ids[0], ids[1], dq, dk, dv, dhalo, datt)]
        + [(HBM, item) for item in (u, x, *saved, w, a, b, wo, wu, wd, vec)],
        [(VMEM,) + wide, (VMEM,) + block, (VMEM,) + block,
         (VMEM, (near_rows, width), F32), (VMEM, (near_rows, width), F32),
         (VMEM, (2, sequences * HALO, width), BF16), (VMEM,) + act, (VMEM,) + act, (VMEM,) + act,
         (HBM,) + grad],
        [small, act, act, stat, deep, act, stat, near, near, ((width, 3 * width), BF16), factors,
         factors, ((width, width), BF16), ((width, hidden), BF16), ((hidden, width), BF16),
         ((8, width), BF16), act, act, small, grad, wide, act, 19, 1],
        2 * tokens * width * (2 * hidden + 4 * width), 24000000, 38)


def last_call(layer, sequences, length, dq, dk, dv, dhalo, u, x, w, a, b, other):
    tokens, width = dq.shape
    rank = a.shape[2]

    def kernel(dq_ref, dk_ref, dv_ref, dhalo_ref, u_hbm, x_hbm, w_hbm, a_hbm, b_hbm, other_hbm,
               dkb_ref, dvb_ref, du_ref, w_ref, down_ref, mine_ref, theirs_ref,
               u_ref, x_ref, a_ref, b_ref, other_ref, grad_ref, sems):
        loads = start_all(copies_of(
            [(a_hbm.at[layer], a_ref), (b_hbm.at[layer], b_ref), (u_hbm, u_ref), (x_hbm, x_ref),
             (other_hbm, other_ref), (w_hbm.at[layer], w_ref)], sems))
        wait_for(loads, 0, 1, 2, 3, 4)()
        adapter_back(sequences, length, dq_ref, dk_ref, dv_ref, dhalo_ref, u_ref, x_ref,
                     a_ref, b_ref, dkb_ref, dvb_ref, du_ref, grad_ref)
        down_ref[...] = low_rank(a_ref, b_ref)[0]
        first = lax.axis_index("seq") == layer
        here, there = grad_ref[...], other_ref[...]
        mine_ref[...] = jnp.where(first, here, there)
        theirs_ref[...] = jnp.where(first, there, here)
        wait_for(loads, 5)()

    act, grad = ((tokens, width), BF16), ((4 * rank, width), F32)
    small, factors = ((tokens, 2 * rank), BF16), ((2, rank, width), F32)
    return call(
        kernel, "adapter_back",
        [(VMEM, dq), (VMEM, dk), (VMEM, dv), (VMEM, dhalo)]
        + [(HBM, item) for item in (u, x, w, a, b, other)],
        [(VMEM,) + act, (VMEM,) + act, (VMEM,) + small, (VMEM, (width, 3 * width), BF16),
         (VMEM, (2 * rank, width), BF16), (VMEM,) + grad, (VMEM,) + grad],
        [small, act, factors, factors, grad, grad, 6], 500000000, 12000000, 8)


def project_back_call(s, sequences, length, datt, dq, dk, dv, du, w, down, out):
    tokens, width = dq.shape

    def kernel(datt_ref, dq_ref, dk_ref, dv_ref, du_ref, w_ref, down_ref, *rest):
        out_hbm, out_ref, sems = rest[-3:]
        rows = slice(s * length, (s + 1) * length)
        out_ref[...] = project_back(rows, rows, datt_ref, dq_ref, dk_ref, dv_ref, du_ref, w_ref,
                                    down_ref[...])
        store = pltpu.make_async_copy(out_ref, out_hbm.at[rows], sems.at[0])
        store.start()
        store.wait()

    args = [(VMEM, item) for item in (datt, dq, dk, dv, du, w, down)]
    return call(
        kernel, "project_back", args + ([] if out is None else [(HBM, out)]),
        [(HBM, (tokens, width), F32)], [((length, width), F32), 1],
        2 * length * width * width * 3, 4000000, 6, {} if out is None else {len(args): 0})[0]


def adam_call(mine, theirs, token_slots, steps, down, up, m_down, v_down, m_up, v_up):
    layers, two, rank, width = down.shape

    def kernel(mine_ref, theirs_ref, steps_ref, down_ref, up_ref, md_ref, vd_ref, mu_ref, vu_ref,
               down_out, up_out, md_out, vd_out, mu_out, vu_out):
        side = lax.axis_index("seq")
        for layer in range(layers):
            for which in range(two):
                for group, (w_ref, m_ref, v_ref, w_out, m_out, v_out, rate, decay) in enumerate((
                    (down_ref, md_ref, vd_ref, down_out, md_out, vd_out, 0.03125, 0.1),
                    (up_ref, mu_ref, vu_ref, up_out, mu_out, vu_out, 0.5, 0.0),
                )):
                    rows = slice((group * two + which) * rank, (group * two + which + 1) * rank)
                    grad = jnp.where(side == layer, mine_ref[rows, :], theirs_ref[rows, :])
                    grad = grad / token_slots
                    step = jnp.full((rank, width), steps_ref[layer, which, group], jnp.int32)
                    correction = 1.0 - jnp.exp2(-step.astype(F32))
                    weight = w_ref[layer, which]
                    moment = 0.5 * m_ref[layer, which] + 0.5 * grad
                    velocity = 0.5 * v_ref[layer, which] + 0.5 * grad * grad
                    size = moment / correction / (jnp.sqrt(velocity / correction) + 1e-08)
                    w_out[layer, which] = weight - rate * (size + decay * weight)
                    m_out[layer, which] = moment
                    v_out[layer, which] = velocity

    shapes = [sds(down.shape, F32)] * 6
    vmem = pl.BlockSpec(memory_space=VMEM)
    return pl.pallas_call(
        kernel, name="adam", out_shape=shapes,
        in_specs=[vmem, vmem, pl.BlockSpec(memory_space=SMEM)] + [vmem] * 6, out_specs=[vmem] * 6,
    )(mine, theirs, steps, down, up, m_down, v_down, m_up, v_up)


def together(*values):
    return lax.optimization_barrier(values)


def sum_while(mine, theirs, work):
    batch = lax.axis_size("batch")
    swap = [(0, 1), (1, 0)]
    mine = mine + lax.ppermute(theirs, "seq", swap)
    done, work, step = None, list(work), 1
    while step < batch:
        come = lax.ppermute(mine, "batch", [(i, i ^ step) for i in range(batch)])
        if work:
            done = work.pop(0)(mine, done)
            come, done = together(come, done)
        mine = mine + come
        step *= 2
    for one in work:
        done = one(mine, done)
    return mine, lax.ppermute(mine, "seq", swap), done


def key_and_query_ids(ids, live, length, swap):
    side = lax.axis_index("seq")
    other = lax.ppermute(ids, "seq", swap)
    halo = jnp.where(side == 0, other[:, :HALO], other[:, length - HALO:])
    own = WINDOW + SUB - HALO
    near = jnp.where(side == 0, jnp.concatenate([ids[:, length - own:], halo], 1),
                     jnp.concatenate([halo, ids[:, :own]], 1)).astype(F32)
    places = jnp.arange(WINDOW + SUB) + jnp.where(side == 0, length - own, length - HALO)
    near = jnp.where(places[None] < live[:, None], near, -1.0)
    values = ids.astype(F32)
    places = jnp.arange(length) + side * length
    far = jnp.where(places[None] < live[:, None], values, -1.0)
    low, high = values[:, :BLOCK], values[:, BLOCK:]
    return (jnp.where(side == 0, high, low), near, jnp.where(side == 0, low, high), far)


def shards(
    first_layer_input,
    output_gradient,
    sentence_pair_index,
    sequence_live_length,
    optimizer_step_count,
    query_key_value_weight,
    attention_output_weight,
    feedforward_up_weight,
    feedforward_down_weight,
    layer_bias_gain_rows,
    feedforward_up_bias,
    adapter_down_factors,
    adapter_up_factors,
    first_moment_down,
    second_moment_down,
    first_moment_up,
    second_moment_up,
):
    sequences, length, width = first_layer_input.shape
    tokens = sequences * length
    swap = [(0, 1), (1, 0)]
    live = sequence_live_length
    a, b = adapter_down_factors, jnp.swapaxes(adapter_up_factors, 2, 3)
    vec = layer_bias_gain_rows
    bias_up = feedforward_up_bias[:, None, :]
    wqkv, wo = query_key_value_weight, attention_output_weight
    wu, wd = feedforward_up_weight, feedforward_down_weight
    ids = key_and_query_ids(sentence_pair_index, live, length, swap)
    shape = (sequences, length)

    x1 = first_layer_input.reshape(tokens, width)
    q1, k1, v1, send, u1 = first_call(0, *shape, x1, wqkv, a, b, vec)
    halo = lax.ppermute(send, "seq", swap)
    far = far_call(*shape, q1, k1, v1, ids)
    q2, k2, v2, send, u2, x2, h1, *saved = middle_call(
        0, *shape, ids, far, q1, k1, v1, halo, x1, wqkv, a, b, wo, wu, wd, vec, bias_up)
    halo = lax.ppermute(send, "seq", swap)
    far = far_call(*shape, q2, k2, v2, ids)
    datt, dfar, dqn, dnk, dnv, dsend, hidden_out = turn_call(
        1, *shape, ids, live, far, q2, k2, v2, halo, h1, output_gradient.reshape(tokens, width),
        wo, wu, wd, vec, bias_up)
    dhalo = lax.ppermute(dsend, "seq", swap)
    dq, dk, dv = back_far_call(*shape, ids, q2, k2, v2, dfar, dqn, dnk, dnv)
    datt, dfar, dqn, dnk, dnv, dsend, q1, k1, v1, grad2 = back_call(
        0, *shape, ids, dq, dk, dv, dhalo, datt, u2, x2, saved, wqkv, a, b, wo, wu, wd, vec)
    dhalo = lax.ppermute(dsend, "seq", swap)
    dq, dk, dv = back_far_call(*shape, ids, q1, k1, v1, dfar, dqn, dnk, dnv)
    dk, dv, du, w1, down1, mine, theirs = last_call(
        0, *shape, dq, dk, dv, dhalo, u1, x1, wqkv, a, b, grad2)

    def part(s):
        def work(token, out):
            now, _ = together(datt, token)
            return project_back_call(s, *shape, now, dq, dk, dv, du, w1, down1, out)

        return work

    mine, theirs, gradient = sum_while(mine, theirs, [part(s) for s in range(sequences)])
    token_slots = tokens * lax.axis_size("seq") * lax.axis_size("batch")
    down, up, m_down, v_down, m_up, v_up = adam_call(
        mine, theirs, token_slots, optimizer_step_count, a, b, first_moment_down,
        second_moment_down, jnp.swapaxes(first_moment_up, 2, 3),
        jnp.swapaxes(second_moment_up, 2, 3))
    return (
        hidden_out.reshape(sequences, length, width),
        gradient.reshape(sequences, length, width),
        down,
        jnp.swapaxes(up, 2, 3),
        m_down,
        v_down,
        jnp.swapaxes(m_up, 2, 3),
        jnp.swapaxes(v_up, 2, 3),
    )


def solution(mesh):
    acts, whole = P("batch", "seq", None), P()
    return jax.shard_map(
        shards,
        mesh=mesh,
        in_specs=(acts, acts, P("batch", "seq"), P("batch")) + (whole,) * 13,
        out_specs=(acts, acts) + (whole,) * 6,
        check_vma=False,
    )
```

time: 559 us -> 161 us (0.29); the launches traced: 550 us -> 161 us
  matrix products: 250 us -> 0 us
  Pallas kernels: 0 us -> 132 us
  waiting for transfers between devices: 120 us -> 7.78 us
  other arithmetic: 95.3 us -> 0.3 us
  local copies, waits for them, and re-layouts: 66.4 us -> 8.22 us
  between operations: 15.5 us -> 0.87 us
  starting transfers between devices: 0.37 us -> 11.5 us
    dot_general x50 -> x0, matrix products: 250 us -> none  [the longest x30 141 us: matmul(): return jnp.dot(left_side, right_side, preferred_element_type=jnp.float32)]
    pallas_call x0 -> x13, Pallas kernels: none -> 132 us  [the longest x12 130 us: call(): pl.pallas_call(kernel, name=name, out_shape=tuple((space(shape, dtype) fo...]
    psum x1 -> x0, waiting for transfers between devices: 115 us -> none  [shards(): lax.psum((down_gradient_total, up_gradient_total), ('seq', 'batch'))]
    another operation x10 -> x0, other arithmetic: 46 us -> none  [the longest x2 43.8 us: gelu_exact(): return jax.nn.gelu(values, approximate=False)]
    convert_element_type x5 -> x1, other arithmetic: 27 us -> 0.01 us  [key_and_query_ids(): values = ids.astype(F32)]
    convert_element_type x10 -> x0, local copies, waits for them, and re-layouts: 23.3 us -> none  [the longest x2 6.75 us: shards(): join_heads(value_terms, seq_width).astype(jnp.bfloat16)]
    unnamed x224 -> x28, local copies, waits for them, and re-layouts: 25.9 us -> 7.52 us
    reduce_sum x7 -> x0, other arithmetic: 13.5 us -> none  [the longest x2 9.73 us: shards(): row_sum = jnp.sum(shifted, axis=-1, keepdims=True)]
  transfers between devices with their start and end apart: 9 -> 11, of which waited for: 3 -> 6; matrix products, arithmetic and copies ran while one was open for 30% -> 1% of each run, Pallas kernels for 0% -> 21%
where the time goes in v1:
time: 161 us
  Pallas kernels  132 us (82%)
  starting transfers between devices  11.5 us (7%)
  local copies, waits for them, and re-layouts  8.22 us (5%)
  waiting for transfers between devices  7.78 us (5%)
    pallas_call x12, Pallas kernels, call(): pl.pallas_call(kernel, name=name, out_shape=tuple((space(shape, dtype) fo...  130 us
    ppermute x4, starting transfers between devices, sum_while(): come = lax.ppermute(mine, 'batch', [(i, i ^ step) for i in range(batch)])  9.56 us
    unnamed x28, local copies, waits for them, and re-layouts  7.52 us
    ppermute x4, waiting for transfers between devices, sum_while(): come = lax.ppermute(mine, 'batch', [(i, i ^ step) for i in range(batch)])  5.23 us
  transfers between devices with their start and end apart: 11, of which 6 were waited for; matrix products, arithmetic and copies ran while one was open for 1% of the time, Pallas kernels for 21%

profile of v1, /device:TPU:0, one launch (start us, length us, event | category | flops | bytes accessed | tf_op | source)
XLA Modules:
  0.0 160.9 jit_solution(15368485352471088030)
XLA Ops:
  1.2 6.7 %project_in.1 = (bf16[768,768]{1,0:T(8,128)(2,1)S(1)}, bf16[768,768]{1,0:T(8,128)(2,1)S(1)}, bf16[768,768]{1,0:T(8,128)(2,1)S(1)}, bf16[2,288,768]{2,1,0:T(8,128)(2,1)S(1)}, bf16[768,16]{1,0:T(8,128)(2,1)}) custom-call(bf16[768,768]{1,0:T(8,128)(2,1)} %bitcast.12, bf16[2,768,2304]{2,1,0:T(8,128)(2,1)} %w_hbm.7, f32[2,2,8,768]{3,2,1,0:T(8,128)} %down_ref.1, ...), custom_call_target="tpu_custom_call" | custom-call | flops 2717908992 | bytes 12000000 | tf_op jit(solution)/shard_map/project_in/pallas_call | solution.py:420
  11.1 1.3 copy-done.1
  12.4 1.3 copy-done.4
  13.6 1.3 copy-done.7
  14.9 3.1 %attention_far.2.far_ref = bf16[384,768]{1,0:T(8,128)(2,1)S(1)} custom-call(bf16[768,768]{1,0:T(8,128)(2,1)S(1)} %copy-done.1, bf16[768,768]{1,0:T(8,128)(2,1)S(1)} %copy-done.4, bf16[768,768]{1,0:T(8,128)(2,1)S(1)} %copy-done.7, f32[3,128]{1,0:T(4,128)S(1)} %get-tuple-element.142.qid_ref, f32[3,256]{1,0:T(4,128)S(1)} %compare_select_fusion.kid_ref), custom_call_target="tpu_custom_call" | custom-call | flops 2000000000 | bytes 6000000 | tf_op jit(solution)/shard_map/attention_far/pallas_call | solution.py:420
  18.9 23.8 %middle.1 = (bf16[768,768]{1,0:T(8,128)(2,1)S(1)}, bf16[768,768]{1,0:T(8,128)(2,1)S(1)}, bf16[768,768]{1,0:T(8,128)(2,1)S(1)}, bf16[2,288,768]{2,1,0:T(8,128)(2,...) custom-call(f32[3,128]{1,0:T(4,128)S(1)} %get-tuple-element.143.qid_, ...), custom_call_target="tpu_custom_call" | custom-call | flops 10871635968 | bytes 24000000 | tf_op jit(solution)/shard_map/middle/pallas_call | solution.py:420
  43.3 3.1 %attention_far.3.far_ref = bf16[384,768]{1,0:T(8,128)(2,1)S(1)} custom-call(bf16[768,768]{1,0:T(8,128)(2,1)S(1)} %get-tuple-element.79.q_ref, bf16[768,768]{1,0:T(8,128)(2,1)S(1)} %get-tuple-element.80.k_ref, bf16[768,768]{1,0:T(8,128)(2,1)S(1)} %get-tuple-element.81.v_ref, f32[3,128]{1,0:T(4,128)S(1)} %get-tuple-element.142.qid_ref, ...), custom_call_target="tpu_custom_call" | custom-call | flops 2000000000 | bytes 6000000 | tf_op jit(solution)/shard_map/attention_far/pallas_call | solution.py:420
  46.4 41.4 %turn.1 = (f32[768,768]{1,0:T(8,128)S(1)}, bf16[384,768]{1,0:T(8,128)(2,1)S(1)}, bf16[384,768]{1,0:T(8,128)(2,1)S(1)}, f32[960,768]{1,0:T(8,128)S(1)}, f32[960,7...) custom-call(f32[3,128]{1,0:T(4,128)S(1)} %get-tuple-element.143.qid_ref, ...), custom_call_target="tpu_custom_call" | custom-call | flops 16307453952 | bytes 24000000 | tf_op jit(solution)/shard_map/turn/pallas_call | solution.py:420
  87.9 7.3 %back_far.2 = (bf16[768,768]{1,0:T(8,128)(2,1)S(1)}, f32[768,768]{1,0:T(8,128)S(1)}, f32[768,768]{1,0:T(8,128)S(1)}) custom-call(f32[3,128]{1,0:T(4,128)S(1)} %get-tuple-element.142.qid_ref, f32[3,256]{1,0:T(4,128)S(1)} %compare_select_fusion.kid_ref, bf16[768,768]{1,0:T(8,128)(2,1)S(1)} %get-tuple-element.79.q_ref, ...), custom_call_target="tpu_custom_call" | custom-call | flops 4000000000 | bytes 16000000 | tf_op jit(solution)/shard_map/back_far/pallas_call | solution.py:420
  95.2 27.6 %back.1 = (f32[768,768]{1,0:T(8,128)S(1)}, bf16[384,768]{1,0:T(8,128)(2,1)S(1)}, bf16[384,768]{1,0:T(8,128)(2,1)S(1)}, f32[960,768]{1,0:T(8,128)S(1)}, f32[960,7...) custom-call(f32[3,128]{1,0:T(4,128)S(1)} %get-tuple-element.143.qid_, ...), custom_call_target="tpu_custom_call" | custom-call | flops 10871635968 | bytes 24000000 | tf_op jit(solution)/shard_map/back/pallas_call | solution.py:420
  123.4 7.4 %back_far.3 = (bf16[768,768]{1,0:T(8,128)(2,1)S(1)}, f32[768,768]{1,0:T(8,128)S(1)}, f32[768,768]{1,0:T(8,128)S(1)}) custom-call(f32[3,128]{1,0:T(4,128)S(1)} %get-tuple-element.142.qid_ref, f32[3,256]{1,0:T(4,128)S(1)} %compare_select_fusion.kid_ref, bf16[768,768]{1,0:T(8,128)(2,1)S(1)} %get-tuple-element.106.q_ref, ...), custom_call_target="tpu_custom_call" | custom-call | flops 4000000000 | bytes 16000000 | tf_op jit(solution)/shard_map/back_far/pallas_call | solution.py:420
  130.8 3.4 %adapter_back.1 = (bf16[768,768]{1,0:T(8,128)(2,1)S(1)}, bf16[768,768]{1,0:T(8,128)(2,1)S(1)}, bf16[768,16]{1,0:T(8,128)(2,1)S(1)}, bf16[768,2304]{1,0:T(8,128)(...) custom-call(bf16[768,768]{1,0:T(8,128)(2,1)S(1)} %get-tuple-element.113.dq_ref, ...), custom_call_target="tpu_custom_call" | custom-call | flops 500000000 | bytes 12000000 | tf_op jit(solution)/shard_map/adapter_back/pallas_call | solution.py:420
  134.3 1.2 collective-permute-done.5
  135.6 2.7 %collective-permute-start.6 = (f32[32,768]{1,0:T(8,128)S(1)}, f32[32,768]{1,0:T(8,128)S(1)}, u32[]{:S(2)}, u32[]{:S(2)}) collective-permute-start(f32[32,768]{1,0:T(8,128)S(1)} %add.39), channel_id=1, source_target_pairs={{0,1},{1,0},{2,3},{3,2},{4,5},{5,4},{6,7},{7,6},{8,9},{9,8},{10,11... | collective-permute-start | bytes 294920 | tf_op jit(solution)/shard_map/ppermute | solution.py:809
  138.3 2.1 %project_back.3.rest_0_ = f32[768,768]{1,0:T(8,128)} custom-call(f32[768,768]{1,0:T(8,128)S(1)} %get-tuple-element.132.datt_ref, bf16[768,768]{1,0:T(8,128)(2,1)S(1)} %get-tuple-element.113.dq_ref, bf16[768,768]{1,0:T(8,128)(2,1)S(1)} %get-tuple-element.123.dk_ref, bf16[768,768]{1,0:T(8,128)(2,1)S(1)} %get-tuple-element.124.dv_ref, ...), custom_call_target="tpu_custom_call" | custom-call | flops 905969664 | bytes 4000000 | tf_op jit(solution)/shard_map/project_back/pallas_call | solution.py:420
  140.4 1.2 collective-permute-done.6
  141.6 1.8 %collective-permute-start.7 = (f32[32,768]{1,0:T(8,128)S(1)}, f32[32,768]{1,0:T(8,128)S(1)}, u32[]{:S(2)}, u32[]{:S(2)}) collective-permute-start(f32[32,768]{1,0:T(8,128)S(1)} %add.40), channel_id=1, source_target_pairs={{0,2},{1,3},{2,0},{3,1},{4,6},{5,7},{6,4},{7,5},{8,10},{9,11},{10,... | collective-permute-start | bytes 294920 | tf_op jit(solution)/shard_map/ppermute | solution.py:809
  143.4 2.1 %project_back.4.rest_0_ = f32[768,768]{1,0:T(8,128)} custom-call(f32[768,768]{1,0:T(8,128)S(1)} %get-tuple-element.132.datt_ref, bf16[768,768]{1,0:T(8,128)(2,1)S(1)} %get-tuple-element.113.dq_ref, bf16[768,768]{1,0:T(8,128)(2,1)S(1)} %get-tuple-element.123.dk_ref, bf16[768,768]{1,0:T(8,128)(2,1)S(1)} %get-tuple-element.124.dv_ref, ...), custom_call_target="tpu_custom_call", output_to_operand_aliasing={{}: (7, {})} | custom-call | flops 905969664 | bytes 4000000 | tf_op jit(solution)/shard_map/project_back/pallas_call | solution.py:420
  146.3 1.9 %collective-permute-start.8 = (f32[32,768]{1,0:T(8,128)S(1)}, f32[32,768]{1,0:T(8,128)S(1)}, u32[]{:S(2)}, u32[]{:S(2)}) collective-permute-start(f32[32,768]{1,0:T(8,128)S(1)} %add.41), channel_id=1, source_target_pairs={{0,4},{1,5},{2,6},{3,7},{4,0},{5,1},{6,2},{7,3},{8,12},{9,13},{10,... | collective-permute-start | bytes 294920 | tf_op jit(solution)/shard_map/ppermute | solution.py:809
  148.2 2.1 %project_back.5 = f32[768,768]{1,0:T(8,128)} custom-call(f32[768,768]{1,0:T(8,128)S(1)} %get-tuple-element.132.datt_ref, bf16[768,768]{1,0:T(8,128)(2,1)S(1)} %get-tuple-element.113.dq_ref, bf16[768,768]{1,0:T(8,128)(2,1)S(1)} %get-tuple-element.123.dk_ref, bf16[768,768]{1,0:T(8,128)(2,1)S(1)} %get-tuple-element.124.dv_ref, ...), custom_call_target="tpu_custom_call", output_to_operand_aliasing={{}: (7, {})} | custom-call | flops 905969664 | bytes 4000000 | tf_op jit(solution)/shard_map/project_back/pallas_call | solution.py:420
  151.0 3.1 %collective-permute-start.9 = (f32[32,768]{1,0:T(8,128)S(1)}, f32[32,768]{1,0:T(8,128)S(1)}, u32[]{:S(2)}, u32[]{:S(2)}) collective-permute-start(f32[32,768]{1,0:T(8,128)S(1)} %add.42), channel_id=1, source_target_pairs={{0,8},{1,9},{2,10},{3,11},{4,12},{5,13},{6,14},{7,15},{8,0},{9,1},... | collective-permute-start | bytes 294920 | tf_op jit(solution)/shard_map/ppermute | solution.py:809
  154.1 2.6 %collective-permute-done.9 = f32[32,768]{1,0:T(8,128)S(1)} collective-permute-done((f32[32,768]{1,0:T(8,128)S(1)}, f32[32,768]{1,0:T(8,128)S(1)}, u32[]{:S(2)}, u32[]{:S(2)}) %collective-permute-start.9) | collective-permute-done | bytes 98336 | tf_op jit(solution)/shard_map/ppermute | solution.py:809
  156.8 1.3 collective-permute-done.10.theirs_ref
  158.7 2.1 %adam.1 = (f32[2,2,8,768]{3,2,1,0:T(8,128)}, f32[2,2,8,768]{3,2,1,0:T(8,128)}, f32[2,2,8,768]{3,2,1,0:T(8,128)}, f32[2,2,8,768]{3,2,1,0:T(8,128)}, f32[2,2,8,768]{3,2,1,0:T(8,128)}, /*index=5*/f32[2,2,8,768]{3,2,1,0:T(8,128)}) custom-call(f32[32,768]{1,0:T(8,128)} %copy-done.9, f32[32,768]{1,0:T(8,128)} %copy-done.10, s32[2,2,2]{2,1,0:T(2,128)} %steps_ref.1, ...), custom_call_target="tpu_custom_call" | custom-call | tf_op jit(solution)/shard_map/adam/pallas_call | solution.py:793
  (53 shorter events, 8.1 us)
Async XLA Ops:
  0.6 18.1 %collective-permute-start = (s32[3,256]{1,0:T(4,128)}, s32[3,256]{1,0:T(4,128)S(1)}, u32[]{:S(2)}, u32[]{:S(2)}) collective-permute-start(s32[3,256]{1,0:T(4,128)} %param.19), channel_id=1, source_target_pairs={{0,16},{16,0},{1,17},{17,1},{2,18},{18,2},{3,19},{19,3},{4,20},{20... | collective-permute-start | bytes 9224 | tf_op jit(solution)/shard_map/ppermute | solution.py:822
  1.2 9.8 %copy-start.11 = (s32[3,256]{1,0:T(4,128)S(1)}, s32[3,256]{1,0:T(4,128)}, u32[]{:S(2)}) copy-start(s32[3,256]{1,0:T(4,128)} %param.19) | copy-start | bytes 9220
  1.2 9.9 %copy-start.13 = (s32[3]{0:T(128)S(1)}, s32[3]{0:T(128)}, u32[]{:S(2)}) copy-start(s32[3]{0:T(128)} %live_ref.1) | copy-start | bytes 40
  7.9 1.0 copy-start
  8.9 1.0 copy-start.3
  9.9 1.0 copy-start.6
  10.9 8.0 %collective-permute-start.1 = (bf16[2,288,768]{2,1,0:T(8,128)(2,1)S(1)}, bf16[2,288,768]{2,1,0:T(8,128)(2,1)S(1)}, u32[]{:S(2)}, u32[]{:S(2)}) collective-permute-start(bf16[2,288,768]{2,1,0:T(8,128)(2,1)S(1)} %get-tuple-element.78), channel_id=1, source_target_pairs={{0,16},{16,0},{1,17},{17,1},{2,18},{18,2},{3,19},{19,3},{4,20},{20... | collective-permute-start | bytes 2654216 | tf_op jit(solution)/shard_map/ppermute | solution.py:869
  11.1 1.3 copy-start.1
  12.4 1.3 copy-start.4
  13.6 1.3 copy-start.7
  14.9 3.2 %copy-start.12 = (bf16[2,3072]{1,0:T(2,128)(2,1)S(1)}, bf16[2,3072]{1,0:T(2,128)(2,1)}, u32[]{:S(2)}) copy-start(bf16[2,3072]{1,0:T(2,128)(2,1)} %param.27) | copy-start | bytes 36868
  14.9 4.0 %copy-start.2 = (bf16[768,768]{1,0:T(8,128)(2,1)S(1)}, bf16[768,768]{1,0:T(8,128)(2,1)}, u32[]{:S(2)}) copy-start(bf16[768,768]{1,0:T(8,128)(2,1)} %copy-done) | copy-start | bytes 3538948
  14.9 4.0 %copy-start.5 = (bf16[768,768]{1,0:T(8,128)(2,1)S(1)}, bf16[768,768]{1,0:T(8,128)(2,1)}, u32[]{:S(2)}) copy-start(bf16[768,768]{1,0:T(8,128)(2,1)} %copy-done.3) | copy-start | bytes 3538948
  14.9 4.0 %copy-start.8 = (bf16[768,768]{1,0:T(8,128)(2,1)S(1)}, bf16[768,768]{1,0:T(8,128)(2,1)}, u32[]{:S(2)}) copy-start(bf16[768,768]{1,0:T(8,128)(2,1)} %copy-done.6) | copy-start | bytes 3538948
  42.8 3.6 %collective-permute-start.2 = (bf16[2,288,768]{2,1,0:T(8,128)(2,1)S(1)}, bf16[2,288,768]{2,1,0:T(8,128)(2,1)S(1)}, u32[]{:S(2)}, u32[]{:S(2)}) collective-permute-start(bf16[2,288,768]{2,1,0:T(8,128)(2,1)S(1)} %get-tuple-element.82), channel_id=1, source_target_pairs={{0,16},{16,0},{1,17},{17,1},{2,18},{18,2},{3,19},{19,3},{4,20},{20... | collective-permute-start | bytes 2654216 | tf_op jit(solution)/shard_map/ppermute | solution.py:873
  87.8 7.4 %collective-permute-start.3 = (bf16[2,288,768]{2,1,0:T(8,128)(2,1)S(1)}, bf16[2,288,768]{2,1,0:T(8,128)(2,1)S(1)}, u32[]{:S(2)}, u32[]{:S(2)}) collective-permute-start(bf16[2,288,768]{2,1,0:T(8,128)(2,1)S(1)} %get-tuple-element.92), channel_id=1, source_target_pairs={{0,16},{16,0},{1,17},{17,1},{2,18},{18,2},{3,19},{19,3},{4,20},{20... | collective-permute-start | bytes 2654216 | tf_op jit(solution)/shard_map/ppermute | solution.py:878
  122.8 7.9 %collective-permute-start.4 = (bf16[2,288,768]{2,1,0:T(8,128)(2,1)S(1)}, bf16[2,288,768]{2,1,0:T(8,128)(2,1)S(1)}, u32[]{:S(2)}, u32[]{:S(2)}) collective-permute-start(bf16[2,288,768]{2,1,0:T(8,128)(2,1)S(1)} %get-tuple-element.116), channel_id=1, source_target_pairs={{0,16},{16,0},{1,17},{17,1},{2,18},{18,2},{3,19},{19,3},{4,20},{20... | collective-permute-start | bytes 2654216 | tf_op jit(solution)/shard_map/ppermute | solution.py:882
  134.2 1.4 collective-permute-start.5
  135.6 6.0 %collective-permute-start.6 = (f32[32,768]{1,0:T(8,128)S(1)}, f32[32,768]{1,0:T(8,128)S(1)}, u32[]{:S(2)}, u32[]{:S(2)}) collective-permute-start(f32[32,768]{1,0:T(8,128)S(1)} %add.39), channel_id=1, source_target_pairs={{0,1},{1,0},{2,3},{3,2},{4,5},{5,4},{6,7},{7,6},{8,9},{9,8},{10,11... | collective-permute-start | bytes 294920 | tf_op jit(solution)/shard_map/ppermute | solution.py:809
  141.6 4.7 %collective-permute-start.7 = (f32[32,768]{1,0:T(8,128)S(1)}, f32[32,768]{1,0:T(8,128)S(1)}, u32[]{:S(2)}, u32[]{:S(2)}) collective-permute-start(f32[32,768]{1,0:T(8,128)S(1)} %add.40), channel_id=1, source_target_pairs={{0,2},{1,3},{2,0},{3,1},{4,6},{5,7},{6,4},{7,5},{8,10},{9,11},{10,... | collective-permute-start | bytes 294920 | tf_op jit(solution)/shard_map/ppermute | solution.py:809
  146.3 4.7 %collective-permute-start.8 = (f32[32,768]{1,0:T(8,128)S(1)}, f32[32,768]{1,0:T(8,128)S(1)}, u32[]{:S(2)}, u32[]{:S(2)}) collective-permute-start(f32[32,768]{1,0:T(8,128)S(1)} %add.41), channel_id=1, source_target_pairs={{0,4},{1,5},{2,6},{3,7},{4,0},{5,1},{6,2},{7,3},{8,12},{9,13},{10,... | collective-permute-start | bytes 294920 | tf_op jit(solution)/shard_map/ppermute | solution.py:809
  151.0 5.7 %collective-permute-start.9 = (f32[32,768]{1,0:T(8,128)S(1)}, f32[32,768]{1,0:T(8,128)S(1)}, u32[]{:S(2)}, u32[]{:S(2)}) collective-permute-start(f32[32,768]{1,0:T(8,128)S(1)} %add.42), channel_id=1, source_target_pairs={{0,8},{1,9},{2,10},{3,11},{4,12},{5,13},{6,14},{7,15},{8,0},{9,1},... | collective-permute-start | bytes 294920 | tf_op jit(solution)/shard_map/ppermute | solution.py:809
  156.7 1.4 copy-start.9
  156.7 1.4 collective-permute-start.10
  (1 other events, 0.6 us)

commit v2 on v1

v2 whole, which is shorter than its diff:
```python
import jax
import jax.numpy as jnp
from jax import lax
from jax.experimental import pallas as pl
from jax.experimental.pallas import tpu as pltpu
from jax.sharding import PartitionSpec as P

HEADS = 12
ENCODER_LAYERS = 2
HALO = 96
BLOCK = 128
SUB = 64
WINDOW = 256
QUAD = 256
HEAD_ROWS = 16
MASKED = -1000000000.0
LOG2E = 1.4426950408889634
F32 = jnp.float32
BF16 = jnp.bfloat16


def dot_nn(a, b):
    return lax.dot_general(a, b, (((1,), (0,)), ((), ())), preferred_element_type=F32)


def dot_nt(a, b):
    return lax.dot_general(a, b, (((1,), (1,)), ((), ())), preferred_element_type=F32)


def dot_tn(a, b):
    return lax.dot_general(a, b, (((0,), (0,)), ((), ())), preferred_element_type=F32)


def rows_at(start, size, multiple):
    return pl.ds(pl.multiple_of(start, multiple), size)


def loop(count, body):
    def step(i, carry):
        body(i)
        return carry

    lax.fori_loop(0, count, step, 0)


def picked(row_ref, i):
    row = row_ref[...].astype(F32)
    at = lax.broadcasted_iota(jnp.int32, row.shape, 1) == i
    return jnp.sum(jnp.where(at, row, 0.0), axis=1, keepdims=True)


def column_of(row):
    n = row.shape[1]
    eye = lax.broadcasted_iota(jnp.int32, (n, n), 0) == lax.broadcasted_iota(jnp.int32, (n, n), 1)
    return jnp.sum(jnp.where(eye, row, 0.0), axis=1, keepdims=True)


def low_lanes():
    return (lax.broadcasted_iota(jnp.int32, (SUB, 128), 1) < 64).astype(F32).astype(BF16)


def spread_heads(tile, low):
    zero = jnp.zeros((2 * SUB, 128), BF16)
    high = 1 - low
    left, right = tile[:, :128], tile[:, 128:]
    left = jnp.concatenate([left * low, left * high], axis=0)
    right = jnp.concatenate([right * low, right * high], axis=0)
    return jnp.concatenate([jnp.concatenate([left, zero], axis=1),
                            jnp.concatenate([zero, right], axis=1)], axis=0)


def gather_heads(wide):
    low = lax.broadcasted_iota(jnp.int32, (SUB, 128), 1) < 64
    parts = []
    for i in range(2):
        cols, top = slice(128 * i, 128 * i + 128), 2 * SUB * i
        parts.append(jnp.where(low, wide[top:top + SUB, cols],
                               wide[top + SUB:top + 2 * SUB, cols]))
    return jnp.concatenate(parts, axis=1)


def pipelined(units):
    units = list(units)
    live = []
    while units or live:
        if units:
            live.append(units.pop(0))
        for unit in list(live):
            if next(unit, None) is None:
                live.remove(unit)


class Side:
    def __init__(self, near, length, ids_refs):
        self.near, self.length, self.ids_refs = near, length, ids_refs
        self.side = lax.axis_index("seq")
        self.row0 = BLOCK * ((1 - self.side) if near else self.side)

    def ids(self, s):
        own_ref, other_ref, live_ref = self.ids_refs
        own = own_ref[pl.ds(s, 1), :].astype(F32)
        query = jnp.where(self.row0 == 0, own[:, :BLOCK], own[:, BLOCK:])
        if self.near:
            other = other_ref[pl.ds(s, 1), :].astype(F32)
            kept = WINDOW + SUB - HALO
            key = jnp.where(
                self.side == 0,
                jnp.concatenate([own[:, self.length - kept:], other[:, :HALO]], axis=1),
                jnp.concatenate([other[:, self.length - HALO:], own[:, :kept]], axis=1))
            start = jnp.where(self.side == 0, self.length - kept, self.length - HALO)
        else:
            key, start = own, self.side * self.length
        places = lax.broadcasted_iota(jnp.int32, key.shape, 1) + start
        return query, jnp.where(places.astype(F32) < picked(live_ref, s), key, -1.0)

    def queries(self, s, sub):
        return rows_at(s * self.length + self.row0 + sub * SUB, SUB, SUB)

    def keys(self, s, sub):
        if self.near:
            return rows_at(s * (WINDOW + SUB) + sub * SUB, WINDOW, SUB)
        return rows_at(s * self.length, WINDOW, WINDOW)

    def biases(self, sequences, rows_ref, columns_ref):
        lane = lax.broadcasted_iota(jnp.int32, (1, 128), 1)
        place = jnp.where(lane < SUB, lane, lane - SUB)
        key_place = lax.broadcasted_iota(jnp.int32, (WINDOW, 128), 0)
        shape = (SUB, WINDOW)
        apart = lax.broadcasted_iota(jnp.int32, shape, 1) - lax.broadcasted_iota(jnp.int32, shape, 0)

        def one(s):
            query, key = self.ids(s)
            for sub in range(2):
                own = HALO if self.near else self.row0 + sub * SUB
                if rows_ref is not None:
                    keys = key[:, sub * SUB:sub * SUB + WINDOW] if self.near else key
                    queries = column_of(query)[sub * SUB:(sub + 1) * SUB]
                    seen = (queries == keys) | (apart == own)
                    rows_ref[rows_at((s * 2 + sub) * SUB, SUB, SUB), :] = jnp.where(
                        seen, 0.0, MASKED)
                if columns_ref is None:
                    continue
                blocks = (128, 128, SUB) if self.near else (128, 128)
                column = jnp.concatenate(
                    [column_of(key[:, 128 * i:128 * i + n]) for i, n in enumerate(blocks)], axis=0)
                keys = column[sub * SUB:sub * SUB + WINDOW] if self.near else column
                turned = pltpu.roll(query, SUB, 1)
                pair = (query, turned) if sub == 0 else (turned, query)
                seen = (keys == jnp.where(lane < SUB, *pair)) | (key_place == place + own)
                columns_ref[rows_at((s * 2 + sub) * WINDOW, WINDOW, WINDOW), :] = jnp.where(
                    seen, 0.0, MASKED)

        loop(sequences, one)


def bias_shape(sequences, turned):
    return ((sequences * 2 * WINDOW, 128) if turned else (sequences * 2 * SUB, WINDOW)), F32


def half(sub):
    return slice(4 * SUB * sub, 4 * SUB * (sub + 1))


SLOTS = 2


def attention_scratch():
    return [((SLOTS, WINDOW, 4 * SUB), F32), ((SLOTS, WINDOW, 4 * SUB), BF16)]


def attention_forward(where, s, q_ref, k_ref, v_ref, out_ref, out_rows, bias_ref, scratch):
    low = low_lanes()
    scores_ref, share_ref = scratch[:2]

    def unit(quad, sub):
        cols = slice(QUAD * quad, QUAD * quad + QUAD)
        keys = where.keys(s, sub)
        q4 = spread_heads(q_ref[where.queries(s, sub), cols], low)
        slot = (2 * quad + sub) % SLOTS
        scores_ref[slot] = dot_nt(q4, k_ref[keys, cols])
        yield True
        bias = bias_ref[rows_at((s * 2 + sub) * SUB, SUB, SUB), :]
        totals = []
        for h in range(4):
            rows = slice(h * SUB, (h + 1) * SUB)
            scores = scores_ref[slot, rows, :] + bias
            share = jnp.exp2(scores - jnp.max(scores, axis=1, keepdims=True))
            totals.append(1.0 / jnp.sum(share, axis=1, keepdims=True))
            share_ref[slot, rows, :] = share.astype(BF16)
        yield True
        mixed = dot_nn(share_ref[slot], v_ref[keys, cols])
        mixed = jnp.concatenate(
            [mixed[h * SUB:(h + 1) * SUB] * totals[h] for h in range(4)], axis=0)
        yield True
        out_ref[out_rows(s, sub), cols] = gather_heads(mixed).astype(BF16)

    width = q_ref.shape[1]
    pipelined(unit(quad, sub) for quad in range(width // QUAD) for sub in range(2))


def attention_backward(where, s, q_ref, k_ref, v_ref, dmix_ref, dmix_rows, delta_ref, dq_ref,
                       dq_rows, key_terms, bias_ref):
    low = low_lanes()
    delta = delta_ref[rows_at(s * HEAD_ROWS, HEAD_ROWS, HEAD_ROWS), :]
    delta = jnp.where(where.row0 == 0, delta[:, :BLOCK], delta[:, BLOCK:])
    turned = pltpu.roll(delta, SUB, 1)
    first_half = lax.broadcasted_iota(jnp.int32, (1, 2 * SUB), 1) < SUB

    def unit(quad, sub, kept):
        cols = slice(QUAD * quad, QUAD * quad + QUAD)
        keys = where.keys(s, sub)
        q4 = spread_heads(q_ref[where.queries(s, sub), cols], low)
        d4 = spread_heads(dmix_ref[dmix_rows(s, sub), cols], low)
        scores = dot_nt(k_ref[keys, cols], q4)
        d_share = dot_nt(v_ref[keys, cols], d4)
        yield True
        bias = bias_ref[rows_at((s * 2 + sub) * WINDOW, WINDOW, WINDOW), :]
        shares, d_scores = [], []
        left, right = (delta, turned) if sub == 0 else (turned, delta)
        for i in range(2):
            head = 4 * quad + 2 * i
            drop = jnp.where(first_half, left[head:head + 1], right[head + 1:head + 2])
            part = scores[:, 128 * i:128 * i + 128] + bias
            part = jnp.exp2(part - jnp.max(part, axis=0, keepdims=True))
            part = part * (1.0 / jnp.sum(part, axis=0, keepdims=True))
            shares.append(part.astype(BF16))
            d_scores.append((part * (d_share[:, 128 * i:128 * i + 128] - drop)).astype(BF16))
        d_scores = jnp.concatenate(d_scores, axis=1)
        kept.append((jnp.concatenate(shares, axis=1), d_scores, q4, d4))
        yield True
        d_query = gather_heads(dot_tn(d_scores, k_ref[keys, cols])) * 0.125
        dq_ref[dq_rows(s, sub), cols] = d_query.astype(BF16)
        if sub == 1:
            key_terms(s, cols, kept)

    width = q_ref.shape[1]

    def units():
        for quad in range(width // QUAD):
            kept = []
            for sub in range(2):
                yield unit(quad, sub, kept)

    pipelined(units())


def row_deltas(sequences, length, dmix_ref, mix_ref, delta_ref):
    width = dmix_ref.shape[1]
    shape = (HEAD_ROWS, width)
    own = (lax.broadcasted_iota(jnp.int32, shape, 1) // 64
           == lax.broadcasted_iota(jnp.int32, shape, 0)).astype(F32).astype(BF16)

    def one(s):
        rows = rows_at(s * length, length, length)
        product = dmix_ref[rows, :].astype(F32) * mix_ref[rows, :].astype(F32)
        high = product.astype(BF16)
        rest = (product - high.astype(F32)).astype(BF16)
        delta_ref[rows_at(s * HEAD_ROWS, HEAD_ROWS, HEAD_ROWS), :] = (
            dot_nt(own, high) + dot_nt(own, rest))

    loop(sequences, one)


def near_keys(s, length, k_ref, v_ref, halo_ref, nk_ref, nv_ref):
    side = lax.axis_index("seq")
    wide, own = WINDOW + SUB, WINDOW + SUB - HALO
    given = rows_at(s * HALO, HALO, 32)
    for i, (src, dst) in enumerate(((k_ref, nk_ref), (v_ref, nv_ref))):
        dst[rows_at(s * wide + HALO * side, own, 32), :] = src[
            rows_at(s * length + (length - own) * (1 - side), own, 32), :]
        dst[rows_at(s * wide + own * (1 - side), HALO, 32), :] = halo_ref[i, given, :]


def norm_forward(values, gain, shift):
    center = values - jnp.mean(values, axis=1, keepdims=True)
    spread = jnp.mean(center * center, axis=1, keepdims=True)
    inverse = lax.rsqrt(spread + 1e-05)
    scaled = center * inverse
    return scaled * gain + shift, scaled, inverse


def norm_backward(gradient, scaled, inverse, gain):
    inner = gradient * gain
    return inverse * (
        inner
        - jnp.mean(inner, axis=1, keepdims=True)
        - scaled * jnp.mean(inner * scaled, axis=1, keepdims=True)
    )


def low_rank(a_ref, b_ref):
    down = jnp.concatenate([a_ref[0], a_ref[1]], axis=0).astype(BF16)
    zero = jnp.zeros_like(b_ref[0])
    up_q = jnp.concatenate([b_ref[0], zero], axis=0).astype(BF16)
    up_v = jnp.concatenate([zero, b_ref[1]], axis=0).astype(BF16)
    return down, up_q, up_v


def project_in(sequences, length, x_ref, w_ref, waits, a_ref, b_ref, vec_ref, q_ref, k_ref, v_ref,
               u_ref, send_ref, sent):
    side = lax.axis_index("seq")
    width = x_ref.shape[1]
    waits[0]()
    down, up_q, up_v = low_rank(a_ref, b_ref)
    vec = vec_ref[...].astype(F32)

    def send(s, i, ref):
        taken = rows_at(s * length + (1 - side) * (length - HALO), HALO, 32)
        send_ref[i, rows_at(s * HALO, HALO, 32), :] = ref[taken, :]

    def queries(s):
        rows = rows_at(s * length, length, length)
        x = x_ref[rows, :]
        inner = dot_nt(x, down).astype(BF16)
        u_ref[rows, :] = inner
        q = dot_nn(x, w_ref[:, :width]) + vec[0:1] + 2.0 * dot_nn(inner, up_q)
        q_ref[rows, :] = (q * (0.125 * LOG2E)).astype(BF16)

    def keys(s):
        rows = rows_at(s * length, length, length)
        k_ref[rows, :] = dot_nn(x_ref[rows, :], w_ref[:, width:2 * width]).astype(BF16)
        send(s, 0, k_ref)

    def values(s):
        rows = rows_at(s * length, length, length)
        v = dot_nn(x_ref[rows, :], w_ref[:, 2 * width:]) + vec[1:2]
        v_ref[rows, :] = (v + 2.0 * dot_nn(u_ref[rows, :], up_v)).astype(BF16)
        send(s, 1, v_ref)

    loop(sequences, queries)
    sent()
    waits[1]()
    loop(sequences, keys)
    waits[2]()
    loop(sequences, values)


def layer_rest(layer, sequences, length, mix_ref, h_ref, wo_ref, wu_ref, wd_ref, waits, vec_ref, bu_ref,
               one_ref, low_ref, act_ref, n1_ref, r1_ref, dg_ref, n2_ref, r2_ref, h_outs, sent):
    hidden = wu_ref.shape[1]
    waits[0]()
    vec = vec_ref[...].astype(F32)

    def mixed(s):
        rows = rows_at(s * length, length, length)
        attended = dot_nn(mix_ref[rows, :], wo_ref[...]) + vec[2:3] + h_ref[rows, :].astype(F32)
        one, scaled, inverse = norm_forward(attended, vec[4:5], vec[5:6])
        n1_ref[rows, :] = scaled.astype(n1_ref.dtype)
        r1_ref[rows, :] = jnp.broadcast_to(inverse, (length, 128))
        one_ref[rows, :] = one
        low_ref[rows, :] = one.astype(BF16)

    loop(sequences, mixed)
    sent(0)
    waits[1]()
    tile = 512

    def up(j):
        cols = rows_at(j * tile, tile, tile)
        bias = bu_ref[layer:layer + 1, cols].astype(F32)
        weights = wu_ref[:, cols]

        def unit(s):
            rows = slice(s * length, (s + 1) * length)
            gate = dot_nn(low_ref[rows, :], weights)
            yield True
            gate = gate + bias
            below = 0.5 * lax.erf(gate * 0.7071067811865476) + 0.5
            act_ref[rows, cols] = (gate * below).astype(BF16)
            density = jnp.exp2(gate * gate * -0.7213475204444817) * 0.3989422804014327
            dg_ref[rows, cols] = (below + gate * density).astype(BF16)

        pipelined(unit(s) for s in range(sequences))

    loop(hidden // tile, up)
    sent(1)
    waits[2]()

    def down(s):
        rows = rows_at(s * length, length, length)
        summed = dot_nn(act_ref[rows, :], wd_ref[...]) + vec[3:4] + one_ref[rows, :]
        out, scaled, inverse = norm_forward(summed, vec[6:7], vec[7:8])
        n2_ref[rows, :] = scaled.astype(n2_ref.dtype)
        r2_ref[rows, :] = jnp.broadcast_to(inverse, (length, 128))
        for h_out in h_outs:
            h_out[rows, :] = out.astype(h_out.dtype)

    loop(sequences, down)
    sent(2)


def layer_rest_back(sequences, length, gradient, waits, n1_ref, r1_ref, dg_ref, n2_ref, r2_ref,
                    wo_ref, wu_ref, wd_ref, vec_ref, two_ref, low_ref, gate_ref, datt_ref,
                    mix_ref, delta_ref):
    hidden = wu_ref.shape[1]
    waits[0]()
    vec = vec_ref[...].astype(F32)

    def second(s):
        rows = rows_at(s * length, length, length)
        two = norm_backward(
            gradient(s, rows), n2_ref[rows, :].astype(F32), r2_ref[rows, 0:1], vec[6:7])
        two_ref[rows, :] = two
        low_ref[rows, :] = two.astype(BF16)

    loop(sequences, second)
    waits[1]()
    tile = 512

    def down(j):
        cols = rows_at(j * tile, tile, tile)
        weights = wd_ref[cols, :]

        def unit(s):
            rows = slice(s * length, (s + 1) * length)
            gate = dot_nt(low_ref[rows, :], weights)
            yield True
            gate_ref[rows, cols] = (gate * dg_ref[rows, cols].astype(F32)).astype(BF16)

        pipelined(unit(s) for s in range(sequences))

    loop(hidden // tile, down)
    waits[2]()
    waits[3]()

    def up(s):
        rows = rows_at(s * length, length, length)
        one = dot_nt(gate_ref[rows, :], wu_ref[...]) + two_ref[rows, :]
        att = norm_backward(one, n1_ref[rows, :].astype(F32), r1_ref[rows, 0:1], vec[4:5])
        datt_ref[rows, :] = att
        dmix = dot_nt(att.astype(BF16), wo_ref[...]).astype(BF16)
        low_ref[rows, :] = dmix

    loop(sequences, up)
    row_deltas(sequences, length, low_ref, mix_ref, delta_ref)


def near_backward(near, sequences, length, q_ref, nk_ref, nv_ref, dmix_ref, delta_ref,
                  dfar_ref, dq_ref, dnk_ref, dnv_ref, dhalo_ref, bias_ref):
    side, wide = near.side, WINDOW + SUB

    def key_terms(s, cols, kept):
        for out, which, other in ((dnv_ref, 0, 3), (dnk_ref, 1, 2)):
            left, right = [item[which] for item in kept], [item[other] for item in kept]
            out[rows_at(s * wide, SUB, SUB), cols] = dot_nn(left[0][:SUB], right[0])
            both = jnp.concatenate([left[0][SUB:], left[1][:WINDOW - SUB]], axis=1)
            out[rows_at(s * wide + SUB, WINDOW - SUB, SUB), cols] = dot_nn(
                both, jnp.concatenate(right, axis=0))
            out[rows_at(s * wide + WINDOW, SUB, SUB), cols] = dot_nn(
                left[1][WINDOW - SUB:], right[1])

    def one(s):
        dfar_ref[rows_at(s * BLOCK, BLOCK, BLOCK), :] = dmix_ref[
            rows_at(s * length + side * BLOCK, BLOCK, BLOCK), :]
        attention_backward(
            near, s, q_ref, nk_ref, nv_ref, dmix_ref, near.queries, delta_ref, dq_ref,
            lambda s, sub: rows_at(s * BLOCK + sub * SUB, SUB, SUB), key_terms, bias_ref)
        halo = rows_at(s * wide + (wide - HALO) * (1 - side), HALO, 32)
        dhalo_ref[0, rows_at(s * HALO, HALO, 32), :] = (
            dnk_ref[halo, :] * (1.0 / LOG2E)).astype(BF16)
        dhalo_ref[1, rows_at(s * HALO, HALO, 32), :] = dnv_ref[halo, :].astype(BF16)

    loop(sequences, one)


def adapter_back(sequences, length, waits, dq_ref, dk_ref, dv_ref, dhalo_ref, u_ref, x_ref, a_ref,
                 b_ref, dkb_ref, dvb_ref, du_ref, grad_ref):
    side = lax.axis_index("seq")
    rank = a_ref.shape[1]
    waits[0]()
    _, up_q, up_v = low_rank(a_ref, b_ref)

    def one(s):
        rows = rows_at(s * length, length, length)
        taken = rows_at(s * length + (1 - side) * (length - HALO), HALO, 32)
        hrows = rows_at(s * HALO, HALO, 32)
        dk_ref[rows, :] = dk_ref[rows, :] * (1.0 / LOG2E)
        dk_ref[taken, :] = dk_ref[taken, :] + dhalo_ref[0, hrows, :].astype(F32)
        dv_ref[taken, :] = dv_ref[taken, :] + dhalo_ref[1, hrows, :].astype(F32)
        dkb_ref[rows, :] = dk_ref[rows, :].astype(BF16)
        dv16 = dv_ref[rows, :].astype(BF16)
        dvb_ref[rows, :] = dv16
        du_ref[rows, :] = (2.0 * (dot_nt(dq_ref[rows, :], up_q) + dot_nt(dv16, up_v))).astype(BF16)

    loop(sequences, one)
    waits[1]()
    u = u_ref[...]
    grad_ref[0:2 * rank, :] = dot_tn(du_ref[...], x_ref[...])
    up_q, up_v = dot_tn(u, dq_ref[...]), dot_tn(u, dvb_ref[...])
    grad_ref[2 * rank:3 * rank, :] = 2.0 * up_q[:rank]
    grad_ref[3 * rank:, :] = 2.0 * up_v[rank:]


def project_back(rows, own_rows, datt_ref, dq_ref, dk_ref, dv_ref, du_ref, w_ref, down):
    width = dq_ref.shape[1]
    out = datt_ref[rows, :] + dot_nn(du_ref[rows, :], down)
    out = out + dot_nt(dq_ref[rows, :], w_ref[:, :width])
    out = out + dot_nt(dk_ref[rows, :], w_ref[:, width:2 * width])
    return out + dot_nt(dv_ref[rows, :], w_ref[:, 2 * width:])


HBM, VMEM = pltpu.HBM, pltpu.VMEM


def call(kernel, name, args, outs, scratch, flops, nbytes, limit, aliases=None):
    scratch = [pltpu.SemaphoreType.DMA((s,)) if isinstance(s, int) else pltpu.VMEM(*s)
               for s in scratch]
    return pl.pallas_call(
        kernel,
        name=name,
        out_shape=tuple(space(shape, dtype) for space, shape, dtype in outs),
        in_specs=[pl.BlockSpec(memory_space=space) for space, _ in args],
        out_specs=tuple(pl.BlockSpec(memory_space=space) for space, _, _ in outs),
        scratch_shapes=scratch,
        input_output_aliases=aliases or {},
        compiler_params=pltpu.CompilerParams(vmem_limit_bytes=limit * 1024 * 1024),
        cost_estimate=pl.CostEstimate(flops=flops, bytes_accessed=nbytes, transcendentals=0),
    )(*[pltpu.with_memory_space_constraint(array, space) for space, array in args])


def sds(shape, dtype):
    return jax.ShapeDtypeStruct(shape, dtype)


def copies_of(pairs, sems):
    return [pltpu.make_async_copy(src, dst, sems.at[i]) for i, (src, dst) in enumerate(pairs)]


def start_all(copies):
    for copy in copies:
        copy.start()
    return copies


def wait_for(copies, *which):
    def wait():
        for i in which:
            copies[i].wait()

    return wait


def first_call(layer, sequences, length, x, w, a, b, vec):
    tokens, width = x.shape
    rank = a.shape[2]

    def kernel(x_hbm, w_hbm, a_hbm, b_hbm, vec_hbm, q_ref, k_ref, v_ref, send_ref, u_out, x_ref,
               w_ref, a_ref, b_ref, vec_ref, u_ref, sems, outs):
        thirds = [slice(i * width, (i + 1) * width) for i in range(3)]
        copies = start_all(copies_of(
            [(a_hbm.at[layer], a_ref), (b_hbm.at[layer], b_ref), (vec_hbm.at[layer], vec_ref),
             (x_hbm, x_ref)] + [(w_hbm.at[layer, :, part], w_ref.at[:, part]) for part in thirds],
            sems))
        store = pltpu.make_async_copy(u_ref, u_out, outs.at[0])
        project_in(sequences, length, x_ref, w_ref,
                   [wait_for(copies, 0, 1, 2, 3, 4), wait_for(copies, 5), wait_for(copies, 6)],
                   a_ref, b_ref, vec_ref, q_ref, k_ref, v_ref, u_ref, send_ref, store.start)
        store.wait()

    act, small = (VMEM, (tokens, width), BF16), ((tokens, 2 * rank), BF16)
    return call(
        kernel, "project_in", [(HBM, x), (HBM, w), (HBM, a), (HBM, b), (HBM, vec)],
        [act, act, act, (VMEM, (2, sequences * HALO, width), BF16), (HBM,) + small],
        [((tokens, width), BF16), ((width, 3 * width), BF16), ((2, rank, width), F32),
         ((2, rank, width), F32), ((8, width), BF16), small, 7, 1],
        2 * tokens * width * width * 3, 12000000, 10)


def far_call(sequences, length, q, k, v, ids):
    tokens, width = q.shape

    def kernel(q_ref, k_ref, v_ref, own_ref, live_ref, out_ref, bias_ref, *scratch):
        where = Side(False, length, (own_ref, None, live_ref))
        where.biases(sequences, bias_ref, None)
        loop(sequences, lambda s: attention_forward(
            where, s, q_ref, k_ref, v_ref, out_ref,
            lambda s, sub: rows_at(s * BLOCK + sub * SUB, SUB, SUB), bias_ref, scratch))

    return call(
        kernel, "attention_far", [(VMEM, item) for item in (q, k, v, ids[0])] + [(VMEM, ids[2])],
        [(VMEM, (sequences * BLOCK, width), BF16)],
        [bias_shape(sequences, False)] + attention_scratch(), 2000000000, 6000000, 8)[0]


def near_forward(near, sequences, length, far_ref, q_ref, k_ref, v_ref, halo_ref, nk_ref,
                 nv_ref, mix_ref, bias_ref, scratch):
    def one(s):
        near_keys(s, length, k_ref, v_ref, halo_ref, nk_ref, nv_ref)
        mix_ref[rows_at(s * length + near.side * BLOCK, BLOCK, BLOCK), :] = far_ref[
            rows_at(s * BLOCK, BLOCK, BLOCK), :]
        attention_forward(near, s, q_ref, nk_ref, nv_ref, mix_ref, near.queries, bias_ref,
                          scratch)

    loop(sequences, one)


def middle_call(layer, sequences, length, ids, far, q, k, v, halo, h, w, a, b, wo, wu, wd, vec,
                bias_up):
    tokens, width = q.shape
    hidden, rank = wu.shape[2], a.shape[2]

    def kernel(own_ref, other_ref, live_ref, far_ref, q_ref, k_ref, v_ref, halo_ref, h_hbm, w_hbm, a_hbm,
               b_hbm, wo_hbm, wu_hbm, wd_hbm, vec_hbm, bu_hbm,
               q2_ref, k2_ref, v2_ref, send_ref,
               u_out, x_out, h_out, n1_out, r1_out, dg_out, n2_out, r2_out, q_out, k_out, v_out,
               nk_out, nv_out, mix_out,
               h_ref, w_ref, wo_ref, wu_ref, wd_ref, vec_ref, bu_ref, vec2_ref, a_ref, b_ref,
               u_ref, mix_ref, one_ref, low_ref, act_ref,
               n1_ref, r1_ref, dg_ref, n2_ref, r2_ref, nk_ref, nv_ref, ins, outs, bias_ref,
               *scratch):
        loads = start_all(copies_of(
            [(h_hbm, h_ref), (vec_hbm.at[layer], vec_ref), (wo_hbm.at[layer], wo_ref),
             (bu_hbm, bu_ref), (wu_hbm.at[layer], wu_ref), (wd_hbm.at[layer], wd_ref),
             (w_hbm.at[layer + 1], w_ref), (a_hbm.at[layer + 1], a_ref),
             (b_hbm.at[layer + 1], b_ref), (vec_hbm.at[layer + 1], vec2_ref)], ins))
        stores = copies_of(
            [(q_ref, q_out), (k_ref, k_out), (v_ref, v_out), (nk_ref, nk_out), (nv_ref, nv_out),
             (n1_ref, n1_out), (r1_ref, r1_out), (dg_ref, dg_out), (n2_ref, n2_out),
             (r2_ref, r2_out), (one_ref, h_out), (low_ref, x_out), (u_ref, u_out),
             (mix_ref, mix_out)], outs)
        near = Side(True, length, (own_ref, other_ref, live_ref))
        near.biases(sequences, bias_ref, None)
        near_forward(near, sequences, length, far_ref, q_ref, k_ref, v_ref, halo_ref, nk_ref,
                     nv_ref, mix_ref, bias_ref, scratch)
        layer_rest(layer, sequences, length, mix_ref, h_ref, wo_ref, wu_ref, wd_ref,
                   [wait_for(loads, 0, 1, 2), wait_for(loads, 3, 4), wait_for(loads, 5)], vec_ref,
                   bu_ref, one_ref, low_ref, act_ref, n1_ref, r1_ref, dg_ref, n2_ref, r2_ref,
                   (one_ref, low_ref),
                   lambda i: start_all((stores[:7] + stores[13:], stores[7:8], stores[8:12])[i]))
        nothing = wait_for(loads)
        project_in(sequences, length, low_ref, w_ref,
                   [wait_for(loads, 6, 7, 8, 9), nothing, nothing], a_ref, b_ref, vec2_ref, q2_ref,
                   k2_ref, v2_ref, u_ref, send_ref, stores[12].start)
        for copy in stores:
            copy.wait()

    act, stat = ((tokens, width), BF16), ((tokens, 128), F32)
    wide, deep = ((tokens, width), F32), ((tokens, hidden), BF16)
    near, small = ((sequences * (WINDOW + SUB), width), BF16), ((tokens, 2 * rank), BF16)
    factors = ((2, rank, width), F32)
    return call(
        kernel, "middle",
        [(VMEM, ids[0]), (VMEM, ids[1]), (VMEM, ids[2]), (VMEM, far), (VMEM, q), (VMEM, k), (VMEM, v),
         (VMEM, halo)]
        + [(HBM, item) for item in (h, w, a, b, wo, wu, wd, vec, bias_up)],
        [(VMEM,) + act, (VMEM,) + act, (VMEM,) + act, (VMEM, (2, sequences * HALO, width), BF16)]
        + [(HBM,) + item for item in (small, act, wide, act, stat, deep, act, stat, act, act, act,
                                      near, near, act)],
        [(h.shape, h.dtype), ((width, 3 * width), BF16), ((width, width), BF16),
         ((width, hidden), BF16), ((hidden, width), BF16), ((8, width), BF16),
         (bias_up.shape, BF16), ((8, width), BF16), factors, factors, small, act, wide, act, deep,
         act, stat, deep, act, stat, near, near, 10, 14,
         bias_shape(sequences, False)] + attention_scratch(),
        2 * tokens * width * (2 * hidden + 4 * width), 24000000, 42)


def turn_call(layer, sequences, length, ids, far, q, k, v, halo, h, gradient, wo, wu, wd,
              vec, bias_up):
    tokens, width = q.shape
    hidden = wu.shape[2]

    def kernel(own_ref, other_ref, live_ref, far_ref, q_ref, k_ref, v_ref, halo_ref, h_hbm, g_hbm,
               wo_hbm, wu_hbm, wd_hbm, vec_hbm, bu_hbm,
               datt_ref, dfar_ref, dq_ref, dnk_ref, dnv_ref, dhalo_ref, delta_ref, hidden_out,
               h_ref, g_ref, wo_ref, wu_ref, wd_ref, vec_ref, bu_ref, mix_ref, one_ref, low_ref,
               act_ref, n1_ref, r1_ref, dg_ref, n2_ref, r2_ref, nk_ref, nv_ref, last_ref, ins, outs,
               bias_ref, columns_ref, *scratch):
        loads = start_all(copies_of(
            [(h_hbm, h_ref), (vec_hbm.at[layer], vec_ref), (wo_hbm.at[layer], wo_ref),
             (bu_hbm, bu_ref), (wu_hbm.at[layer], wu_ref), (wd_hbm.at[layer], wd_ref),
             (g_hbm, g_ref)], ins))
        store = pltpu.make_async_copy(last_ref, hidden_out, outs.at[0])
        near = Side(True, length, (own_ref, other_ref, live_ref))
        near.biases(sequences, bias_ref, columns_ref)
        near_forward(near, sequences, length, far_ref, q_ref, k_ref, v_ref, halo_ref, nk_ref,
                     nv_ref, mix_ref, bias_ref, scratch)
        side = lax.axis_index("seq")
        layer_rest(layer, sequences, length, mix_ref, h_ref, wo_ref, wu_ref, wd_ref,
                   [wait_for(loads, 0, 1, 2), wait_for(loads, 3, 4), wait_for(loads, 5)], vec_ref,
                   bu_ref, one_ref, low_ref, act_ref, n1_ref, r1_ref, dg_ref, n2_ref, r2_ref,
                   (last_ref,), lambda i: None)
        store.start()

        def given(s, rows):
            places = lax.broadcasted_iota(jnp.int32, (length, 1), 0) + side * length
            return jnp.where(
                places.astype(F32) < picked(live_ref, s), g_ref[rows, :].astype(F32), 0.0)

        nothing = wait_for(loads)
        layer_rest_back(sequences, length, given,
                        [wait_for(loads, 6), nothing, nothing, nothing], n1_ref,
                        r1_ref, dg_ref, n2_ref, r2_ref, wo_ref, wu_ref, wd_ref, vec_ref, one_ref,
                        low_ref, act_ref, datt_ref, mix_ref, delta_ref)
        near_backward(near, sequences, length, q_ref, nk_ref, nv_ref, low_ref,
                      delta_ref, dfar_ref, dq_ref, dnk_ref, dnv_ref, dhalo_ref, columns_ref)
        store.wait()

    act, stat = ((tokens, width), BF16), ((tokens, 128), F32)
    wide, deep = ((tokens, width), F32), ((tokens, hidden), BF16)
    near_rows = sequences * (WINDOW + SUB)
    near, block = ((near_rows, width), BF16), ((sequences * BLOCK, width), BF16)
    return call(
        kernel, "turn",
        [(VMEM, ids[0]), (VMEM, ids[1]), (VMEM, ids[2]), (VMEM, far), (VMEM, q), (VMEM, k),
         (VMEM, v), (VMEM, halo)]
        + [(HBM, item) for item in (h, gradient, wo, wu, wd, vec, bias_up)],
        [(VMEM,) + wide, (VMEM,) + block, (VMEM,) + block, (VMEM, (near_rows, width), F32),
         (VMEM, (near_rows, width), F32), (VMEM, (2, sequences * HALO, width), BF16),
         (VMEM, (HEAD_ROWS * sequences, length), F32), (HBM,) + act],
        [(h.shape, h.dtype), act, ((width, width), BF16), ((width, hidden), BF16),
         ((hidden, width), BF16), ((8, width), BF16), (bias_up.shape, BF16), act, wide, act, deep,
         act, stat, deep, act, stat, near, near, act, 7, 1, bias_shape(sequences, False),
         bias_shape(sequences, True)] + attention_scratch(),
        4 * tokens * width * (2 * hidden + width), 24000000, 42)


def back_far_call(sequences, length, ids, q, k, v, dfar, delta, dq_near, dnk, dnv):
    tokens, width = q.shape

    def kernel(own_ref, live_ref, q_ref, k_ref, v_ref, dfar_ref, delta_ref, dqn_ref, dnk_ref,
               dnv_ref, dq_ref, dk_ref, dv_ref, bias_ref):
        far = Side(False, length, (own_ref, None, live_ref))
        far.biases(sequences, None, bias_ref)
        side, wide, own = far.side, WINDOW + SUB, WINDOW + SUB - HALO

        def key_terms(s, cols, kept):
            for out, which, other in ((dv_ref, 0, 3), (dk_ref, 1, 2)):
                left = jnp.concatenate([item[which] for item in kept], axis=1)
                right = jnp.concatenate([item[other] for item in kept], axis=0)
                out[far.keys(s, 0), cols] = dot_nn(left, right)

        def one(s):
            attention_backward(
                far, s, q_ref, k_ref, v_ref, dfar_ref,
                lambda s, sub: rows_at(s * BLOCK + sub * SUB, SUB, SUB), delta_ref, dq_ref,
                far.queries, key_terms, bias_ref)
            dq_ref[rows_at(s * length + (1 - side) * BLOCK, BLOCK, BLOCK), :] = dqn_ref[
                rows_at(s * BLOCK, BLOCK, BLOCK), :]
            mine = rows_at(s * length + (length - own) * (1 - side), own, 32)
            theirs = rows_at(s * wide + HALO * side, own, 32)
            dk_ref[mine, :] = dk_ref[mine, :] + dnk_ref[theirs, :]
            dv_ref[mine, :] = dv_ref[mine, :] + dnv_ref[theirs, :]

        loop(sequences, one)

    wide = (VMEM, (tokens, width), F32)
    return call(
        kernel, "back_far",
        [(VMEM, ids[0]), (VMEM, ids[2])]
        + [(VMEM, item) for item in (q, k, v, dfar, delta, dq_near, dnk, dnv)],
        [(VMEM, (tokens, width), BF16), wide, wide],
        [bias_shape(sequences, True)], 4000000000, 16000000, 8)


def back_call(layer, sequences, length, ids, dq, dk, dv, dhalo, datt, u, x, saved, w, a, b, wo, wu,
              wd, vec):
    tokens, width = dq.shape
    hidden, rank = wu.shape[2], a.shape[2]

    def kernel(own_ref, other_ref, live_ref, dq_ref, dk_ref, dv_ref, dhalo_ref, datt_ref, u_hbm, x_hbm,
               n1_hbm, r1_hbm, dg_hbm, n2_hbm, r2_hbm, q_hbm, k_hbm, v_hbm, nk_hbm, nv_hbm, mix_hbm,
               w_hbm, a_hbm, b_hbm, wo_hbm, wu_hbm, wd_hbm, vec_hbm,
               datt_out, dfar_ref, dqn_ref, dnk_ref, dnv_ref, dhalo_out, delta_ref, q_ref, k_ref,
               v_ref, grad_out,
               u_ref, x_ref, n1_ref, r1_ref, dg_ref, n2_ref, r2_ref, nk_ref, nv_ref, w_ref,
               a_ref, b_ref, wo_ref, wu_ref, wd_ref, vec_ref, dkb_ref, dvb_ref, du_ref, grad_ref,
               two_ref, low_ref, mix_ref, ins, outs, bias_ref):
        loads = start_all(copies_of(
            [(a_hbm.at[layer + 1], a_ref), (b_hbm.at[layer + 1], b_ref), (u_hbm, u_ref),
             (x_hbm, x_ref), (w_hbm.at[layer + 1], w_ref), (vec_hbm.at[layer], vec_ref),
             (n2_hbm, n2_ref), (r2_hbm, r2_ref), (wd_hbm.at[layer], wd_ref), (dg_hbm, dg_ref),
             (wu_hbm.at[layer], wu_ref), (n1_hbm, n1_ref), (r1_hbm, r1_ref),
             (wo_hbm.at[layer], wo_ref), (q_hbm, q_ref), (nk_hbm, nk_ref), (nv_hbm, nv_ref),
             (k_hbm, k_ref), (v_hbm, v_ref), (mix_hbm, mix_ref)], ins))
        adapter_back(sequences, length, [wait_for(loads, 0, 1), wait_for(loads, 2, 3)], dq_ref, dk_ref, dv_ref, dhalo_ref, u_ref, x_ref,
                     a_ref, b_ref, dkb_ref, dvb_ref, du_ref, grad_ref)
        store = pltpu.make_async_copy(grad_ref, grad_out, outs.at[0])
        store.start()
        down, _, _ = low_rank(a_ref, b_ref)

        def given(s, rows):
            return project_back(rows, rows, datt_ref, dq_ref, dkb_ref, dvb_ref, du_ref, w_ref,
                                down)

        layer_rest_back(sequences, length, given,
                        [wait_for(loads, 4, 5, 6, 7), wait_for(loads, 8, 9), wait_for(loads, 10),
                         wait_for(loads, 11, 12, 13, 19)], n1_ref, r1_ref, dg_ref, n2_ref, r2_ref,
                        wo_ref, wu_ref, wd_ref, vec_ref, two_ref, low_ref, dg_ref, datt_out,
                        mix_ref, delta_ref)
        wait_for(loads, 14, 15, 16)()
        near = Side(True, length, (own_ref, other_ref, live_ref))
        near.biases(sequences, None, bias_ref)
        near_backward(near, sequences, length, q_ref, nk_ref, nv_ref, low_ref,
                      delta_ref, dfar_ref, dqn_ref, dnk_ref, dnv_ref, dhalo_out, bias_ref)
        wait_for(loads, 17, 18)()
        store.wait()

    act, stat = ((tokens, width), BF16), ((tokens, 128), F32)
    wide, deep = ((tokens, width), F32), ((tokens, hidden), BF16)
    near_rows = sequences * (WINDOW + SUB)
    near, block = ((near_rows, width), BF16), ((sequences * BLOCK, width), BF16)
    small, factors = ((tokens, 2 * rank), BF16), ((2, rank, width), F32)
    grad = ((4 * rank, width), F32)
    return call(
        kernel, "back",
        [(VMEM, ids[0]), (VMEM, ids[1]), (VMEM, ids[2])]
        + [(VMEM, item) for item in (dq, dk, dv, dhalo, datt)]
        + [(HBM, item) for item in (u, x, *saved, w, a, b, wo, wu, wd, vec)],
        [(VMEM,) + wide, (VMEM,) + block, (VMEM,) + block,
         (VMEM, (near_rows, width), F32), (VMEM, (near_rows, width), F32),
         (VMEM, (2, sequences * HALO, width), BF16), (VMEM, (HEAD_ROWS * sequences, length), F32),
         (VMEM,) + act, (VMEM,) + act, (VMEM,) + act,
         (HBM,) + grad],
        [small, act, act, stat, deep, act, stat, near, near, ((width, 3 * width), BF16), factors,
         factors, ((width, width), BF16), ((width, hidden), BF16), ((hidden, width), BF16),
         ((8, width), BF16), act, act, small, grad, wide, act, act, 20, 1, bias_shape(sequences, True)],
        2 * tokens * width * (2 * hidden + 4 * width), 24000000, 38)


def last_call(layer, sequences, length, dq, dk, dv, dhalo, u, x, w, a, b, other, *state):
    tokens, width = dq.shape
    rank = a.shape[2]

    def kernel(dq_ref, dk_ref, dv_ref, dhalo_ref, u_hbm, x_hbm, w_hbm, a_hbm, b_hbm, other_hbm,
               *rest):
        given, rest = rest[:len(state)], rest[len(state):]
        (dkb_ref, dvb_ref, du_ref, w_ref, down_ref, mine_ref, theirs_ref), rest = rest[:7], rest[7:]
        taken, rest = rest[:len(state)], rest[len(state):]
        u_ref, x_ref, a_ref, b_ref, other_ref, grad_ref, sems, state_sems = rest
        loads = start_all(copies_of(
            [(a_hbm.at[layer], a_ref), (b_hbm.at[layer], b_ref), (u_hbm, u_ref), (x_hbm, x_ref),
             (other_hbm, other_ref), (w_hbm.at[layer], w_ref)], sems))
        more = start_all(copies_of(zip(given, taken), state_sems))
        adapter_back(sequences, length, [wait_for(loads, 0, 1), wait_for(loads, 2, 3)], dq_ref, dk_ref, dv_ref, dhalo_ref, u_ref, x_ref,
                     a_ref, b_ref, dkb_ref, dvb_ref, du_ref, grad_ref)
        down_ref[...] = low_rank(a_ref, b_ref)[0]
        wait_for(loads, 4)()
        first = lax.axis_index("seq") == layer
        here, there = grad_ref[...], other_ref[...]
        mine_ref[...] = jnp.where(first, here, there)
        theirs_ref[...] = jnp.where(first, there, here)
        wait_for(loads, 5)()
        for copy in more:
            copy.wait()

    act, grad = ((tokens, width), BF16), ((4 * rank, width), F32)
    small, factors = ((tokens, 2 * rank), BF16), ((2, rank, width), F32)
    return call(
        kernel, "adapter_back",
        [(VMEM, dq), (VMEM, dk), (VMEM, dv), (VMEM, dhalo)]
        + [(HBM, item) for item in (u, x, w, a, b, other, *state)],
        [(VMEM,) + act, (VMEM,) + act, (VMEM,) + small, (VMEM, (width, 3 * width), BF16),
         (VMEM, (2 * rank, width), BF16), (VMEM,) + grad, (VMEM,) + grad]
        + [(VMEM, item.shape, F32) for item in state],
        [small, act, factors, factors, grad, grad, 6, len(state)], 500000000, 12000000, 8)


def project_back_call(part, parts, datt, dq, dk, dv, du, w, down, out):
    tokens, width = dq.shape
    length = tokens // parts

    def kernel(datt_ref, dq_ref, dk_ref, dv_ref, du_ref, w_ref, down_ref, *rest):
        out_hbm, out_ref, sems = rest[-3:]
        rows = slice(part * length, (part + 1) * length)
        out_ref[...] = project_back(rows, rows, datt_ref, dq_ref, dk_ref, dv_ref, du_ref, w_ref,
                                    down_ref[...])
        store = pltpu.make_async_copy(out_ref, out_hbm.at[rows], sems.at[0])
        store.start()
        store.wait()

    args = [(VMEM, item) for item in (datt, dq, dk, dv, du, w, down)]
    return call(
        kernel, "project_back", args + ([] if out is None else [(HBM, out)]),
        [(HBM, (tokens, width), F32)], [((length, width), F32), 1],
        2 * length * width * width * 3, 4000000, 6, {} if out is None else {len(args): 0})[0]


def adam_call(mine, theirs, token_slots, steps, down, up, m_down, v_down, m_up, v_up):
    layers, two, rank, width = down.shape

    def kernel(mine_ref, theirs_ref, steps_ref, down_ref, up_ref, md_ref, vd_ref, mu_ref, vu_ref,
               *rest):
        outs, results, sems = rest[:6], rest[6:12], rest[12]
        down_out, up_out, md_out, vd_out, mu_out, vu_out = results
        side = lax.axis_index("seq")
        for layer in range(layers):
            for which in range(two):
                for group, (w_ref, m_ref, v_ref, w_out, m_out, v_out, rate, decay) in enumerate((
                    (down_ref, md_ref, vd_ref, down_out, md_out, vd_out, 0.03125, 0.1),
                    (up_ref, mu_ref, vu_ref, up_out, mu_out, vu_out, 0.5, 0.0),
                )):
                    rows = slice((group * two + which) * rank, (group * two + which + 1) * rank)
                    grad = jnp.where(side == layer, mine_ref[rows, :], theirs_ref[rows, :])
                    grad = grad / token_slots
                    step = picked(steps_ref, (layer * two + which) * 2 + group)
                    correction = jnp.broadcast_to(1.0 - jnp.exp2(-step), (rank, width))
                    weight = w_ref[layer, which]
                    moment = 0.5 * m_ref[layer, which] + 0.5 * grad
                    velocity = 0.5 * v_ref[layer, which] + 0.5 * grad * grad
                    size = moment / correction / (jnp.sqrt(velocity / correction) + 1e-08)
                    w_out[layer, which] = weight - rate * (size + decay * weight)
                    m_out[layer, which] = moment
                    v_out[layer, which] = velocity

        for store in start_all(copies_of(zip(results, outs), sems)):
            store.wait()

    return call(
        kernel, "adam",
        [(VMEM, mine), (VMEM, theirs), (VMEM, steps)]
        + [(VMEM, item) for item in (down, up, m_down, v_down, m_up, v_up)],
        [(HBM, down.shape, F32)] * 6, [(down.shape, F32)] * 6 + [6], 1000000, 2000000, 4)


def together(*values):
    return lax.optimization_barrier(values)


def sum_while(mine, theirs, work):
    batch = lax.axis_size("batch")
    swap = [(0, 1), (1, 0)]
    mine = mine + lax.ppermute(theirs, "seq", swap)
    done, work, step = None, list(work), 1
    while step < batch:
        ways = 4 if batch % (4 * step) == 0 else 2
        given = mine.astype(BF16)
        come = [lax.ppermute(given, "batch", [(i, i ^ (step * d)) for i in range(batch)])
                for d in range(1, ways)]
        if work:
            done = work.pop(0)(mine, done)
            *come, done = together(*come, done)
        mine = mine + sum(item.astype(F32) for item in come)
        step *= ways
    for one in work:
        done = one(mine, done)
    return mine, lax.ppermute(mine, "seq", swap), done


def shards(
    first_layer_input,
    output_gradient,
    sentence_pair_index,
    sequence_live_length,
    optimizer_step_count,
    query_key_value_weight,
    attention_output_weight,
    feedforward_up_weight,
    feedforward_down_weight,
    layer_bias_gain_rows,
    feedforward_up_bias,
    adapter_down_factors,
    adapter_up_factors,
    first_moment_down,
    second_moment_down,
    first_moment_up,
    second_moment_up,
):
    sequences, length, width = first_layer_input.shape
    tokens = sequences * length
    swap = [(0, 1), (1, 0)]
    a, b = adapter_down_factors, jnp.swapaxes(adapter_up_factors, 2, 3)
    vec = layer_bias_gain_rows
    bias_up = feedforward_up_bias
    wqkv, wo = query_key_value_weight, attention_output_weight
    wu, wd = feedforward_up_weight, feedforward_down_weight
    ids = (sentence_pair_index, lax.ppermute(sentence_pair_index, "seq", swap),
           sequence_live_length[None, :])
    shape = (sequences, length)

    x1 = first_layer_input.reshape(tokens, width)
    q1, k1, v1, send, u1 = first_call(0, *shape, x1, wqkv, a, b, vec)
    halo = lax.ppermute(send, "seq", swap)
    far = far_call(*shape, q1, k1, v1, ids)
    q2, k2, v2, send, u2, x2, h1, *saved = middle_call(
        0, *shape, ids, far, q1, k1, v1, halo, x1, wqkv, a, b, wo, wu, wd, vec, bias_up)
    halo = lax.ppermute(send, "seq", swap)
    far = far_call(*shape, q2, k2, v2, ids)
    datt, dfar, dqn, dnk, dnv, dsend, delta, hidden_out = turn_call(
        1, *shape, ids, far, q2, k2, v2, halo, h1, output_gradient.reshape(tokens, width),
        wo, wu, wd, vec, bias_up)
    dhalo = lax.ppermute(dsend, "seq", swap)
    dq, dk, dv = back_far_call(*shape, ids, q2, k2, v2, dfar, delta, dqn, dnk, dnv)
    datt, dfar, dqn, dnk, dnv, dsend, delta, q1, k1, v1, grad2 = back_call(
        0, *shape, ids, dq, dk, dv, dhalo, datt, u2, x2, saved, wqkv, a, b, wo, wu, wd, vec)
    dhalo = lax.ppermute(dsend, "seq", swap)
    dq, dk, dv = back_far_call(*shape, ids, q1, k1, v1, dfar, delta, dqn, dnk, dnv)
    dk, dv, du, w1, down1, mine, theirs, *state = last_call(
        0, *shape, dq, dk, dv, dhalo, u1, x1, wqkv, a, b, grad2, a, b, first_moment_down,
        second_moment_down, jnp.swapaxes(first_moment_up, 2, 3),
        jnp.swapaxes(second_moment_up, 2, 3))

    def part(i, parts):
        def work(token, out):
            now, _ = together(datt, token)
            return project_back_call(i, parts, now, dq, dk, dv, du, w1, down1, out)

        return work

    mine, theirs, gradient = sum_while(mine, theirs, [part(i, 2) for i in range(2)])
    token_slots = tokens * lax.axis_size("seq") * lax.axis_size("batch")
    down, up, m_down, v_down, m_up, v_up = adam_call(
        mine, theirs, token_slots, optimizer_step_count.reshape(1, -1), *state)
    return (
        hidden_out.reshape(sequences, length, width),
        gradient.reshape(sequences, length, width),
        down,
        jnp.swapaxes(up, 2, 3),
        m_down,
        v_down,
        jnp.swapaxes(m_up, 2, 3),
        jnp.swapaxes(v_up, 2, 3),
    )


def solution(mesh):
    acts, whole = P("batch", "seq", None), P()
    return jax.shard_map(
        shards,
        mesh=mesh,
        in_specs=(acts, acts, P("batch", "seq"), P("batch")) + (whole,) * 13,
        out_specs=(acts, acts) + (whole,) * 6,
        check_vma=False,
    )
```

time: 161 us -> 146 us (0.907)
  local copies, waits for them, and re-layouts: 8.22 us -> 0.09 us
  Pallas kernels: 132 us -> 126 us
    unnamed x28 -> x6, local copies, waits for them, and re-layouts: 7.52 us -> 0.01 us
    pallas_call x12, Pallas kernels: 130 us -> 126 us  [call(): pl.pallas_call(kernel, name=name, out_shape=tuple((space(shape, dtype) fo...]
    pallas_call x1 -> x0, Pallas kernels: 2.12 us -> none  [adam_call(): pl.pallas_call(kernel, name='adam', out_shape=shapes, in_specs=[vmem, vme...]
    ppermute x5 -> x7, starting transfers between devices: 10.1 us -> 8.8 us  [the longest x6 8.72 us: sum_while(): lax.ppermute(given, 'batch', [(i, i ^ step * d) for i in range(batch)])]
    ppermute x5 -> x7, waiting for transfers between devices: 5.23 us -> 5.1 us  [the longest x6 5.1 us: sum_while(): lax.ppermute(given, 'batch', [(i, i ^ step * d) for i in range(batch)])]
  transfers between devices with their start and end apart: 11 -> 13, of which waited for: 6 -> 5; matrix products, arithmetic and copies ran while one was open for 1% -> 0% of each run, Pallas kernels for 21% -> 17%
where the time goes in v2:
time: 146 us; the launch traced here: 145 us
  Pallas kernels  126 us (86%)
  starting transfers between devices  10.7 us (7%)
  waiting for transfers between devices  7.56 us (5%)
    pallas_call x12, Pallas kernels, call(): pl.pallas_call(kernel, name=name, out_shape=tuple((space(shape, dtype) fo...  126 us
    ppermute x6, starting transfers between devices, sum_while(): lax.ppermute(given, 'batch', [(i, i ^ step * d) for i in range(batch)])  8.72 us
    ppermute x6, waiting for transfers between devices, sum_while(): lax.ppermute(given, 'batch', [(i, i ^ step * d) for i in range(batch)])  5.1 us
  transfers between devices with their start and end apart: 13, of which 5 were waited for; matrix products, arithmetic and copies ran while one was open for 0% of the time, Pallas kernels for 17%

profile of v2, /device:TPU:0, one launch (start us, length us, event | category | flops | bytes accessed | tf_op | source)
XLA Modules:
  0.0 145.4 jit_solution(17192585772105973460)
XLA Ops:
  0.7 7.0 %project_in.1 = (bf16[768,768]{1,0:T(8,128)(2,1)S(1)}, bf16[768,768]{1,0:T(8,128)(2,1)S(1)}, bf16[768,768]{1,0:T(8,128)(2,1)S(1)}, bf16[2,288,768]{2,1,0:T(8,128)(2,1)S(1)}, bf16[768,16]{1,0:T(8,128)(2,1)}) custom-call(bf16[768,768]{1,0:T(8,128)(2,1)} %bitcast.19, bf16[2,768,2304]{2,1,0:T(8,128)(2,1)} %w_hbm.7, f32[2,2,8,768]{3,2,1,0:T(8,128)} %rest_0_.1, ...), custom_call_target="tpu_custom_call" | custom-call | flops 2717908992 | bytes 12000000 | tf_op jit(solution)/shard_map/project_in/pallas_call | solution.py:508
  7.7 0.5 collective-permute-start.1
  8.3 2.7 %attention_far.2.far_ref = bf16[384,768]{1,0:T(8,128)(2,1)S(1)} custom-call(bf16[768,768]{1,0:T(8,128)(2,1)S(1)} %get-tuple-element.85.q_ref, bf16[768,768]{1,0:T(8,128)(2,1)S(1)} %get-tuple-element.86.k_ref, bf16[768,768]{1,0:T(8,128)(2,1)S(1)} %get-tuple-element.87.v_ref, s32[3,256]{1,0:T(4,128)S(1)} %copy-done, s32[1,3]{1,0:T(1,128)S(1)} %bitcast.11), custom_call_target="tpu_custom_call" | custom-call | flops 2000000000 | bytes 6000000 | tf_op jit(solution)/shard_map/attention_far/pallas_call | solution.py:508
  11.0 22.9 %middle.1 = (bf16[768,768]{1,0:T(8,128)(2,1)S(1)}, bf16[768,768]{1,0:T(8,128)(2,1)S(1)}, bf16[768,768]{1,0:T(8,128)(2,1)S(1)}, bf16[2,288,768]{2,1,0:T(8,128)(2,...) custom-call(s32[3,256]{1,0:T(4,128)S(1)} %copy-done, ...), custom_call_target="tpu_custom_call" | custom-call | flops 10871635968 | bytes 24000000 | tf_op jit(solution)/shard_map/middle/pallas_call | solution.py:508
  33.9 0.5 collective-permute-start.2
  34.4 2.8 %attention_far.3.far_ref = bf16[384,768]{1,0:T(8,128)(2,1)S(1)} custom-call(bf16[768,768]{1,0:T(8,128)(2,1)S(1)} %get-tuple-element.89.q_ref, bf16[768,768]{1,0:T(8,128)(2,1)S(1)} %get-tuple-element.90.k_ref, bf16[768,768]{1,0:T(8,128)(2,1)S(1)} %get-tuple-element.91.v_ref, s32[3,256]{1,0:T(4,128)S(1)} %copy-done, s32[1,3]{1,0:T(1,128)S(1)} %bitcast.13), custom_call_target="tpu_custom_call" | custom-call | flops 2000000000 | bytes 6000000 | tf_op jit(solution)/shard_map/attention_far/pallas_call | solution.py:508
  37.2 39.3 %turn.1 = (f32[768,768]{1,0:T(8,128)S(1)}, bf16[384,768]{1,0:T(8,128)(2,1)S(1)}, bf16[384,768]{1,0:T(8,128)(2,1)S(1)}, f32[960,768]{1,0:T(8,128)S(1)}, f32[960,7...) custom-call(s32[3,256]{1,0:T(4,128)S(1)} %copy-done, ...), custom_call_target="tpu_custom_call" | custom-call | flops 16307453952 | bytes 24000000 | tf_op jit(solution)/shard_map/turn/pallas_call | solution.py:508
  76.6 6.8 %back_far.2 = (bf16[768,768]{1,0:T(8,128)(2,1)S(1)}, f32[768,768]{1,0:T(8,128)S(1)}, f32[768,768]{1,0:T(8,128)S(1)}) custom-call(s32[3,256]{1,0:T(4,128)S(1)} %copy-done, s32[1,3]{1,0:T(1,128)S(1)} %bitcast.15, bf16[768,768]{1,0:T(8,128)(2,1)S(1)} %get-tuple-element.89.q_ref, bf16[768,768]{1,0:T(8,128)(2,1)S(1)} %get-tuple-element.90.k_ref, ...), custom_call_target="tpu_custom_call" | custom-call | flops 4000000000 | bytes 16000000 | tf_op jit(solution)/shard_map/back_far/pallas_call | solution.py:508
  83.5 27.9 %back.1 = (f32[768,768]{1,0:T(8,128)S(1)}, bf16[384,768]{1,0:T(8,128)(2,1)S(1)}, bf16[384,768]{1,0:T(8,128)(2,1)S(1)}, f32[960,768]{1,0:T(8,128)S(1)}, f32[960,7...) custom-call(s32[3,256]{1,0:T(4,128)S(1)} %copy-done, ...), custom_call_target="tpu_custom_call" | custom-call | flops 10871635968 | bytes 24000000 | tf_op jit(solution)/shard_map/back/pallas_call | solution.py:508
  111.4 0.5 collective-permute-start.4
  112.0 7.0 %back_far.3 = (bf16[768,768]{1,0:T(8,128)(2,1)S(1)}, f32[768,768]{1,0:T(8,128)S(1)}, f32[768,768]{1,0:T(8,128)S(1)}) custom-call(s32[3,256]{1,0:T(4,128)S(1)} %copy-done, s32[1,3]{1,0:T(1,128)S(1)} %bitcast.17, bf16[768,768]{1,0:T(8,128)(2,1)S(1)} %get-tuple-element.118.q_ref, bf16[768,768]{1,0:T(8,128)(2,1)S(1)} %get-tuple-element.119.k_ref, ...), custom_call_target="tpu_custom_call" | custom-call | flops 4000000000 | bytes 16000000 | tf_op jit(solution)/shard_map/back_far/pallas_call | solution.py:508
  119.0 3.1 %adapter_back.1 = (bf16[768,768]{1,0:T(8,128)(2,1)S(1)}, bf16[768,768]{1,0:T(8,128)(2,1)S(1)}, bf16[768,16]{1,0:T(8,128)(2,1)S(1)}, bf16[768,2304]{1,0:T(8,128)(...) custom-call(bf16[768,768]{1,0:T(8,128)(2,1)S(1)} %get-tuple-element., ...), custom_call_target="tpu_custom_call" | custom-call | flops 500000000 | bytes 12000000 | tf_op jit(solution)/shard_map/adapter_back/pallas_call | solution.py:508
  122.2 1.3 collective-permute-done.5
  123.4 2.7 %collective-permute-start.6 = (bf16[32,768]{1,0:T(8,128)(2,1)S(1)}, bf16[32,768]{1,0:T(8,128)(2,1)S(1)}, u32[]{:S(2)}, u32[]{:S(2)}) collective-permute-start(bf16[32,768]{1,0:T(8,128)(2,1)S(1)} %get-tuple-element.164), channel_id=1, source_target_pairs={{0,1},{1,0},{2,3},{3,2},{4,5},{5,4},{6,7},{7,6},{8,9},{9,8},{10,11... | collective-permute-start | bytes 147464 | tf_op jit(solution)/shard_map/ppermute | solution.py:927
  126.2 1.5 %collective-permute-start.7 = (bf16[32,768]{1,0:T(8,128)(2,1)S(1)}, bf16[32,768]{1,0:T(8,128)(2,1)S(1)}, u32[]{:S(2)}, u32[]{:S(2)}) collective-permute-start(bf16[32,768]{1,0:T(8,128)(2,1)S(1)} %get-tuple-element.164), channel_id=1, source_target_pairs={{0,2},{1,3},{2,0},{3,1},{4,6},{5,7},{6,4},{7,5},{8,10},{9,11},{10,... | collective-permute-start | bytes 147464 | tf_op jit(solution)/shard_map/ppermute | solution.py:927
  127.7 2.7 %project_back.2.rest_0_ = f32[768,768]{1,0:T(8,128)} custom-call(f32[768,768]{1,0:T(8,128)S(1)} %get-tuple-element.144.datt_ref, bf16[768,768]{1,0:T(8,128)(2,1)S(1)} %get-tuple-element.126.dq_ref, bf16[768,768]{1,0:T(8,128)(2,1)S(1)} %get-tuple-element.136.dk_ref, bf16[768,768]{1,0:T(8,128)(2,1)S(1)} %get-tuple-element.137.dv_ref, ...), custom_call_target="tpu_custom_call" | custom-call | flops 1358954496 | bytes 4000000 | tf_op jit(solution)/shard_map/project_back/pallas_call | solution.py:508
  130.5 2.2 %collective-permute-done.8 = bf16[32,768]{1,0:T(8,128)(2,1)S(1)} collective-permute-done((bf16[32,768]{1,0:T(8,128)(2,1)S(1)}, bf16[32,768]{1,0:T(8,128)(2,1)S(1)}, u32[]{:S(2)}, u32[]{:S(2)}) %collective-permute-start.8) | collective-permute-done | bytes 49184 | tf_op jit(solution)/shard_map/ppermute | solution.py:927
  132.7 1.6 %collective-permute-start.9 = (bf16[32,768]{1,0:T(8,128)(2,1)S(1)}, bf16[32,768]{1,0:T(8,128)(2,1)S(1)}, u32[]{:S(2)}, u32[]{:S(2)}) collective-permute-start(bf16[32,768]{1,0:T(8,128)(2,1)S(1)} %get-tuple-element.162), channel_id=1, source_target_pairs={{0,4},{1,5},{2,6},{3,7},{4,0},{5,1},{6,2},{7,3},{8,12},{9,13},{10,... | collective-permute-start | bytes 147464 | tf_op jit(solution)/shard_map/ppermute | solution.py:927
  134.3 2.5 %collective-permute-start.10 = (bf16[32,768]{1,0:T(8,128)(2,1)S(1)}, bf16[32,768]{1,0:T(8,128)(2,1)S(1)}, u32[]{:S(2)}, u32[]{:S(2)}) collective-permute-start(bf16[32,768]{1,0:T(8,128)(2,1)S(1)} %get-tuple-element.162), channel_id=1, source_target_pairs={{0,8},{1,9},{2,10},{3,11},{4,12},{5,13},{6,14},{7,15},{8,0},{9,1},... | collective-permute-start | bytes 147464 | tf_op jit(solution)/shard_map/ppermute | solution.py:927
  137.2 2.7 %project_back.3 = f32[768,768]{1,0:T(8,128)} custom-call(f32[768,768]{1,0:T(8,128)S(1)} %get-tuple-element.144.datt_ref, bf16[768,768]{1,0:T(8,128)(2,1)S(1)} %get-tuple-element.126.dq_ref, bf16[768,768]{1,0:T(8,128)(2,1)S(1)} %get-tuple-element.136.dk_ref, bf16[768,768]{1,0:T(8,128)(2,1)S(1)} %get-tuple-element.137.dv_ref, ...), custom_call_target="tpu_custom_call", output_to_operand_aliasing={{}: (7, {})} | custom-call | flops 1358954496 | bytes 4000000 | tf_op jit(solution)/shard_map/project_back/pallas_call | solution.py:508
  139.9 0.5 collective-permute-done.10
  140.4 2.4 %collective-permute-done.11 = bf16[32,768]{1,0:T(8,128)(2,1)S(1)} collective-permute-done((bf16[32,768]{1,0:T(8,128)(2,1)S(1)}, bf16[32,768]{1,0:T(8,128)(2,1)S(1)}, u32[]{:S(2)}, u32[]{:S(2)}) %collective-permute-start.11) | collective-permute-done | bytes 49184 | tf_op jit(solution)/shard_map/ppermute | solution.py:927
  143.0 1.2 collective-permute-done.12.theirs_ref
  144.2 1.1 adam.1
  (24 shorter events, 0.8 us)
Async XLA Ops:
  0.6 7.6 %copy-start = (s32[3,256]{1,0:T(4,128)S(1)}, s32[3,256]{1,0:T(4,128)}, u32[]{:S(2)}) copy-start(s32[3,256]{1,0:T(4,128)} %own_ref.13) | copy-start | bytes 9220
  0.6 7.7 %copy-start.1 = (s32[3]{0:T(128)S(1)}, s32[3]{0:T(128)}, u32[]{:S(2)}) copy-start(s32[3]{0:T(128)} %param.20) | copy-start | bytes 40
  7.7 3.3 %collective-permute-start.1 = (bf16[2,288,768]{2,1,0:T(8,128)(2,1)S(1)}, bf16[2,288,768]{2,1,0:T(8,128)(2,1)S(1)}, u32[]{:S(2)}, u32[]{:S(2)}) collective-permute-start(bf16[2,288,768]{2,1,0:T(8,128)(2,1)S(1)} %get-tuple-element.88), channel_id=1, source_target_pairs={{0,16},{16,0},{1,17},{17,1},{2,18},{18,2},{3,19},{19,3},{4,20},{20... | collective-permute-start | bytes 2654216 | tf_op jit(solution)/shard_map/ppermute | solution.py:972
  8.2 2.8 %collective-permute-start = (s32[3,256]{1,0:T(4,128)S(1)}, s32[3,256]{1,0:T(4,128)S(1)}, u32[]{:S(2)}, u32[]{:S(2)}) collective-permute-start(s32[3,256]{1,0:T(4,128)S(1)} %copy-done), channel_id=1, source_target_pairs={{0,16},{16,0},{1,17},{17,1},{2,18},{18,2},{3,19},{19,3},{4,20},{20... | collective-permute-start | bytes 9224 | tf_op jit(solution)/shard_map/ppermute | solution.py:966
  33.9 3.3 %collective-permute-start.2 = (bf16[2,288,768]{2,1,0:T(8,128)(2,1)S(1)}, bf16[2,288,768]{2,1,0:T(8,128)(2,1)S(1)}, u32[]{:S(2)}, u32[]{:S(2)}) collective-permute-start(bf16[2,288,768]{2,1,0:T(8,128)(2,1)S(1)} %get-tuple-element.92), channel_id=1, source_target_pairs={{0,16},{16,0},{1,17},{17,1},{2,18},{18,2},{3,19},{19,3},{4,20},{20... | collective-permute-start | bytes 2654216 | tf_op jit(solution)/shard_map/ppermute | solution.py:976
  76.5 7.0 %collective-permute-start.3 = (bf16[2,288,768]{2,1,0:T(8,128)(2,1)S(1)}, bf16[2,288,768]{2,1,0:T(8,128)(2,1)S(1)}, u32[]{:S(2)}, u32[]{:S(2)}) collective-permute-start(bf16[2,288,768]{2,1,0:T(8,128)(2,1)S(1)} %get-tuple-element.103), channel_id=1, source_target_pairs={{0,16},{16,0},{1,17},{17,1},{2,18},{18,2},{3,19},{19,3},{4,20},{20... | collective-permute-start | bytes 2654216 | tf_op jit(solution)/shard_map/ppermute | solution.py:981
  111.4 7.5 %collective-permute-start.4 = (bf16[2,288,768]{2,1,0:T(8,128)(2,1)S(1)}, bf16[2,288,768]{2,1,0:T(8,128)(2,1)S(1)}, u32[]{:S(2)}, u32[]{:S(2)}) collective-permute-start(bf16[2,288,768]{2,1,0:T(8,128)(2,1)S(1)} %get-tuple-element.129), channel_id=1, source_target_pairs={{0,16},{16,0},{1,17},{17,1},{2,18},{18,2},{3,19},{19,3},{4,20},{20... | collective-permute-start | bytes 2654216 | tf_op jit(solution)/shard_map/ppermute | solution.py:985
  122.1 1.4 collective-permute-start.5
  123.4 7.0 %collective-permute-start.6 = (bf16[32,768]{1,0:T(8,128)(2,1)S(1)}, bf16[32,768]{1,0:T(8,128)(2,1)S(1)}, u32[]{:S(2)}, u32[]{:S(2)}) collective-permute-start(bf16[32,768]{1,0:T(8,128)(2,1)S(1)} %get-tuple-element.164), channel_id=1, source_target_pairs={{0,1},{1,0},{2,3},{3,2},{4,5},{5,4},{6,7},{7,6},{8,9},{9,8},{10,11... | collective-permute-start | bytes 147464 | tf_op jit(solution)/shard_map/ppermute | solution.py:927
  126.2 4.3 %collective-permute-start.7 = (bf16[32,768]{1,0:T(8,128)(2,1)S(1)}, bf16[32,768]{1,0:T(8,128)(2,1)S(1)}, u32[]{:S(2)}, u32[]{:S(2)}) collective-permute-start(bf16[32,768]{1,0:T(8,128)(2,1)S(1)} %get-tuple-element.164), channel_id=1, source_target_pairs={{0,2},{1,3},{2,0},{3,1},{4,6},{5,7},{6,4},{7,5},{8,10},{9,11},{10,... | collective-permute-start | bytes 147464 | tf_op jit(solution)/shard_map/ppermute | solution.py:927
  127.7 5.0 %collective-permute-start.8 = (bf16[32,768]{1,0:T(8,128)(2,1)S(1)}, bf16[32,768]{1,0:T(8,128)(2,1)S(1)}, u32[]{:S(2)}, u32[]{:S(2)}) collective-permute-start(bf16[32,768]{1,0:T(8,128)(2,1)S(1)} %get-tuple-element.164), channel_id=1, source_target_pairs={{0,3},{1,2},{2,1},{3,0},{4,7},{5,6},{6,5},{7,4},{8,11},{9,10},{10,... | collective-permute-start | bytes 147464 | tf_op jit(solution)/shard_map/ppermute | solution.py:927
  132.7 7.2 %collective-permute-start.9 = (bf16[32,768]{1,0:T(8,128)(2,1)S(1)}, bf16[32,768]{1,0:T(8,128)(2,1)S(1)}, u32[]{:S(2)}, u32[]{:S(2)}) collective-permute-start(bf16[32,768]{1,0:T(8,128)(2,1)S(1)} %get-tuple-element.162), channel_id=1, source_target_pairs={{0,4},{1,5},{2,6},{3,7},{4,0},{5,1},{6,2},{7,3},{8,12},{9,13},{10,... | collective-permute-start | bytes 147464 | tf_op jit(solution)/shard_map/ppermute | solution.py:927
  134.3 6.0 %collective-permute-start.10 = (bf16[32,768]{1,0:T(8,128)(2,1)S(1)}, bf16[32,768]{1,0:T(8,128)(2,1)S(1)}, u32[]{:S(2)}, u32[]{:S(2)}) collective-permute-start(bf16[32,768]{1,0:T(8,128)(2,1)S(1)} %get-tuple-element.162), channel_id=1, source_target_pairs={{0,8},{1,9},{2,10},{3,11},{4,12},{5,13},{6,14},{7,15},{8,0},{9,1},... | collective-permute-start | bytes 147464 | tf_op jit(solution)/shard_map/ppermute | solution.py:927
  136.9 5.9 %collective-permute-start.11 = (bf16[32,768]{1,0:T(8,128)(2,1)S(1)}, bf16[32,768]{1,0:T(8,128)(2,1)S(1)}, u32[]{:S(2)}, u32[]{:S(2)}) collective-permute-start(bf16[32,768]{1,0:T(8,128)(2,1)S(1)} %get-tuple-element.162), channel_id=1, source_target_pairs={{0,12},{1,13},{2,14},{3,15},{4,8},{5,9},{6,10},{7,11},{8,4},{9,5},... | collective-permute-start | bytes 147464 | tf_op jit(solution)/shard_map/ppermute | solution.py:927
  137.2 5.7 %copy-start.2 = (s32[2,2,2]{2,1,0:T(2,128)S(1)}, s32[2,2,2]{2,1,0:T(2,128)}, u32[]{:S(2)}) copy-start(s32[2,2,2]{2,1,0:T(2,128)} %param.21) | copy-start | bytes 100
  142.8 1.4 collective-permute-start.12

commit v3 on v2

--- a/solution.py
+++ b/solution.py
@@ -15,6 +15,10 @@
 HEAD_ROWS = 16
 MASKED = -1000000000.0
 LOG2E = 1.4426950408889634
+HALF_ROOT_PI = 0.886226925452758
+ROOT_HALF = 0.7071067811865476
+ACTIVE = 0.7978845608028654
+SLOPE = 0.5641895835477563
 F32 = jnp.float32
 BF16 = jnp.bfloat16
 
@@ -304,73 +308,80 @@
     down, up_q, up_v = low_rank(a_ref, b_ref)
     vec = vec_ref[...].astype(F32)
 
-    def send(s, i, ref):
-        taken = rows_at(s * length + (1 - side) * (length - HALO), HALO, 32)
-        send_ref[i, rows_at(s * HALO, HALO, 32), :] = ref[taken, :]
-
-    def queries(s):
-        rows = rows_at(s * length, length, length)
+    tall = x_ref.shape[0] // 2
+
+    def queries(i):
+        rows = rows_at(i * tall, tall, 128)
         x = x_ref[rows, :]
         inner = dot_nt(x, down).astype(BF16)
         u_ref[rows, :] = inner
         q = dot_nn(x, w_ref[:, :width]) + vec[0:1] + 2.0 * dot_nn(inner, up_q)
         q_ref[rows, :] = (q * (0.125 * LOG2E)).astype(BF16)
 
-    def keys(s):
-        rows = rows_at(s * length, length, length)
+    def keys(i):
+        rows = rows_at(i * tall, tall, 128)
         k_ref[rows, :] = dot_nn(x_ref[rows, :], w_ref[:, width:2 * width]).astype(BF16)
-        send(s, 0, k_ref)
-
-    def values(s):
-        rows = rows_at(s * length, length, length)
+
+    def values(i):
+        rows = rows_at(i * tall, tall, 128)
         v = dot_nn(x_ref[rows, :], w_ref[:, 2 * width:]) + vec[1:2]
         v_ref[rows, :] = (v + 2.0 * dot_nn(u_ref[rows, :], up_v)).astype(BF16)
-        send(s, 1, v_ref)
-
-    loop(sequences, queries)
+
+    def send(s):
+        taken = rows_at(s * length + (1 - side) * (length - HALO), HALO, 32)
+        for i, ref in enumerate((k_ref, v_ref)):
+            send_ref[i, rows_at(s * HALO, HALO, 32), :] = ref[taken, :]
+
+    loop(2, queries)
     sent()
     waits[1]()
-    loop(sequences, keys)
+    loop(2, keys)
     waits[2]()
-    loop(sequences, values)
+    loop(2, values)
+    loop(sequences, send)
 
 
 def layer_rest(layer, sequences, length, mix_ref, h_ref, wo_ref, wu_ref, wd_ref, waits, vec_ref, bu_ref,
                one_ref, low_ref, act_ref, n1_ref, r1_ref, dg_ref, n2_ref, r2_ref, h_outs, sent):
-    hidden = wu_ref.shape[1]
+    tokens, hidden = mix_ref.shape[0], wu_ref.shape[1]
     waits[0]()
     vec = vec_ref[...].astype(F32)
-
-    def mixed(s):
-        rows = rows_at(s * length, length, length)
-        attended = dot_nn(mix_ref[rows, :], wo_ref[...]) + vec[2:3] + h_ref[rows, :].astype(F32)
-        one, scaled, inverse = norm_forward(attended, vec[4:5], vec[5:6])
-        n1_ref[rows, :] = scaled.astype(n1_ref.dtype)
-        r1_ref[rows, :] = jnp.broadcast_to(inverse, (length, 128))
-        one_ref[rows, :] = one
-        low_ref[rows, :] = one.astype(BF16)
-
-    loop(sequences, mixed)
+    short, units = 128, 3
+
+    def mixed(i):
+        def unit(k):
+            rows = rows_at((i * units + k) * short, short, short)
+            attended = dot_nn(mix_ref[rows, :], wo_ref[...]) + vec[2:3] + h_ref[rows, :].astype(F32)
+            yield True
+            one, scaled, inverse = norm_forward(attended, vec[4:5], vec[5:6])
+            n1_ref[rows, :] = scaled.astype(n1_ref.dtype)
+            r1_ref[rows, :] = jnp.broadcast_to(inverse, (short, 128))
+            one_ref[rows, :] = one
+            low_ref[rows, :] = (one * ROOT_HALF).astype(BF16)
+
+        pipelined(unit(k) for k in range(units))
+
+    loop(tokens // short // units, mixed)
     sent(0)
     waits[1]()
-    tile = 512
+    tile = 1024
 
     def up(j):
         cols = rows_at(j * tile, tile, tile)
-        bias = bu_ref[layer:layer + 1, cols].astype(F32)
+        bias = bu_ref[layer:layer + 1, cols].astype(F32) * ROOT_HALF
         weights = wu_ref[:, cols]
 
-        def unit(s):
-            rows = slice(s * length, (s + 1) * length)
+        def unit(k):
+            rows = slice(k * short, (k + 1) * short)
             gate = dot_nn(low_ref[rows, :], weights)
             yield True
             gate = gate + bias
-            below = 0.5 * lax.erf(gate * 0.7071067811865476) + 0.5
+            below = HALF_ROOT_PI * lax.erf(gate) + HALF_ROOT_PI
             act_ref[rows, cols] = (gate * below).astype(BF16)
-            density = jnp.exp2(gate * gate * -0.7213475204444817) * 0.3989422804014327
+            density = jnp.exp2(gate * gate * -LOG2E)
             dg_ref[rows, cols] = (below + gate * density).astype(BF16)
 
-        pipelined(unit(s) for s in range(sequences))
+        pipelined(unit(k) for k in range(tokens // short))
 
     loop(hidden // tile, up)
     sent(1)
@@ -378,7 +389,7 @@
 
     def down(s):
         rows = rows_at(s * length, length, length)
-        summed = dot_nn(act_ref[rows, :], wd_ref[...]) + vec[3:4] + one_ref[rows, :]
+        summed = dot_nn(act_ref[rows, :], wd_ref[...]) * ACTIVE + vec[3:4] + one_ref[rows, :]
         out, scaled, inverse = norm_forward(summed, vec[6:7], vec[7:8])
         n2_ref[rows, :] = scaled.astype(n2_ref.dtype)
         r2_ref[rows, :] = jnp.broadcast_to(inverse, (length, 128))
@@ -392,20 +403,21 @@
 def layer_rest_back(sequences, length, gradient, waits, n1_ref, r1_ref, dg_ref, n2_ref, r2_ref,
                     wo_ref, wu_ref, wd_ref, vec_ref, two_ref, low_ref, gate_ref, datt_ref,
                     mix_ref, delta_ref):
-    hidden = wu_ref.shape[1]
+    tokens, hidden = low_ref.shape[0], wu_ref.shape[1]
     waits[0]()
     vec = vec_ref[...].astype(F32)
+    tall = tokens // 2
 
     def second(s):
         rows = rows_at(s * length, length, length)
         two = norm_backward(
             gradient(s, rows), n2_ref[rows, :].astype(F32), r2_ref[rows, 0:1], vec[6:7])
         two_ref[rows, :] = two
-        low_ref[rows, :] = two.astype(BF16)
+        low_ref[rows, :] = (two * SLOPE).astype(BF16)
 
     loop(sequences, second)
     waits[1]()
-    tile = 512
+    tile = 1024
 
     def down(j):
         cols = rows_at(j * tile, tile, tile)
@@ -423,15 +435,24 @@
     waits[2]()
     waits[3]()
 
-    def up(s):
+    def up(i):
+        rows = rows_at(i * tall, tall, 128)
+        datt_ref[rows, :] = dot_nt(gate_ref[rows, :], wu_ref[...])
+
+    def first(s):
         rows = rows_at(s * length, length, length)
-        one = dot_nt(gate_ref[rows, :], wu_ref[...]) + two_ref[rows, :]
-        att = norm_backward(one, n1_ref[rows, :].astype(F32), r1_ref[rows, 0:1], vec[4:5])
+        att = norm_backward(datt_ref[rows, :] + two_ref[rows, :], n1_ref[rows, :].astype(F32),
+                            r1_ref[rows, 0:1], vec[4:5])
         datt_ref[rows, :] = att
-        dmix = dot_nt(att.astype(BF16), wo_ref[...]).astype(BF16)
-        low_ref[rows, :] = dmix
-
-    loop(sequences, up)
+        low_ref[rows, :] = att.astype(BF16)
+
+    def mixture(i):
+        rows = rows_at(i * tall, tall, 128)
+        low_ref[rows, :] = dot_nt(low_ref[rows, :], wo_ref[...]).astype(BF16)
+
+    loop(2, up)
+    loop(sequences, first)
+    loop(2, mixture)
     row_deltas(sequences, length, low_ref, mix_ref, delta_ref)
 
 
@@ -778,12 +799,20 @@
         store.start()
         down, _, _ = low_rank(a_ref, b_ref)
 
+        wait_for(loads, 4)()
+        tall = tokens // 2
+
         def given(s, rows):
-            return project_back(rows, rows, datt_ref, dq_ref, dkb_ref, dvb_ref, du_ref, w_ref,
-                                down)
-
+            return two_ref[rows, :]
+
+        def project(i):
+            rows = rows_at(i * tall, tall, 128)
+            two_ref[rows, :] = project_back(rows, rows, datt_ref, dq_ref, dkb_ref, dvb_ref, du_ref,
+                                            w_ref, down)
+
+        loop(2, project)
         layer_rest_back(sequences, length, given,
-                        [wait_for(loads, 4, 5, 6, 7), wait_for(loads, 8, 9), wait_for(loads, 10),
+                        [wait_for(loads, 5, 6, 7), wait_for(loads, 8, 9), wait_for(loads, 10),
                          wait_for(loads, 11, 12, 13, 19)], n1_ref, r1_ref, dg_ref, n2_ref, r2_ref,
                         wo_ref, wu_ref, wd_ref, vec_ref, two_ref, low_ref, dg_ref, datt_out,
                         mix_ref, delta_ref)
@@ -855,24 +884,30 @@
         [small, act, factors, factors, grad, grad, 6, len(state)], 500000000, 12000000, 8)
 
 
-def project_back_call(part, parts, datt, dq, dk, dv, du, w, down, out):
+def project_back_call(datt, dq, dk, dv, du, w, down):
     tokens, width = dq.shape
+    parts = 2
     length = tokens // parts
 
-    def kernel(datt_ref, dq_ref, dk_ref, dv_ref, du_ref, w_ref, down_ref, *rest):
-        out_hbm, out_ref, sems = rest[-3:]
-        rows = slice(part * length, (part + 1) * length)
-        out_ref[...] = project_back(rows, rows, datt_ref, dq_ref, dk_ref, dv_ref, du_ref, w_ref,
-                                    down_ref[...])
-        store = pltpu.make_async_copy(out_ref, out_hbm.at[rows], sems.at[0])
-        store.start()
-        store.wait()
-
-    args = [(VMEM, item) for item in (datt, dq, dk, dv, du, w, down)]
+    def kernel(datt_ref, dq_ref, dk_ref, dv_ref, du_ref, w_ref, down_ref, out_hbm, out_ref, sems):
+        def part(i):
+            rows = rows_at(i * length, length, 128)
+            return pltpu.make_async_copy(out_ref.at[rows], out_hbm.at[rows], sems.at[i])
+
+        def one(i):
+            rows = rows_at(i * length, length, 128)
+            out_ref[rows, :] = project_back(rows, rows, datt_ref, dq_ref, dk_ref, dv_ref, du_ref,
+                                            w_ref, down_ref[...])
+            part(i).start()
+
+        loop(parts, one)
+        for i in range(parts):
+            part(i).wait()
+
     return call(
-        kernel, "project_back", args + ([] if out is None else [(HBM, out)]),
-        [(HBM, (tokens, width), F32)], [((length, width), F32), 1],
-        2 * length * width * width * 3, 4000000, 6, {} if out is None else {len(args): 0})[0]
+        kernel, "project_back", [(VMEM, item) for item in (datt, dq, dk, dv, du, w, down)],
+        [(HBM, (tokens, width), F32)], [((tokens, width), F32), parts],
+        2 * tokens * width * width * 3, 4000000, 6)[0]
 
 
 def adam_call(mine, theirs, token_slots, steps, down, up, m_down, v_down, m_up, v_up):
@@ -989,14 +1024,11 @@
         second_moment_down, jnp.swapaxes(first_moment_up, 2, 3),
         jnp.swapaxes(second_moment_up, 2, 3))
 
-    def part(i, parts):
-        def work(token, out):
-            now, _ = together(datt, token)
-            return project_back_call(i, parts, now, dq, dk, dv, du, w1, down1, out)
-
-        return work
-
-    mine, theirs, gradient = sum_while(mine, theirs, [part(i, 2) for i in range(2)])
+    def work(token, out):
+        now, _ = together(datt, token)
+        return project_back_call(now, dq, dk, dv, du, w1, down1)
+
+    mine, theirs, gradient = sum_while(mine, theirs, [work])
     token_slots = tokens * lax.axis_size("seq") * lax.axis_size("batch")
     down, up, m_down, v_down, m_up, v_up = adam_call(
         mine, theirs, token_slots, optimizer_step_count.reshape(1, -1), *state)

time: 146 us -> 135 us (0.925)
  Pallas kernels: 126 us -> 116 us
    pallas_call x12 -> x11, Pallas kernels: 126 us -> 116 us  [call(): pl.pallas_call(kernel, name=name, out_shape=tuple((space(shape, dtype) fo...]
  transfers between devices with their start and end apart: 13 -> 13, of which waited for: 5 -> 5; matrix products, arithmetic and copies ran while one was open for 0% -> 0% of each run, Pallas kernels for 17% -> 18%
where the time goes in v3:
time: 135 us
  Pallas kernels  116 us (86%)
  starting transfers between devices  10.7 us (8%)
  waiting for transfers between devices  7.11 us (5%)
    pallas_call x11, Pallas kernels, call(): pl.pallas_call(kernel, name=name, out_shape=tuple((space(shape, dtype) fo...  116 us
    ppermute x6, starting transfers between devices, sum_while(): lax.ppermute(given, 'batch', [(i, i ^ step * d) for i in range(batch)])  8.73 us
    ppermute x6, waiting for transfers between devices, sum_while(): lax.ppermute(given, 'batch', [(i, i ^ step * d) for i in range(batch)])  4.69 us
  transfers between devices with their start and end apart: 13, of which 5 were waited for; matrix products, arithmetic and copies ran while one was open for 0% of the time, Pallas kernels for 18%

profile of v3, /device:TPU:0, one launch (start us, length us, event | category | flops | bytes accessed | tf_op | source)
XLA Modules:
  0.0 134.9 jit_solution(16942739671107148696)
XLA Ops:
  0.7 6.5 %project_in.1 = (bf16[768,768]{1,0:T(8,128)(2,1)S(1)}, bf16[768,768]{1,0:T(8,128)(2,1)S(1)}, bf16[768,768]{1,0:T(8,128)(2,1)S(1)}, bf16[2,288,768]{2,1,0:T(8,128)(2,1)S(1)}, bf16[768,16]{1,0:T(8,128)(2,1)}) custom-call(bf16[768,768]{1,0:T(8,128)(2,1)} %bitcast.19, bf16[2,768,2304]{2,1,0:T(8,128)(2,1)} %w_hbm.7, f32[2,2,8,768]{3,2,1,0:T(8,128)} %rest_0_.1, ...), custom_call_target="tpu_custom_call" | custom-call | flops 2717908992 | bytes 12000000 | tf_op jit(solution)/shard_map/project_in/pallas_call | solution.py:529
  7.2 0.5 collective-permute-start.1
  7.8 2.7 %attention_far.2.far_ref = bf16[384,768]{1,0:T(8,128)(2,1)S(1)} custom-call(bf16[768,768]{1,0:T(8,128)(2,1)S(1)} %get-tuple-element.80.q_ref, bf16[768,768]{1,0:T(8,128)(2,1)S(1)} %get-tuple-element.81.k_ref, bf16[768,768]{1,0:T(8,128)(2,1)S(1)} %get-tuple-element.82.v_ref, s32[3,256]{1,0:T(4,128)S(1)} %copy-done, s32[1,3]{1,0:T(1,128)S(1)} %bitcast.11), custom_call_target="tpu_custom_call" | custom-call | flops 2000000000 | bytes 6000000 | tf_op jit(solution)/shard_map/attention_far/pallas_call | solution.py:529
  10.5 19.9 %middle.1 = (bf16[768,768]{1,0:T(8,128)(2,1)S(1)}, bf16[768,768]{1,0:T(8,128)(2,1)S(1)}, bf16[768,768]{1,0:T(8,128)(2,1)S(1)}, bf16[2,288,768]{2,1,0:T(8,128)(2,...) custom-call(s32[3,256]{1,0:T(4,128)S(1)} %copy-done, ...), custom_call_target="tpu_custom_call" | custom-call | flops 10871635968 | bytes 24000000 | tf_op jit(solution)/shard_map/middle/pallas_call | solution.py:529
  30.4 0.5 collective-permute-start.2
  30.9 2.8 %attention_far.3.far_ref = bf16[384,768]{1,0:T(8,128)(2,1)S(1)} custom-call(bf16[768,768]{1,0:T(8,128)(2,1)S(1)} %get-tuple-element.84.q_ref, bf16[768,768]{1,0:T(8,128)(2,1)S(1)} %get-tuple-element.85.k_ref, bf16[768,768]{1,0:T(8,128)(2,1)S(1)} %get-tuple-element.86.v_ref, s32[3,256]{1,0:T(4,128)S(1)} %copy-done, s32[1,3]{1,0:T(1,128)S(1)} %bitcast.13), custom_call_target="tpu_custom_call" | custom-call | flops 2000000000 | bytes 6000000 | tf_op jit(solution)/shard_map/attention_far/pallas_call | solution.py:529
  33.7 35.1 %turn.1 = (f32[768,768]{1,0:T(8,128)S(1)}, bf16[384,768]{1,0:T(8,128)(2,1)S(1)}, bf16[384,768]{1,0:T(8,128)(2,1)S(1)}, f32[960,768]{1,0:T(8,128)S(1)}, f32[960,7...) custom-call(s32[3,256]{1,0:T(4,128)S(1)} %copy-done, ...), custom_call_target="tpu_custom_call" | custom-call | flops 16307453952 | bytes 24000000 | tf_op jit(solution)/shard_map/turn/pallas_call | solution.py:529
  69.0 6.9 %back_far.2 = (bf16[768,768]{1,0:T(8,128)(2,1)S(1)}, f32[768,768]{1,0:T(8,128)S(1)}, f32[768,768]{1,0:T(8,128)S(1)}) custom-call(s32[3,256]{1,0:T(4,128)S(1)} %copy-done, s32[1,3]{1,0:T(1,128)S(1)} %bitcast.15, bf16[768,768]{1,0:T(8,128)(2,1)S(1)} %get-tuple-element.84.q_ref, bf16[768,768]{1,0:T(8,128)(2,1)S(1)} %get-tuple-element.85.k_ref, ...), custom_call_target="tpu_custom_call" | custom-call | flops 4000000000 | bytes 16000000 | tf_op jit(solution)/shard_map/back_far/pallas_call | solution.py:529
  75.9 26.4 %back.1 = (f32[768,768]{1,0:T(8,128)S(1)}, bf16[384,768]{1,0:T(8,128)(2,1)S(1)}, bf16[384,768]{1,0:T(8,128)(2,1)S(1)}, f32[960,768]{1,0:T(8,128)S(1)}, f32[960,7...) custom-call(s32[3,256]{1,0:T(4,128)S(1)} %copy-done, ...), custom_call_target="tpu_custom_call" | custom-call | flops 10871635968 | bytes 24000000 | tf_op jit(solution)/shard_map/back/pallas_call | solution.py:529
  102.3 0.5 collective-permute-start.4
  102.8 7.0 %back_far.3 = (bf16[768,768]{1,0:T(8,128)(2,1)S(1)}, f32[768,768]{1,0:T(8,128)S(1)}, f32[768,768]{1,0:T(8,128)S(1)}) custom-call(s32[3,256]{1,0:T(4,128)S(1)} %copy-done, s32[1,3]{1,0:T(1,128)S(1)} %bitcast.17, bf16[768,768]{1,0:T(8,128)(2,1)S(1)} %get-tuple-element.113.q_ref, bf16[768,768]{1,0:T(8,128)(2,1)S(1)} %get-tuple-element.114.k_ref, ...), custom_call_target="tpu_custom_call" | custom-call | flops 4000000000 | bytes 16000000 | tf_op jit(solution)/shard_map/back_far/pallas_call | solution.py:529
  109.8 3.1 %adapter_back.1 = (bf16[768,768]{1,0:T(8,128)(2,1)S(1)}, bf16[768,768]{1,0:T(8,128)(2,1)S(1)}, bf16[768,16]{1,0:T(8,128)(2,1)S(1)}, bf16[768,2304]{1,0:T(8,128)(...) custom-call(bf16[768,768]{1,0:T(8,128)(2,1)S(1)} %get-tuple-element., ...), custom_call_target="tpu_custom_call" | custom-call | flops 500000000 | bytes 12000000 | tf_op jit(solution)/shard_map/adapter_back/pallas_call | solution.py:529
  112.9 0.2 collective-permute-start.5
  113.0 1.2 collective-permute-done.5
  114.3 2.7 %collective-permute-start.6 = (bf16[32,768]{1,0:T(8,128)(2,1)S(1)}, bf16[32,768]{1,0:T(8,128)(2,1)S(1)}, u32[]{:S(2)}, u32[]{:S(2)}) collective-permute-start(bf16[32,768]{1,0:T(8,128)(2,1)S(1)} %get-tuple-element.152), channel_id=1, source_target_pairs={{0,1},{1,0},{2,3},{3,2},{4,5},{5,4},{6,7},{7,6},{8,9},{9,8},{10,11... | collective-permute-start | bytes 147464 | tf_op jit(solution)/shard_map/ppermute | solution.py:962
  117.0 1.5 %collective-permute-start.7 = (bf16[32,768]{1,0:T(8,128)(2,1)S(1)}, bf16[32,768]{1,0:T(8,128)(2,1)S(1)}, u32[]{:S(2)}, u32[]{:S(2)}) collective-permute-start(bf16[32,768]{1,0:T(8,128)(2,1)S(1)} %get-tuple-element.152), channel_id=1, source_target_pairs={{0,2},{1,3},{2,0},{3,1},{4,6},{5,7},{6,4},{7,5},{8,10},{9,11},{10,... | collective-permute-start | bytes 147464 | tf_op jit(solution)/shard_map/ppermute | solution.py:962
  118.6 4.5 %project_back.1 = f32[768,768]{1,0:T(8,128)} custom-call(f32[768,768]{1,0:T(8,128)S(1)} %get-tuple-element.130.datt_ref, bf16[768,768]{1,0:T(8,128)(2,1)S(1)} %get-tuple-element.121.dq_ref, bf16[768,768]{1,0:T(8,128)(2,1)S(1)} %get-tuple-element.131.dk_ref, bf16[768,768]{1,0:T(8,128)(2,1)S(1)} %get-tuple-element.132.dv_ref, ...), custom_call_target="tpu_custom_call" | custom-call | flops 2717908992 | bytes 4000000 | tf_op jit(solution)/shard_map/project_back/pallas_call | solution.py:529
  123.1 0.4 collective-permute-done.8
  123.5 3.7 %collective-permute-start.11 = (bf16[32,768]{1,0:T(8,128)(2,1)S(1)}, bf16[32,768]{1,0:T(8,128)(2,1)S(1)}, u32[]{:S(2)}, u32[]{:S(2)}) collective-permute-start(bf16[32,768]{1,0:T(8,128)(2,1)S(1)} %fusion), channel_id=1, source_target_pairs={{0,12},{1,13},{2,14},{3,15},{4,8},{5,9},{6,10},{7,11},{8,4},{9,5},... | collective-permute-start | bytes 147464 | tf_op jit(solution)/shard_map/ppermute | solution.py:962
  127.2 0.8 collective-permute-start.9
  128.0 2.1 %collective-permute-done.11 = bf16[32,768]{1,0:T(8,128)(2,1)S(1)} collective-permute-done((bf16[32,768]{1,0:T(8,128)(2,1)S(1)}, bf16[32,768]{1,0:T(8,128)(2,1)S(1)}, u32[]{:S(2)}, u32[]{:S(2)}) %collective-permute-start.11) | collective-permute-done | bytes 49184 | tf_op jit(solution)/shard_map/ppermute | solution.py:962
  130.1 2.2 %collective-permute-done.10 = bf16[32,768]{1,0:T(8,128)(2,1)S(1)} collective-permute-done((bf16[32,768]{1,0:T(8,128)(2,1)S(1)}, bf16[32,768]{1,0:T(8,128)(2,1)S(1)}, u32[]{:S(2)}, u32[]{:S(2)}) %collective-permute-start.10) | collective-permute-done | bytes 49184 | tf_op jit(solution)/shard_map/ppermute | solution.py:962
  132.5 1.2 collective-permute-done.12.theirs_ref
  133.6 1.1 adam.1
  (23 shorter events, 0.5 us)
Async XLA Ops:
  0.6 7.1 %copy-start = (s32[3,256]{1,0:T(4,128)S(1)}, s32[3,256]{1,0:T(4,128)}, u32[]{:S(2)}) copy-start(s32[3,256]{1,0:T(4,128)} %own_ref.13) | copy-start | bytes 9220
  0.6 7.2 %copy-start.1 = (s32[3]{0:T(128)S(1)}, s32[3]{0:T(128)}, u32[]{:S(2)}) copy-start(s32[3]{0:T(128)} %param.20) | copy-start | bytes 40
  7.2 3.3 %collective-permute-start.1 = (bf16[2,288,768]{2,1,0:T(8,128)(2,1)S(1)}, bf16[2,288,768]{2,1,0:T(8,128)(2,1)S(1)}, u32[]{:S(2)}, u32[]{:S(2)}) collective-permute-start(bf16[2,288,768]{2,1,0:T(8,128)(2,1)S(1)} %get-tuple-element.83), channel_id=1, source_target_pairs={{0,16},{16,0},{1,17},{17,1},{2,18},{18,2},{3,19},{19,3},{4,20},{20... | collective-permute-start | bytes 2654216 | tf_op jit(solution)/shard_map/ppermute | solution.py:1007
  7.7 2.8 %collective-permute-start = (s32[3,256]{1,0:T(4,128)S(1)}, s32[3,256]{1,0:T(4,128)S(1)}, u32[]{:S(2)}, u32[]{:S(2)}) collective-permute-start(s32[3,256]{1,0:T(4,128)S(1)} %copy-done), channel_id=1, source_target_pairs={{0,16},{16,0},{1,17},{17,1},{2,18},{18,2},{3,19},{19,3},{4,20},{20... | collective-permute-start | bytes 9224 | tf_op jit(solution)/shard_map/ppermute | solution.py:1001
  30.4 3.3 %collective-permute-start.2 = (bf16[2,288,768]{2,1,0:T(8,128)(2,1)S(1)}, bf16[2,288,768]{2,1,0:T(8,128)(2,1)S(1)}, u32[]{:S(2)}, u32[]{:S(2)}) collective-permute-start(bf16[2,288,768]{2,1,0:T(8,128)(2,1)S(1)} %get-tuple-element.87), channel_id=1, source_target_pairs={{0,16},{16,0},{1,17},{17,1},{2,18},{18,2},{3,19},{19,3},{4,20},{20... | collective-permute-start | bytes 2654216 | tf_op jit(solution)/shard_map/ppermute | solution.py:1011
  68.9 7.0 %collective-permute-start.3 = (bf16[2,288,768]{2,1,0:T(8,128)(2,1)S(1)}, bf16[2,288,768]{2,1,0:T(8,128)(2,1)S(1)}, u32[]{:S(2)}, u32[]{:S(2)}) collective-permute-start(bf16[2,288,768]{2,1,0:T(8,128)(2,1)S(1)} %get-tuple-element.98), channel_id=1, source_target_pairs={{0,16},{16,0},{1,17},{17,1},{2,18},{18,2},{3,19},{19,3},{4,20},{20... | collective-permute-start | bytes 2654216 | tf_op jit(solution)/shard_map/ppermute | solution.py:1016
  102.3 7.5 %collective-permute-start.4 = (bf16[2,288,768]{2,1,0:T(8,128)(2,1)S(1)}, bf16[2,288,768]{2,1,0:T(8,128)(2,1)S(1)}, u32[]{:S(2)}, u32[]{:S(2)}) collective-permute-start(bf16[2,288,768]{2,1,0:T(8,128)(2,1)S(1)} %get-tuple-element.124), channel_id=1, source_target_pairs={{0,16},{16,0},{1,17},{17,1},{2,18},{18,2},{3,19},{19,3},{4,20},{20... | collective-permute-start | bytes 2654216 | tf_op jit(solution)/shard_map/ppermute | solution.py:1020
  112.9 1.4 %collective-permute-start.5 = (f32[32,768]{1,0:T(8,128)S(1)}, f32[32,768]{1,0:T(8,128)S(1)}, u32[]{:S(2)}, u32[]{:S(2)}) collective-permute-start(f32[32,768]{1,0:T(8,128)S(1)} %get-tuple-element.128), channel_id=1, source_target_pairs={{0,16},{16,0},{1,17},{17,1},{2,18},{18,2},{3,19},{19,3},{4,20},{20... | collective-permute-start | bytes 294920 | tf_op jit(solution)/shard_map/ppermute | solution.py:957
  114.3 8.8 %collective-permute-start.6 = (bf16[32,768]{1,0:T(8,128)(2,1)S(1)}, bf16[32,768]{1,0:T(8,128)(2,1)S(1)}, u32[]{:S(2)}, u32[]{:S(2)}) collective-permute-start(bf16[32,768]{1,0:T(8,128)(2,1)S(1)} %get-tuple-element.152), channel_id=1, source_target_pairs={{0,1},{1,0},{2,3},{3,2},{4,5},{5,4},{6,7},{7,6},{8,9},{9,8},{10,11... | collective-permute-start | bytes 147464 | tf_op jit(solution)/shard_map/ppermute | solution.py:962
  117.0 6.0 %collective-permute-start.7 = (bf16[32,768]{1,0:T(8,128)(2,1)S(1)}, bf16[32,768]{1,0:T(8,128)(2,1)S(1)}, u32[]{:S(2)}, u32[]{:S(2)}) collective-permute-start(bf16[32,768]{1,0:T(8,128)(2,1)S(1)} %get-tuple-element.152), channel_id=1, source_target_pairs={{0,2},{1,3},{2,0},{3,1},{4,6},{5,7},{6,4},{7,5},{8,10},{9,11},{10,... | collective-permute-start | bytes 147464 | tf_op jit(solution)/shard_map/ppermute | solution.py:962
  118.5 5.0 %collective-permute-start.8 = (bf16[32,768]{1,0:T(8,128)(2,1)S(1)}, bf16[32,768]{1,0:T(8,128)(2,1)S(1)}, u32[]{:S(2)}, u32[]{:S(2)}) collective-permute-start(bf16[32,768]{1,0:T(8,128)(2,1)S(1)} %get-tuple-element.152), channel_id=1, source_target_pairs={{0,3},{1,2},{2,1},{3,0},{4,7},{5,6},{6,5},{7,4},{8,11},{9,10},{10,... | collective-permute-start | bytes 147464 | tf_op jit(solution)/shard_map/ppermute | solution.py:962
  118.5 13.8 %copy-start.2 = (s32[2,2,2]{2,1,0:T(2,128)S(1)}, s32[2,2,2]{2,1,0:T(2,128)}, u32[]{:S(2)}) copy-start(s32[2,2,2]{2,1,0:T(2,128)} %param.21) | copy-start | bytes 100
  123.5 6.5 %collective-permute-start.11 = (bf16[32,768]{1,0:T(8,128)(2,1)S(1)}, bf16[32,768]{1,0:T(8,128)(2,1)S(1)}, u32[]{:S(2)}, u32[]{:S(2)}) collective-permute-start(bf16[32,768]{1,0:T(8,128)(2,1)S(1)} %fusion), channel_id=1, source_target_pairs={{0,12},{1,13},{2,14},{3,15},{4,8},{5,9},{6,10},{7,11},{8,4},{9,5},... | collective-permute-start | bytes 147464 | tf_op jit(solution)/shard_map/ppermute | solution.py:962
  127.2 5.0 %collective-permute-start.10 = (bf16[32,768]{1,0:T(8,128)(2,1)S(1)}, bf16[32,768]{1,0:T(8,128)(2,1)S(1)}, u32[]{:S(2)}, u32[]{:S(2)}) collective-permute-start(bf16[32,768]{1,0:T(8,128)(2,1)S(1)} %fusion), channel_id=1, source_target_pairs={{0,8},{1,9},{2,10},{3,11},{4,12},{5,13},{6,14},{7,15},{8,0},{9,1},... | collective-permute-start | bytes 147464 | tf_op jit(solution)/shard_map/ppermute | solution.py:962
  127.2 5.0 %collective-permute-start.9 = (bf16[32,768]{1,0:T(8,128)(2,1)S(1)}, bf16[32,768]{1,0:T(8,128)(2,1)S(1)}, u32[]{:S(2)}, u32[]{:S(2)}) collective-permute-start(bf16[32,768]{1,0:T(8,128)(2,1)S(1)} %fusion), channel_id=1, source_target_pairs={{0,4},{1,5},{2,6},{3,7},{4,0},{5,1},{6,2},{7,3},{8,12},{9,13},{10,... | collective-permute-start | bytes 147464 | tf_op jit(solution)/shard_map/ppermute | solution.py:962
  132.3 1.4 %collective-permute-start.12 = (f32[32,768]{1,0:T(8,128)S(1)}, f32[32,768]{1,0:T(8,128)S(1)}, u32[]{:S(2)}, u32[]{:S(2)}) collective-permute-start(f32[32,768]{1,0:T(8,128)S(1)} %add_add_fusion.mine_ref), channel_id=1, source_target_pairs={{0,16},{16,0},{1,17},{17,1},{2,18},{18,2},{3,19},{19,3},{4,20},{20... | collective-permute-start | bytes 294920 | tf_op jit(solution)/shard_map/ppermute | solution.py:971

commit v4 on v3

--- a/solution.py
+++ b/solution.py
@@ -89,7 +89,7 @@
     while units or live:
         if units:
             live.append(units.pop(0))
-        for unit in list(live):
+        for unit in reversed(list(live)):
             if next(unit, None) is None:
                 live.remove(unit)
 
@@ -168,8 +168,9 @@
 SLOTS = 2
 
 
-def attention_scratch():
-    return [((SLOTS, WINDOW, 4 * SUB), F32), ((SLOTS, WINDOW, 4 * SUB), BF16)]
+def attention_scratch(backward=False):
+    pair = [((SLOTS, WINDOW, 4 * SUB), F32), ((SLOTS, WINDOW, 4 * SUB), BF16)]
+    return pair * 2 if backward else pair
 
 
 def attention_forward(where, s, q_ref, k_ref, v_ref, out_ref, out_rows, bias_ref, scratch):
@@ -203,8 +204,9 @@
 
 
 def attention_backward(where, s, q_ref, k_ref, v_ref, dmix_ref, dmix_rows, delta_ref, dq_ref,
-                       dq_rows, key_terms, bias_ref):
+                       dq_rows, key_terms, bias_ref, scratch):
     low = low_lanes()
+    scores_ref, share_ref, d_share_ref, d_scores_ref = scratch
     delta = delta_ref[rows_at(s * HEAD_ROWS, HEAD_ROWS, HEAD_ROWS), :]
     delta = jnp.where(where.row0 == 0, delta[:, :BLOCK], delta[:, BLOCK:])
     turned = pltpu.roll(delta, SUB, 1)
@@ -213,10 +215,11 @@
     def unit(quad, sub, kept):
         cols = slice(QUAD * quad, QUAD * quad + QUAD)
         keys = where.keys(s, sub)
+        slot = (2 * quad + sub) % SLOTS
         q4 = spread_heads(q_ref[where.queries(s, sub), cols], low)
         d4 = spread_heads(dmix_ref[dmix_rows(s, sub), cols], low)
-        scores = dot_nt(k_ref[keys, cols], q4)
-        d_share = dot_nt(v_ref[keys, cols], d4)
+        scores_ref[slot] = dot_nt(k_ref[keys, cols], q4)
+        d_share_ref[slot] = dot_nt(v_ref[keys, cols], d4)
         yield True
         bias = bias_ref[rows_at((s * 2 + sub) * WINDOW, WINDOW, WINDOW), :]
         shares, d_scores = [], []
@@ -224,18 +227,19 @@
         for i in range(2):
             head = 4 * quad + 2 * i
             drop = jnp.where(first_half, left[head:head + 1], right[head + 1:head + 2])
-            part = scores[:, 128 * i:128 * i + 128] + bias
+            part = scores_ref[slot, :, 128 * i:128 * i + 128] + bias
             part = jnp.exp2(part - jnp.max(part, axis=0, keepdims=True))
             part = part * (1.0 / jnp.sum(part, axis=0, keepdims=True))
             shares.append(part.astype(BF16))
-            d_scores.append((part * (d_share[:, 128 * i:128 * i + 128] - drop)).astype(BF16))
+            d_scores.append((part * (d_share_ref[slot, :, 128 * i:128 * i + 128] - drop)).astype(BF16))
         d_scores = jnp.concatenate(d_scores, axis=1)
         kept.append((jnp.concatenate(shares, axis=1), d_scores, q4, d4))
         yield True
+        if sub == 1:
+            key_terms(s, cols, kept)
+        yield True
         d_query = gather_heads(dot_tn(d_scores, k_ref[keys, cols])) * 0.125
         dq_ref[dq_rows(s, sub), cols] = d_query.astype(BF16)
-        if sub == 1:
-            key_terms(s, cols, kept)
 
     width = q_ref.shape[1]
 
@@ -457,7 +461,7 @@
 
 
 def near_backward(near, sequences, length, q_ref, nk_ref, nv_ref, dmix_ref, delta_ref,
-                  dfar_ref, dq_ref, dnk_ref, dnv_ref, dhalo_ref, bias_ref):
+                  dfar_ref, dq_ref, dnk_ref, dnv_ref, dhalo_ref, bias_ref, scratch):
     side, wide = near.side, WINDOW + SUB
 
     def key_terms(s, cols, kept):
@@ -475,7 +479,8 @@
             rows_at(s * length + side * BLOCK, BLOCK, BLOCK), :]
         attention_backward(
             near, s, q_ref, nk_ref, nv_ref, dmix_ref, near.queries, delta_ref, dq_ref,
-            lambda s, sub: rows_at(s * BLOCK + sub * SUB, SUB, SUB), key_terms, bias_ref)
+            lambda s, sub: rows_at(s * BLOCK + sub * SUB, SUB, SUB), key_terms, bias_ref,
+            scratch)
         halo = rows_at(s * wide + (wide - HALO) * (1 - side), HALO, 32)
         dhalo_ref[0, rows_at(s * HALO, HALO, 32), :] = (
             dnk_ref[halo, :] * (1.0 / LOG2E)).astype(BF16)
@@ -713,7 +718,7 @@
                         r1_ref, dg_ref, n2_ref, r2_ref, wo_ref, wu_ref, wd_ref, vec_ref, one_ref,
                         low_ref, act_ref, datt_ref, mix_ref, delta_ref)
         near_backward(near, sequences, length, q_ref, nk_ref, nv_ref, low_ref,
-                      delta_ref, dfar_ref, dq_ref, dnk_ref, dnv_ref, dhalo_ref, columns_ref)
+                      delta_ref, dfar_ref, dq_ref, dnk_ref, dnv_ref, dhalo_ref, columns_ref, scratch)
         store.wait()
 
     act, stat = ((tokens, width), BF16), ((tokens, 128), F32)
@@ -731,7 +736,7 @@
         [(h.shape, h.dtype), act, ((width, width), BF16), ((width, hidden), BF16),
          ((hidden, width), BF16), ((8, width), BF16), (bias_up.shape, BF16), act, wide, act, deep,
          act, stat, deep, act, stat, near, near, act, 7, 1, bias_shape(sequences, False),
-         bias_shape(sequences, True)] + attention_scratch(),
+         bias_shape(sequences, True)] + attention_scratch(True),
         4 * tokens * width * (2 * hidden + width), 24000000, 42)
 
 
@@ -739,7 +744,8 @@
     tokens, width = q.shape
 
     def kernel(own_ref, live_ref, q_ref, k_ref, v_ref, dfar_ref, delta_ref, dqn_ref, dnk_ref,
-               dnv_ref, dq_ref, dk_ref, dv_ref, bias_ref):
+               dnv_ref, dq_ref, dk_ref, dv_ref, bias_ref,
+               *scratch):
         far = Side(False, length, (own_ref, None, live_ref))
         far.biases(sequences, None, bias_ref)
         side, wide, own = far.side, WINDOW + SUB, WINDOW + SUB - HALO
@@ -754,7 +760,7 @@
             attention_backward(
                 far, s, q_ref, k_ref, v_ref, dfar_ref,
                 lambda s, sub: rows_at(s * BLOCK + sub * SUB, SUB, SUB), delta_ref, dq_ref,
-                far.queries, key_terms, bias_ref)
+                far.queries, key_terms, bias_ref, scratch)
             dq_ref[rows_at(s * length + (1 - side) * BLOCK, BLOCK, BLOCK), :] = dqn_ref[
                 rows_at(s * BLOCK, BLOCK, BLOCK), :]
             mine = rows_at(s * length + (length - own) * (1 - side), own, 32)
@@ -770,7 +776,7 @@
         [(VMEM, ids[0]), (VMEM, ids[2])]
         + [(VMEM, item) for item in (q, k, v, dfar, delta, dq_near, dnk, dnv)],
         [(VMEM, (tokens, width), BF16), wide, wide],
-        [bias_shape(sequences, True)], 4000000000, 16000000, 8)
+        [bias_shape(sequences, True)] + attention_scratch(True), 4000000000, 16000000, 8)
 
 
 def back_call(layer, sequences, length, ids, dq, dk, dv, dhalo, datt, u, x, saved, w, a, b, wo, wu,
@@ -785,7 +791,7 @@
                v_ref, grad_out,
                u_ref, x_ref, n1_ref, r1_ref, dg_ref, n2_ref, r2_ref, nk_ref, nv_ref, w_ref,
                a_ref, b_ref, wo_ref, wu_ref, wd_ref, vec_ref, dkb_ref, dvb_ref, du_ref, grad_ref,
-               two_ref, low_ref, mix_ref, ins, outs, bias_ref):
+               two_ref, low_ref, mix_ref, ins, outs, bias_ref, *scratch):
         loads = start_all(copies_of(
             [(a_hbm.at[layer + 1], a_ref), (b_hbm.at[layer + 1], b_ref), (u_hbm, u_ref),
              (x_hbm, x_ref), (w_hbm.at[layer + 1], w_ref), (vec_hbm.at[layer], vec_ref),
@@ -820,7 +826,7 @@
         near = Side(True, length, (own_ref, other_ref, live_ref))
         near.biases(sequences, None, bias_ref)
         near_backward(near, sequences, length, q_ref, nk_ref, nv_ref, low_ref,
-                      delta_ref, dfar_ref, dqn_ref, dnk_ref, dnv_ref, dhalo_out, bias_ref)
+                      delta_ref, dfar_ref, dqn_ref, dnk_ref, dnv_ref, dhalo_out, bias_ref, scratch)
         wait_for(loads, 17, 18)()
         store.wait()
 
@@ -842,7 +848,8 @@
          (HBM,) + grad],
         [small, act, act, stat, deep, act, stat, near, near, ((width, 3 * width), BF16), factors,
          factors, ((width, width), BF16), ((width, hidden), BF16), ((hidden, width), BF16),
-         ((8, width), BF16), act, act, small, grad, wide, act, act, 20, 1, bias_shape(sequences, True)],
+         ((8, width), BF16), act, act, small, grad, wide, act, act, 20, 1, bias_shape(sequences, True)]
+        + attention_scratch(True),
         2 * tokens * width * (2 * hidden + 4 * width), 24000000, 38)
 
 

time: 135 us -> 130 us (0.963)
  Pallas kernels: 116 us -> 111 us
    pallas_call x11, Pallas kernels: 116 us -> 111 us  [call(): pl.pallas_call(kernel, name=name, out_shape=tuple((space(shape, dtype) fo...]
  transfers between devices with their start and end apart: 13 -> 13, of which waited for: 5 -> 5; matrix products, arithmetic and copies ran while one was open for 0% -> 0% of each run, Pallas kernels for 18% -> 16%
where the time goes in v4:
time: 130 us
  Pallas kernels  111 us (85%)
  starting transfers between devices  10.6 us (8%)
  waiting for transfers between devices  7.16 us (6%)
    pallas_call x11, Pallas kernels, call(): pl.pallas_call(kernel, name=name, out_shape=tuple((space(shape, dtype) fo...  111 us
    ppermute x6, starting transfers between devices, sum_while(): lax.ppermute(given, 'batch', [(i, i ^ step * d) for i in range(batch)])  8.67 us
    ppermute x6, waiting for transfers between devices, sum_while(): lax.ppermute(given, 'batch', [(i, i ^ step * d) for i in range(batch)])  4.71 us
  transfers between devices with their start and end apart: 13, of which 5 were waited for; matrix products, arithmetic and copies ran while one was open for 0% of the time, Pallas kernels for 16%

profile of v4, /device:TPU:0, one launch (start us, length us, event | category | flops | bytes accessed | tf_op | source)
XLA Modules:
  0.0 130.2 jit_solution(10201352261780401534)
XLA Ops:
  0.7 6.5 %project_in.1 = (bf16[768,768]{1,0:T(8,128)(2,1)S(1)}, bf16[768,768]{1,0:T(8,128)(2,1)S(1)}, bf16[768,768]{1,0:T(8,128)(2,1)S(1)}, bf16[2,288,768]{2,1,0:T(8,128)(2,1)S(1)}, bf16[768,16]{1,0:T(8,128)(2,1)}) custom-call(bf16[768,768]{1,0:T(8,128)(2,1)} %bitcast.19, bf16[2,768,2304]{2,1,0:T(8,128)(2,1)} %w_hbm.7, f32[2,2,8,768]{3,2,1,0:T(8,128)} %rest_0_.1, ...), custom_call_target="tpu_custom_call" | custom-call | flops 2717908992 | bytes 12000000 | tf_op jit(solution)/shard_map/project_in/pallas_call | solution.py:534
  7.2 0.5 collective-permute-start.1
  7.8 2.7 %attention_far.2.far_ref = bf16[384,768]{1,0:T(8,128)(2,1)S(1)} custom-call(bf16[768,768]{1,0:T(8,128)(2,1)S(1)} %get-tuple-element.80.q_ref, bf16[768,768]{1,0:T(8,128)(2,1)S(1)} %get-tuple-element.81.k_ref, bf16[768,768]{1,0:T(8,128)(2,1)S(1)} %get-tuple-element.82.v_ref, s32[3,256]{1,0:T(4,128)S(1)} %copy-done, s32[1,3]{1,0:T(1,128)S(1)} %bitcast.11), custom_call_target="tpu_custom_call" | custom-call | flops 2000000000 | bytes 6000000 | tf_op jit(solution)/shard_map/attention_far/pallas_call | solution.py:534
  10.6 19.9 %middle.1 = (bf16[768,768]{1,0:T(8,128)(2,1)S(1)}, bf16[768,768]{1,0:T(8,128)(2,1)S(1)}, bf16[768,768]{1,0:T(8,128)(2,1)S(1)}, bf16[2,288,768]{2,1,0:T(8,128)(2,...) custom-call(s32[3,256]{1,0:T(4,128)S(1)} %copy-done, ...), custom_call_target="tpu_custom_call" | custom-call | flops 10871635968 | bytes 24000000 | tf_op jit(solution)/shard_map/middle/pallas_call | solution.py:534
  30.5 0.5 collective-permute-start.2
  31.0 2.8 %attention_far.3.far_ref = bf16[384,768]{1,0:T(8,128)(2,1)S(1)} custom-call(bf16[768,768]{1,0:T(8,128)(2,1)S(1)} %get-tuple-element.84.q_ref, bf16[768,768]{1,0:T(8,128)(2,1)S(1)} %get-tuple-element.85.k_ref, bf16[768,768]{1,0:T(8,128)(2,1)S(1)} %get-tuple-element.86.v_ref, s32[3,256]{1,0:T(4,128)S(1)} %copy-done, s32[1,3]{1,0:T(1,128)S(1)} %bitcast.13), custom_call_target="tpu_custom_call" | custom-call | flops 2000000000 | bytes 6000000 | tf_op jit(solution)/shard_map/attention_far/pallas_call | solution.py:534
  33.8 34.2 %turn.1 = (f32[768,768]{1,0:T(8,128)S(1)}, bf16[384,768]{1,0:T(8,128)(2,1)S(1)}, bf16[384,768]{1,0:T(8,128)(2,1)S(1)}, f32[960,768]{1,0:T(8,128)S(1)}, f32[960,7...) custom-call(s32[3,256]{1,0:T(4,128)S(1)} %copy-done, ...), custom_call_target="tpu_custom_call" | custom-call | flops 16307453952 | bytes 24000000 | tf_op jit(solution)/shard_map/turn/pallas_call | solution.py:534
  68.2 5.5 %back_far.2 = (bf16[768,768]{1,0:T(8,128)(2,1)S(1)}, f32[768,768]{1,0:T(8,128)S(1)}, f32[768,768]{1,0:T(8,128)S(1)}) custom-call(s32[3,256]{1,0:T(4,128)S(1)} %copy-done, s32[1,3]{1,0:T(1,128)S(1)} %bitcast.15, bf16[768,768]{1,0:T(8,128)(2,1)S(1)} %get-tuple-element.84.q_ref, bf16[768,768]{1,0:T(8,128)(2,1)S(1)} %get-tuple-element.85.k_ref, ...), custom_call_target="tpu_custom_call" | custom-call | flops 4000000000 | bytes 16000000 | tf_op jit(solution)/shard_map/back_far/pallas_call | solution.py:534
  73.7 25.3 %back.1 = (f32[768,768]{1,0:T(8,128)S(1)}, bf16[384,768]{1,0:T(8,128)(2,1)S(1)}, bf16[384,768]{1,0:T(8,128)(2,1)S(1)}, f32[960,768]{1,0:T(8,128)S(1)}, f32[960,7...) custom-call(s32[3,256]{1,0:T(4,128)S(1)} %copy-done, ...), custom_call_target="tpu_custom_call" | custom-call | flops 10871635968 | bytes 24000000 | tf_op jit(solution)/shard_map/back/pallas_call | solution.py:534
  99.0 0.5 collective-permute-start.4
  99.5 5.6 %back_far.3 = (bf16[768,768]{1,0:T(8,128)(2,1)S(1)}, f32[768,768]{1,0:T(8,128)S(1)}, f32[768,768]{1,0:T(8,128)S(1)}) custom-call(s32[3,256]{1,0:T(4,128)S(1)} %copy-done, s32[1,3]{1,0:T(1,128)S(1)} %bitcast.17, bf16[768,768]{1,0:T(8,128)(2,1)S(1)} %get-tuple-element.113.q_ref, bf16[768,768]{1,0:T(8,128)(2,1)S(1)} %get-tuple-element.114.k_ref, ...), custom_call_target="tpu_custom_call" | custom-call | flops 4000000000 | bytes 16000000 | tf_op jit(solution)/shard_map/back_far/pallas_call | solution.py:534
  105.1 3.1 %adapter_back.1 = (bf16[768,768]{1,0:T(8,128)(2,1)S(1)}, bf16[768,768]{1,0:T(8,128)(2,1)S(1)}, bf16[768,16]{1,0:T(8,128)(2,1)S(1)}, bf16[768,2304]{1,0:T(8,128)(...) custom-call(bf16[768,768]{1,0:T(8,128)(2,1)S(1)} %get-tuple-element., ...), custom_call_target="tpu_custom_call" | custom-call | flops 500000000 | bytes 12000000 | tf_op jit(solution)/shard_map/adapter_back/pallas_call | solution.py:534
  108.2 0.1 collective-permute-start.5
  108.3 1.2 collective-permute-done.5
  109.6 2.7 %collective-permute-start.6 = (bf16[32,768]{1,0:T(8,128)(2,1)S(1)}, bf16[32,768]{1,0:T(8,128)(2,1)S(1)}, u32[]{:S(2)}, u32[]{:S(2)}) collective-permute-start(bf16[32,768]{1,0:T(8,128)(2,1)S(1)} %get-tuple-element.152), channel_id=1, source_target_pairs={{0,1},{1,0},{2,3},{3,2},{4,5},{5,4},{6,7},{7,6},{8,9},{9,8},{10,11... | collective-permute-start | bytes 147464 | tf_op jit(solution)/shard_map/ppermute | solution.py:969
  112.3 1.5 %collective-permute-start.7 = (bf16[32,768]{1,0:T(8,128)(2,1)S(1)}, bf16[32,768]{1,0:T(8,128)(2,1)S(1)}, u32[]{:S(2)}, u32[]{:S(2)}) collective-permute-start(bf16[32,768]{1,0:T(8,128)(2,1)S(1)} %get-tuple-element.152), channel_id=1, source_target_pairs={{0,2},{1,3},{2,0},{3,1},{4,6},{5,7},{6,4},{7,5},{8,10},{9,11},{10,... | collective-permute-start | bytes 147464 | tf_op jit(solution)/shard_map/ppermute | solution.py:969
  113.8 4.5 %project_back.1 = f32[768,768]{1,0:T(8,128)} custom-call(f32[768,768]{1,0:T(8,128)S(1)} %get-tuple-element.130.datt_ref, bf16[768,768]{1,0:T(8,128)(2,1)S(1)} %get-tuple-element.121.dq_ref, bf16[768,768]{1,0:T(8,128)(2,1)S(1)} %get-tuple-element.131.dk_ref, bf16[768,768]{1,0:T(8,128)(2,1)S(1)} %get-tuple-element.132.dv_ref, ...), custom_call_target="tpu_custom_call" | custom-call | flops 2717908992 | bytes 4000000 | tf_op jit(solution)/shard_map/project_back/pallas_call | solution.py:534
  118.3 0.5 collective-permute-done.8
  118.8 3.7 %collective-permute-start.11 = (bf16[32,768]{1,0:T(8,128)(2,1)S(1)}, bf16[32,768]{1,0:T(8,128)(2,1)S(1)}, u32[]{:S(2)}, u32[]{:S(2)}) collective-permute-start(bf16[32,768]{1,0:T(8,128)(2,1)S(1)} %fusion), channel_id=1, source_target_pairs={{0,12},{1,13},{2,14},{3,15},{4,8},{5,9},{6,10},{7,11},{8,4},{9,5},... | collective-permute-start | bytes 147464 | tf_op jit(solution)/shard_map/ppermute | solution.py:969
  122.5 0.8 collective-permute-start.9
  123.3 2.1 %collective-permute-done.11 = bf16[32,768]{1,0:T(8,128)(2,1)S(1)} collective-permute-done((bf16[32,768]{1,0:T(8,128)(2,1)S(1)}, bf16[32,768]{1,0:T(8,128)(2,1)S(1)}, u32[]{:S(2)}, u32[]{:S(2)}) %collective-permute-start.11) | collective-permute-done | bytes 49184 | tf_op jit(solution)/shard_map/ppermute | solution.py:969
  125.3 2.2 %collective-permute-done.10 = bf16[32,768]{1,0:T(8,128)(2,1)S(1)} collective-permute-done((bf16[32,768]{1,0:T(8,128)(2,1)S(1)}, bf16[32,768]{1,0:T(8,128)(2,1)S(1)}, u32[]{:S(2)}, u32[]{:S(2)}) %collective-permute-start.10) | collective-permute-done | bytes 49184 | tf_op jit(solution)/shard_map/ppermute | solution.py:969
  127.7 1.2 collective-permute-done.12.theirs_ref
  128.9 1.1 adam.1
  (23 shorter events, 0.5 us)
Async XLA Ops:
  0.6 7.1 %copy-start = (s32[3,256]{1,0:T(4,128)S(1)}, s32[3,256]{1,0:T(4,128)}, u32[]{:S(2)}) copy-start(s32[3,256]{1,0:T(4,128)} %own_ref.13) | copy-start | bytes 9220
  0.6 7.2 %copy-start.1 = (s32[3]{0:T(128)S(1)}, s32[3]{0:T(128)}, u32[]{:S(2)}) copy-start(s32[3]{0:T(128)} %param.20) | copy-start | bytes 40
  7.2 3.4 %collective-permute-start.1 = (bf16[2,288,768]{2,1,0:T(8,128)(2,1)S(1)}, bf16[2,288,768]{2,1,0:T(8,128)(2,1)S(1)}, u32[]{:S(2)}, u32[]{:S(2)}) collective-permute-start(bf16[2,288,768]{2,1,0:T(8,128)(2,1)S(1)} %get-tuple-element.83), channel_id=1, source_target_pairs={{0,16},{16,0},{1,17},{17,1},{2,18},{18,2},{3,19},{19,3},{4,20},{20... | collective-permute-start | bytes 2654216 | tf_op jit(solution)/shard_map/ppermute | solution.py:1014
  7.7 2.8 %collective-permute-start = (s32[3,256]{1,0:T(4,128)S(1)}, s32[3,256]{1,0:T(4,128)S(1)}, u32[]{:S(2)}, u32[]{:S(2)}) collective-permute-start(s32[3,256]{1,0:T(4,128)S(1)} %copy-done), channel_id=1, source_target_pairs={{0,16},{16,0},{1,17},{17,1},{2,18},{18,2},{3,19},{19,3},{4,20},{20... | collective-permute-start | bytes 9224 | tf_op jit(solution)/shard_map/ppermute | solution.py:1008
  30.5 3.4 %collective-permute-start.2 = (bf16[2,288,768]{2,1,0:T(8,128)(2,1)S(1)}, bf16[2,288,768]{2,1,0:T(8,128)(2,1)S(1)}, u32[]{:S(2)}, u32[]{:S(2)}) collective-permute-start(bf16[2,288,768]{2,1,0:T(8,128)(2,1)S(1)} %get-tuple-element.87), channel_id=1, source_target_pairs={{0,16},{16,0},{1,17},{17,1},{2,18},{18,2},{3,19},{19,3},{4,20},{20... | collective-permute-start | bytes 2654216 | tf_op jit(solution)/shard_map/ppermute | solution.py:1018
  68.1 5.6 %collective-permute-start.3 = (bf16[2,288,768]{2,1,0:T(8,128)(2,1)S(1)}, bf16[2,288,768]{2,1,0:T(8,128)(2,1)S(1)}, u32[]{:S(2)}, u32[]{:S(2)}) collective-permute-start(bf16[2,288,768]{2,1,0:T(8,128)(2,1)S(1)} %get-tuple-element.98), channel_id=1, source_target_pairs={{0,16},{16,0},{1,17},{17,1},{2,18},{18,2},{3,19},{19,3},{4,20},{20... | collective-permute-start | bytes 2654216 | tf_op jit(solution)/shard_map/ppermute | solution.py:1023
  99.0 6.1 %collective-permute-start.4 = (bf16[2,288,768]{2,1,0:T(8,128)(2,1)S(1)}, bf16[2,288,768]{2,1,0:T(8,128)(2,1)S(1)}, u32[]{:S(2)}, u32[]{:S(2)}) collective-permute-start(bf16[2,288,768]{2,1,0:T(8,128)(2,1)S(1)} %get-tuple-element.124), channel_id=1, source_target_pairs={{0,16},{16,0},{1,17},{17,1},{2,18},{18,2},{3,19},{19,3},{4,20},{20... | collective-permute-start | bytes 2654216 | tf_op jit(solution)/shard_map/ppermute | solution.py:1027
  108.2 1.4 %collective-permute-start.5 = (f32[32,768]{1,0:T(8,128)S(1)}, f32[32,768]{1,0:T(8,128)S(1)}, u32[]{:S(2)}, u32[]{:S(2)}) collective-permute-start(f32[32,768]{1,0:T(8,128)S(1)} %get-tuple-element.128), channel_id=1, source_target_pairs={{0,16},{16,0},{1,17},{17,1},{2,18},{18,2},{3,19},{19,3},{4,20},{20... | collective-permute-start | bytes 294920 | tf_op jit(solution)/shard_map/ppermute | solution.py:964
  109.6 8.7 %collective-permute-start.6 = (bf16[32,768]{1,0:T(8,128)(2,1)S(1)}, bf16[32,768]{1,0:T(8,128)(2,1)S(1)}, u32[]{:S(2)}, u32[]{:S(2)}) collective-permute-start(bf16[32,768]{1,0:T(8,128)(2,1)S(1)} %get-tuple-element.152), channel_id=1, source_target_pairs={{0,1},{1,0},{2,3},{3,2},{4,5},{5,4},{6,7},{7,6},{8,9},{9,8},{10,11... | collective-permute-start | bytes 147464 | tf_op jit(solution)/shard_map/ppermute | solution.py:969
  112.3 6.0 %collective-permute-start.7 = (bf16[32,768]{1,0:T(8,128)(2,1)S(1)}, bf16[32,768]{1,0:T(8,128)(2,1)S(1)}, u32[]{:S(2)}, u32[]{:S(2)}) collective-permute-start(bf16[32,768]{1,0:T(8,128)(2,1)S(1)} %get-tuple-element.152), channel_id=1, source_target_pairs={{0,2},{1,3},{2,0},{3,1},{4,6},{5,7},{6,4},{7,5},{8,10},{9,11},{10,... | collective-permute-start | bytes 147464 | tf_op jit(solution)/shard_map/ppermute | solution.py:969
  113.8 5.0 %collective-permute-start.8 = (bf16[32,768]{1,0:T(8,128)(2,1)S(1)}, bf16[32,768]{1,0:T(8,128)(2,1)S(1)}, u32[]{:S(2)}, u32[]{:S(2)}) collective-permute-start(bf16[32,768]{1,0:T(8,128)(2,1)S(1)} %get-tuple-element.152), channel_id=1, source_target_pairs={{0,3},{1,2},{2,1},{3,0},{4,7},{5,6},{6,5},{7,4},{8,11},{9,10},{10,... | collective-permute-start | bytes 147464 | tf_op jit(solution)/shard_map/ppermute | solution.py:969
  113.8 13.8 %copy-start.2 = (s32[2,2,2]{2,1,0:T(2,128)S(1)}, s32[2,2,2]{2,1,0:T(2,128)}, u32[]{:S(2)}) copy-start(s32[2,2,2]{2,1,0:T(2,128)} %param.21) | copy-start | bytes 100
  118.8 6.5 %collective-permute-start.11 = (bf16[32,768]{1,0:T(8,128)(2,1)S(1)}, bf16[32,768]{1,0:T(8,128)(2,1)S(1)}, u32[]{:S(2)}, u32[]{:S(2)}) collective-permute-start(bf16[32,768]{1,0:T(8,128)(2,1)S(1)} %fusion), channel_id=1, source_target_pairs={{0,12},{1,13},{2,14},{3,15},{4,8},{5,9},{6,10},{7,11},{8,4},{9,5},... | collective-permute-start | bytes 147464 | tf_op jit(solution)/shard_map/ppermute | solution.py:969
  122.5 5.0 %collective-permute-start.10 = (bf16[32,768]{1,0:T(8,128)(2,1)S(1)}, bf16[32,768]{1,0:T(8,128)(2,1)S(1)}, u32[]{:S(2)}, u32[]{:S(2)}) collective-permute-start(bf16[32,768]{1,0:T(8,128)(2,1)S(1)} %fusion), channel_id=1, source_target_pairs={{0,8},{1,9},{2,10},{3,11},{4,12},{5,13},{6,14},{7,15},{8,0},{9,1},... | collective-permute-start | bytes 147464 | tf_op jit(solution)/shard_map/ppermute | solution.py:969
  122.5 5.0 %collective-permute-start.9 = (bf16[32,768]{1,0:T(8,128)(2,1)S(1)}, bf16[32,768]{1,0:T(8,128)(2,1)S(1)}, u32[]{:S(2)}, u32[]{:S(2)}) collective-permute-start(bf16[32,768]{1,0:T(8,128)(2,1)S(1)} %fusion), channel_id=1, source_target_pairs={{0,4},{1,5},{2,6},{3,7},{4,0},{5,1},{6,2},{7,3},{8,12},{9,13},{10,... | collective-permute-start | bytes 147464 | tf_op jit(solution)/shard_map/ppermute | solution.py:969
  127.6 1.4 %collective-permute-start.12 = (f32[32,768]{1,0:T(8,128)S(1)}, f32[32,768]{1,0:T(8,128)S(1)}, u32[]{:S(2)}, u32[]{:S(2)}) collective-permute-start(f32[32,768]{1,0:T(8,128)S(1)} %add_add_fusion.mine_ref), channel_id=1, source_target_pairs={{0,16},{16,0},{1,17},{17,1},{2,18},{18,2},{3,19},{19,3},{4,20},{20... | collective-permute-start | bytes 294920 | tf_op jit(solution)/shard_map/ppermute | solution.py:978

commit v5 on v4

--- a/solution.py
+++ b/solution.py
@@ -125,40 +125,34 @@
             return rows_at(s * (WINDOW + SUB) + sub * SUB, WINDOW, SUB)
         return rows_at(s * self.length, WINDOW, WINDOW)
 
-    def biases(self, sequences, rows_ref, columns_ref):
+    def biases(self, s, rows_ref=None, columns_ref=None):
         lane = lax.broadcasted_iota(jnp.int32, (1, 128), 1)
         place = jnp.where(lane < SUB, lane, lane - SUB)
         key_place = lax.broadcasted_iota(jnp.int32, (WINDOW, 128), 0)
         shape = (SUB, WINDOW)
         apart = lax.broadcasted_iota(jnp.int32, shape, 1) - lax.broadcasted_iota(jnp.int32, shape, 0)
-
-        def one(s):
-            query, key = self.ids(s)
-            for sub in range(2):
-                own = HALO if self.near else self.row0 + sub * SUB
-                if rows_ref is not None:
-                    keys = key[:, sub * SUB:sub * SUB + WINDOW] if self.near else key
-                    queries = column_of(query)[sub * SUB:(sub + 1) * SUB]
-                    seen = (queries == keys) | (apart == own)
-                    rows_ref[rows_at((s * 2 + sub) * SUB, SUB, SUB), :] = jnp.where(
-                        seen, 0.0, MASKED)
-                if columns_ref is None:
-                    continue
-                blocks = (128, 128, SUB) if self.near else (128, 128)
-                column = jnp.concatenate(
-                    [column_of(key[:, 128 * i:128 * i + n]) for i, n in enumerate(blocks)], axis=0)
-                keys = column[sub * SUB:sub * SUB + WINDOW] if self.near else column
-                turned = pltpu.roll(query, SUB, 1)
-                pair = (query, turned) if sub == 0 else (turned, query)
-                seen = (keys == jnp.where(lane < SUB, *pair)) | (key_place == place + own)
-                columns_ref[rows_at((s * 2 + sub) * WINDOW, WINDOW, WINDOW), :] = jnp.where(
-                    seen, 0.0, MASKED)
-
-        loop(sequences, one)
-
-
-def bias_shape(sequences, turned):
-    return ((sequences * 2 * WINDOW, 128) if turned else (sequences * 2 * SUB, WINDOW)), F32
+        query, key = self.ids(s)
+        if rows_ref is None:
+            blocks = (128, 128, SUB) if self.near else (128, 128)
+            column = jnp.concatenate(
+                [column_of(key[:, 128 * i:128 * i + n]) for i, n in enumerate(blocks)], axis=0)
+            turned = pltpu.roll(query, SUB, 1)
+        for sub in range(2):
+            own = HALO if self.near else self.row0 + sub * SUB
+            if rows_ref is not None:
+                keys = key[:, sub * SUB:sub * SUB + WINDOW] if self.near else key
+                queries = column_of(query)[sub * SUB:(sub + 1) * SUB]
+                seen = (queries == keys) | (apart == own)
+                rows_ref[sub * SUB:(sub + 1) * SUB, :] = jnp.where(seen, 0.0, MASKED)
+                continue
+            keys = column[sub * SUB:sub * SUB + WINDOW] if self.near else column
+            pair = (query, turned) if sub == 0 else (turned, query)
+            seen = (keys == jnp.where(lane < SUB, *pair)) | (key_place == place + own)
+            columns_ref[sub * WINDOW:(sub + 1) * WINDOW, :] = jnp.where(seen, 0.0, MASKED)
+
+
+def bias_shape(turned):
+    return ((2 * WINDOW, 128) if turned else (2 * SUB, WINDOW)), F32
 
 
 def half(sub):
@@ -184,7 +178,7 @@
         slot = (2 * quad + sub) % SLOTS
         scores_ref[slot] = dot_nt(q4, k_ref[keys, cols])
         yield True
-        bias = bias_ref[rows_at((s * 2 + sub) * SUB, SUB, SUB), :]
+        bias = bias_ref[sub * SUB:(sub + 1) * SUB, :]
         totals = []
         for h in range(4):
             rows = slice(h * SUB, (h + 1) * SUB)
@@ -203,11 +197,10 @@
     pipelined(unit(quad, sub) for quad in range(width // QUAD) for sub in range(2))
 
 
-def attention_backward(where, s, q_ref, k_ref, v_ref, dmix_ref, dmix_rows, delta_ref, dq_ref,
+def attention_backward(where, s, q_ref, k_ref, v_ref, dmix_ref, dmix_rows, delta, dq_ref,
                        dq_rows, key_terms, bias_ref, scratch):
     low = low_lanes()
     scores_ref, share_ref, d_share_ref, d_scores_ref = scratch
-    delta = delta_ref[rows_at(s * HEAD_ROWS, HEAD_ROWS, HEAD_ROWS), :]
     delta = jnp.where(where.row0 == 0, delta[:, :BLOCK], delta[:, BLOCK:])
     turned = pltpu.roll(delta, SUB, 1)
     first_half = lax.broadcasted_iota(jnp.int32, (1, 2 * SUB), 1) < SUB
@@ -221,7 +214,7 @@
         scores_ref[slot] = dot_nt(k_ref[keys, cols], q4)
         d_share_ref[slot] = dot_nt(v_ref[keys, cols], d4)
         yield True
-        bias = bias_ref[rows_at((s * 2 + sub) * WINDOW, WINDOW, WINDOW), :]
+        bias = bias_ref[sub * WINDOW:(sub + 1) * WINDOW, :]
         shares, d_scores = [], []
         left, right = (delta, turned) if sub == 0 else (turned, delta)
         for i in range(2):
@@ -252,21 +245,14 @@
     pipelined(units())
 
 
-def row_deltas(sequences, length, dmix_ref, mix_ref, delta_ref):
-    width = dmix_ref.shape[1]
-    shape = (HEAD_ROWS, width)
+def row_deltas(dmix, mix):
+    shape = (HEAD_ROWS, dmix.shape[1])
     own = (lax.broadcasted_iota(jnp.int32, shape, 1) // 64
            == lax.broadcasted_iota(jnp.int32, shape, 0)).astype(F32).astype(BF16)
-
-    def one(s):
-        rows = rows_at(s * length, length, length)
-        product = dmix_ref[rows, :].astype(F32) * mix_ref[rows, :].astype(F32)
-        high = product.astype(BF16)
-        rest = (product - high.astype(F32)).astype(BF16)
-        delta_ref[rows_at(s * HEAD_ROWS, HEAD_ROWS, HEAD_ROWS), :] = (
-            dot_nt(own, high) + dot_nt(own, rest))
-
-    loop(sequences, one)
+    product = dmix.astype(F32) * mix.astype(F32)
+    high = product.astype(BF16)
+    rest = (product - high.astype(F32)).astype(BF16)
+    return dot_nt(own, high) + dot_nt(own, rest)
 
 
 def near_keys(s, length, k_ref, v_ref, halo_ref, nk_ref, nv_ref):
@@ -405,8 +391,7 @@
 
 
 def layer_rest_back(sequences, length, gradient, waits, n1_ref, r1_ref, dg_ref, n2_ref, r2_ref,
-                    wo_ref, wu_ref, wd_ref, vec_ref, two_ref, low_ref, gate_ref, datt_ref,
-                    mix_ref, delta_ref):
+                    wo_ref, wu_ref, wd_ref, vec_ref, two_ref, low_ref, gate_ref, datt_ref):
     tokens, hidden = low_ref.shape[0], wu_ref.shape[1]
     waits[0]()
     vec = vec_ref[...].astype(F32)
@@ -457,31 +442,39 @@
     loop(2, up)
     loop(sequences, first)
     loop(2, mixture)
-    row_deltas(sequences, length, low_ref, mix_ref, delta_ref)
-
-
-def near_backward(near, sequences, length, q_ref, nk_ref, nv_ref, dmix_ref, delta_ref,
-                  dfar_ref, dq_ref, dnk_ref, dnv_ref, dhalo_ref, bias_ref, scratch):
-    side, wide = near.side, WINDOW + SUB
+
+
+def near_backward(near, sequences, length, q_ref, nk_ref, nv_ref, dmix_ref, mix_ref,
+                  delta_ref, dfar_ref, dq_ref, dnk_ref, dnv_ref, dhalo_ref, bias_ref, scratch):
+    side, all_rows = near.side, length + HALO
+    width = q_ref.shape[1]
 
     def key_terms(s, cols, kept):
         for out, which, other in ((dnv_ref, 0, 3), (dnk_ref, 1, 2)):
             left, right = [item[which] for item in kept], [item[other] for item in kept]
-            out[rows_at(s * wide, SUB, SUB), cols] = dot_nn(left[0][:SUB], right[0])
+            start = s * all_rows + (length + HALO - WINDOW - SUB) * (1 - side)
+            out[rows_at(start, SUB, 32), cols] = dot_nn(left[0][:SUB], right[0])
             both = jnp.concatenate([left[0][SUB:], left[1][:WINDOW - SUB]], axis=1)
-            out[rows_at(s * wide + SUB, WINDOW - SUB, SUB), cols] = dot_nn(
+            out[rows_at(start + SUB, WINDOW - SUB, 32), cols] = dot_nn(
                 both, jnp.concatenate(right, axis=0))
-            out[rows_at(s * wide + WINDOW, SUB, SUB), cols] = dot_nn(
+            out[rows_at(start + WINDOW, SUB, 32), cols] = dot_nn(
                 left[1][WINDOW - SUB:], right[1])
 
     def one(s):
         dfar_ref[rows_at(s * BLOCK, BLOCK, BLOCK), :] = dmix_ref[
             rows_at(s * length + side * BLOCK, BLOCK, BLOCK), :]
+        near.biases(s, None, bias_ref)
+        rows = rows_at(s * length, length, length)
+        delta = row_deltas(dmix_ref[rows, :], mix_ref[rows, :])
+        delta_ref[rows_at(s * HEAD_ROWS, HEAD_ROWS, HEAD_ROWS), :] = delta
         attention_backward(
-            near, s, q_ref, nk_ref, nv_ref, dmix_ref, near.queries, delta_ref, dq_ref,
+            near, s, q_ref, nk_ref, nv_ref, dmix_ref, near.queries, delta, dq_ref,
             lambda s, sub: rows_at(s * BLOCK + sub * SUB, SUB, SUB), key_terms, bias_ref,
             scratch)
-        halo = rows_at(s * wide + (wide - HALO) * (1 - side), HALO, 32)
+        unseen = rows_at(s * all_rows + (WINDOW + SUB) * side, all_rows - WINDOW - SUB, 32)
+        for out in (dnk_ref, dnv_ref):
+            out[unseen, :] = jnp.zeros((all_rows - WINDOW - SUB, width), F32)
+        halo = rows_at(s * all_rows + length * (1 - side), HALO, 32)
         dhalo_ref[0, rows_at(s * HALO, HALO, 32), :] = (
             dnk_ref[halo, :] * (1.0 / LOG2E)).astype(BF16)
         dhalo_ref[1, rows_at(s * HALO, HALO, 32), :] = dnv_ref[halo, :].astype(BF16)
@@ -500,12 +493,12 @@
         rows = rows_at(s * length, length, length)
         taken = rows_at(s * length + (1 - side) * (length - HALO), HALO, 32)
         hrows = rows_at(s * HALO, HALO, 32)
-        dk_ref[rows, :] = dk_ref[rows, :] * (1.0 / LOG2E)
-        dk_ref[taken, :] = dk_ref[taken, :] + dhalo_ref[0, hrows, :].astype(F32)
-        dv_ref[taken, :] = dv_ref[taken, :] + dhalo_ref[1, hrows, :].astype(F32)
-        dkb_ref[rows, :] = dk_ref[rows, :].astype(BF16)
-        dv16 = dv_ref[rows, :].astype(BF16)
-        dvb_ref[rows, :] = dv16
+        dvb_ref[rows, :] = dv_ref[rows, :].astype(BF16)
+        dvb_ref[taken, :] = (dv_ref[taken, :] + dhalo_ref[1, hrows, :].astype(F32)).astype(BF16)
+        dkb_ref[rows, :] = (dk_ref[rows, :] * (1.0 / LOG2E)).astype(BF16)
+        dkb_ref[taken, :] = (
+            dk_ref[taken, :] * (1.0 / LOG2E) + dhalo_ref[0, hrows, :].astype(F32)).astype(BF16)
+        dv16 = dvb_ref[rows, :]
         du_ref[rows, :] = (2.0 * (dot_nt(dq_ref[rows, :], up_q) + dot_nt(dv16, up_v))).astype(BF16)
 
     loop(sequences, one)
@@ -597,20 +590,25 @@
 
     def kernel(q_ref, k_ref, v_ref, own_ref, live_ref, out_ref, bias_ref, *scratch):
         where = Side(False, length, (own_ref, None, live_ref))
-        where.biases(sequences, bias_ref, None)
-        loop(sequences, lambda s: attention_forward(
-            where, s, q_ref, k_ref, v_ref, out_ref,
-            lambda s, sub: rows_at(s * BLOCK + sub * SUB, SUB, SUB), bias_ref, scratch))
+
+        def one(s):
+            where.biases(s, bias_ref)
+            attention_forward(
+                where, s, q_ref, k_ref, v_ref, out_ref,
+                lambda s, sub: rows_at(s * BLOCK + sub * SUB, SUB, SUB), bias_ref, scratch)
+
+        loop(sequences, one)
 
     return call(
         kernel, "attention_far", [(VMEM, item) for item in (q, k, v, ids[0])] + [(VMEM, ids[2])],
         [(VMEM, (sequences * BLOCK, width), BF16)],
-        [bias_shape(sequences, False)] + attention_scratch(), 2000000000, 6000000, 8)[0]
+        [bias_shape(False)] + attention_scratch(), 2000000000, 6000000, 8)[0]
 
 
 def near_forward(near, sequences, length, far_ref, q_ref, k_ref, v_ref, halo_ref, nk_ref,
                  nv_ref, mix_ref, bias_ref, scratch):
     def one(s):
+        near.biases(s, bias_ref)
         near_keys(s, length, k_ref, v_ref, halo_ref, nk_ref, nv_ref)
         mix_ref[rows_at(s * length + near.side * BLOCK, BLOCK, BLOCK), :] = far_ref[
             rows_at(s * BLOCK, BLOCK, BLOCK), :]
@@ -645,7 +643,6 @@
              (r2_ref, r2_out), (one_ref, h_out), (low_ref, x_out), (u_ref, u_out),
              (mix_ref, mix_out)], outs)
         near = Side(True, length, (own_ref, other_ref, live_ref))
-        near.biases(sequences, bias_ref, None)
         near_forward(near, sequences, length, far_ref, q_ref, k_ref, v_ref, halo_ref, nk_ref,
                      nv_ref, mix_ref, bias_ref, scratch)
         layer_rest(layer, sequences, length, mix_ref, h_ref, wo_ref, wu_ref, wd_ref,
@@ -676,7 +673,7 @@
          ((width, hidden), BF16), ((hidden, width), BF16), ((8, width), BF16),
          (bias_up.shape, BF16), ((8, width), BF16), factors, factors, small, act, wide, act, deep,
          act, stat, deep, act, stat, near, near, 10, 14,
-         bias_shape(sequences, False)] + attention_scratch(),
+         bias_shape(False)] + attention_scratch(),
         2 * tokens * width * (2 * hidden + 4 * width), 24000000, 42)
 
 
@@ -697,7 +694,6 @@
              (g_hbm, g_ref)], ins))
         store = pltpu.make_async_copy(last_ref, hidden_out, outs.at[0])
         near = Side(True, length, (own_ref, other_ref, live_ref))
-        near.biases(sequences, bias_ref, columns_ref)
         near_forward(near, sequences, length, far_ref, q_ref, k_ref, v_ref, halo_ref, nk_ref,
                      nv_ref, mix_ref, bias_ref, scratch)
         side = lax.axis_index("seq")
@@ -716,27 +712,27 @@
         layer_rest_back(sequences, length, given,
                         [wait_for(loads, 6), nothing, nothing, nothing], n1_ref,
                         r1_ref, dg_ref, n2_ref, r2_ref, wo_ref, wu_ref, wd_ref, vec_ref, one_ref,
-                        low_ref, act_ref, datt_ref, mix_ref, delta_ref)
-        near_backward(near, sequences, length, q_ref, nk_ref, nv_ref, low_ref,
+                        low_ref, act_ref, datt_ref)
+        near_backward(near, sequences, length, q_ref, nk_ref, nv_ref, low_ref, mix_ref,
                       delta_ref, dfar_ref, dq_ref, dnk_ref, dnv_ref, dhalo_ref, columns_ref, scratch)
         store.wait()
 
     act, stat = ((tokens, width), BF16), ((tokens, 128), F32)
     wide, deep = ((tokens, width), F32), ((tokens, hidden), BF16)
-    near_rows = sequences * (WINDOW + SUB)
+    near_rows, ordered = sequences * (WINDOW + SUB), sequences * (length + HALO)
     near, block = ((near_rows, width), BF16), ((sequences * BLOCK, width), BF16)
     return call(
         kernel, "turn",
         [(VMEM, ids[0]), (VMEM, ids[1]), (VMEM, ids[2]), (VMEM, far), (VMEM, q), (VMEM, k),
          (VMEM, v), (VMEM, halo)]
         + [(HBM, item) for item in (h, gradient, wo, wu, wd, vec, bias_up)],
-        [(VMEM,) + wide, (VMEM,) + block, (VMEM,) + block, (VMEM, (near_rows, width), F32),
-         (VMEM, (near_rows, width), F32), (VMEM, (2, sequences * HALO, width), BF16),
+        [(VMEM,) + wide, (VMEM,) + block, (VMEM,) + block, (VMEM, (ordered, width), F32),
+         (VMEM, (ordered, width), F32), (VMEM, (2, sequences * HALO, width), BF16),
          (VMEM, (HEAD_ROWS * sequences, length), F32), (HBM,) + act],
         [(h.shape, h.dtype), act, ((width, width), BF16), ((width, hidden), BF16),
          ((hidden, width), BF16), ((8, width), BF16), (bias_up.shape, BF16), act, wide, act, deep,
-         act, stat, deep, act, stat, near, near, act, 7, 1, bias_shape(sequences, False),
-         bias_shape(sequences, True)] + attention_scratch(True),
+         act, stat, deep, act, stat, near, near, act, 7, 1, bias_shape(False),
+         bias_shape(True)] + attention_scratch(True),
         4 * tokens * width * (2 * hidden + width), 24000000, 42)
 
 
@@ -747,26 +743,24 @@
                dnv_ref, dq_ref, dk_ref, dv_ref, bias_ref,
                *scratch):
         far = Side(False, length, (own_ref, None, live_ref))
-        far.biases(sequences, None, bias_ref)
-        side, wide, own = far.side, WINDOW + SUB, WINDOW + SUB - HALO
+        side = far.side
 
         def key_terms(s, cols, kept):
-            for out, which, other in ((dv_ref, 0, 3), (dk_ref, 1, 2)):
+            near = rows_at(s * (length + HALO) + HALO * side, length, 32)
+            for out, term, which, other in ((dv_ref, dnv_ref, 0, 3), (dk_ref, dnk_ref, 1, 2)):
                 left = jnp.concatenate([item[which] for item in kept], axis=1)
                 right = jnp.concatenate([item[other] for item in kept], axis=0)
-                out[far.keys(s, 0), cols] = dot_nn(left, right)
+                out[far.keys(s, 0), cols] = dot_nn(left, right) + term[near, cols]
 
         def one(s):
+            far.biases(s, None, bias_ref)
+            delta = delta_ref[rows_at(s * HEAD_ROWS, HEAD_ROWS, HEAD_ROWS), :]
             attention_backward(
                 far, s, q_ref, k_ref, v_ref, dfar_ref,
-                lambda s, sub: rows_at(s * BLOCK + sub * SUB, SUB, SUB), delta_ref, dq_ref,
+                lambda s, sub: rows_at(s * BLOCK + sub * SUB, SUB, SUB), delta, dq_ref,
                 far.queries, key_terms, bias_ref, scratch)
             dq_ref[rows_at(s * length + (1 - side) * BLOCK, BLOCK, BLOCK), :] = dqn_ref[
                 rows_at(s * BLOCK, BLOCK, BLOCK), :]
-            mine = rows_at(s * length + (length - own) * (1 - side), own, 32)
-            theirs = rows_at(s * wide + HALO * side, own, 32)
-            dk_ref[mine, :] = dk_ref[mine, :] + dnk_ref[theirs, :]
-            dv_ref[mine, :] = dv_ref[mine, :] + dnv_ref[theirs, :]
 
         loop(sequences, one)
 
@@ -776,7 +770,7 @@
         [(VMEM, ids[0]), (VMEM, ids[2])]
         + [(VMEM, item) for item in (q, k, v, dfar, delta, dq_near, dnk, dnv)],
         [(VMEM, (tokens, width), BF16), wide, wide],
-        [bias_shape(sequences, True)] + attention_scratch(True), 4000000000, 16000000, 8)
+        [bias_shape(True)] + attention_scratch(True), 4000000000, 16000000, 8)
 
 
 def back_call(layer, sequences, length, ids, dq, dk, dv, dhalo, datt, u, x, saved, w, a, b, wo, wu,
@@ -820,19 +814,17 @@
         layer_rest_back(sequences, length, given,
                         [wait_for(loads, 5, 6, 7), wait_for(loads, 8, 9), wait_for(loads, 10),
                          wait_for(loads, 11, 12, 13, 19)], n1_ref, r1_ref, dg_ref, n2_ref, r2_ref,
-                        wo_ref, wu_ref, wd_ref, vec_ref, two_ref, low_ref, dg_ref, datt_out,
-                        mix_ref, delta_ref)
+                        wo_ref, wu_ref, wd_ref, vec_ref, two_ref, low_ref, dg_ref, datt_out)
         wait_for(loads, 14, 15, 16)()
         near = Side(True, length, (own_ref, other_ref, live_ref))
-        near.biases(sequences, None, bias_ref)
-        near_backward(near, sequences, length, q_ref, nk_ref, nv_ref, low_ref,
+        near_backward(near, sequences, length, q_ref, nk_ref, nv_ref, low_ref, mix_ref,
                       delta_ref, dfar_ref, dqn_ref, dnk_ref, dnv_ref, dhalo_out, bias_ref, scratch)
         wait_for(loads, 17, 18)()
         store.wait()
 
     act, stat = ((tokens, width), BF16), ((tokens, 128), F32)
     wide, deep = ((tokens, width), F32), ((tokens, hidden), BF16)
-    near_rows = sequences * (WINDOW + SUB)
+    near_rows, ordered = sequences * (WINDOW + SUB), sequences * (length + HALO)
     near, block = ((near_rows, width), BF16), ((sequences * BLOCK, width), BF16)
     small, factors = ((tokens, 2 * rank), BF16), ((2, rank, width), F32)
     grad = ((4 * rank, width), F32)
@@ -842,13 +834,13 @@
         + [(VMEM, item) for item in (dq, dk, dv, dhalo, datt)]
         + [(HBM, item) for item in (u, x, *saved, w, a, b, wo, wu, wd, vec)],
         [(VMEM,) + wide, (VMEM,) + block, (VMEM,) + block,
-         (VMEM, (near_rows, width), F32), (VMEM, (near_rows, width), F32),
+         (VMEM, (ordered, width), F32), (VMEM, (ordered, width), F32),
          (VMEM, (2, sequences * HALO, width), BF16), (VMEM, (HEAD_ROWS * sequences, length), F32),
          (VMEM,) + act, (VMEM,) + act, (VMEM,) + act,
          (HBM,) + grad],
         [small, act, act, stat, deep, act, stat, near, near, ((width, 3 * width), BF16), factors,
          factors, ((width, width), BF16), ((width, hidden), BF16), ((hidden, width), BF16),
-         ((8, width), BF16), act, act, small, grad, wide, act, act, 20, 1, bias_shape(sequences, True)]
+         ((8, width), BF16), act, act, small, grad, wide, act, act, 20, 1, bias_shape(True)]
         + attention_scratch(True),
         2 * tokens * width * (2 * hidden + 4 * width), 24000000, 38)
 

time: 130 us -> 126 us (0.969)
  Pallas kernels: 111 us -> 107 us
    pallas_call x11, Pallas kernels: 111 us -> 107 us  [call(): pl.pallas_call(kernel, name=name, out_shape=tuple((space(shape, dtype) fo...]
  transfers between devices with their start and end apart: 13 -> 13, of which waited for: 5 -> 5; matrix products, arithmetic and copies ran while one was open for 0% -> 0% of each run, Pallas kernels for 16% -> 15%
where the time goes in v5:
time: 126 us; the launch traced here: 125 us
  Pallas kernels  107 us (85%)
  starting transfers between devices  10.7 us (8%)
  waiting for transfers between devices  7.11 us (6%)
    pallas_call x11, Pallas kernels, call(): pl.pallas_call(kernel, name=name, out_shape=tuple((space(shape, dtype) fo...  107 us
    ppermute x6, starting transfers between devices, sum_while(): lax.ppermute(given, 'batch', [(i, i ^ step * d) for i in range(batch)])  8.72 us
    ppermute x6, waiting for transfers between devices, sum_while(): lax.ppermute(given, 'batch', [(i, i ^ step * d) for i in range(batch)])  4.69 us
  transfers between devices with their start and end apart: 13, of which 5 were waited for; matrix products, arithmetic and copies ran while one was open for 0% of the time, Pallas kernels for 15%

profile of v5, /device:TPU:0, one launch (start us, length us, event | category | flops | bytes accessed | tf_op | source)
XLA Modules:
  0.0 125.5 jit_solution(9492584650200950076)
XLA Ops:
  0.7 6.5 %project_in.1 = (bf16[768,768]{1,0:T(8,128)(2,1)S(1)}, bf16[768,768]{1,0:T(8,128)(2,1)S(1)}, bf16[768,768]{1,0:T(8,128)(2,1)S(1)}, bf16[2,288,768]{2,1,0:T(8,128)(2,1)S(1)}, bf16[768,16]{1,0:T(8,128)(2,1)}) custom-call(bf16[768,768]{1,0:T(8,128)(2,1)} %bitcast.19, bf16[2,768,2304]{2,1,0:T(8,128)(2,1)} %w_hbm.7, f32[2,2,8,768]{3,2,1,0:T(8,128)} %rest_0_.1, ...), custom_call_target="tpu_custom_call" | custom-call | flops 2717908992 | bytes 12000000 | tf_op jit(solution)/shard_map/project_in/pallas_call | solution.py:527
  7.2 0.5 collective-permute-start.1
  7.8 2.5 %attention_far.2.far_ref = bf16[384,768]{1,0:T(8,128)(2,1)S(1)} custom-call(bf16[768,768]{1,0:T(8,128)(2,1)S(1)} %get-tuple-element.80.q_ref, bf16[768,768]{1,0:T(8,128)(2,1)S(1)} %get-tuple-element.81.k_ref, bf16[768,768]{1,0:T(8,128)(2,1)S(1)} %get-tuple-element.82.v_ref, s32[3,256]{1,0:T(4,128)S(1)} %copy-done, s32[1,3]{1,0:T(1,128)S(1)} %bitcast.11), custom_call_target="tpu_custom_call" | custom-call | flops 2000000000 | bytes 6000000 | tf_op jit(solution)/shard_map/attention_far/pallas_call | solution.py:527
  10.4 19.5 %middle.1 = (bf16[768,768]{1,0:T(8,128)(2,1)S(1)}, bf16[768,768]{1,0:T(8,128)(2,1)S(1)}, bf16[768,768]{1,0:T(8,128)(2,1)S(1)}, bf16[2,288,768]{2,1,0:T(8,128)(2,...) custom-call(s32[3,256]{1,0:T(4,128)S(1)} %copy-done, ...), custom_call_target="tpu_custom_call" | custom-call | flops 10871635968 | bytes 24000000 | tf_op jit(solution)/shard_map/middle/pallas_call | solution.py:527
  29.8 0.5 collective-permute-start.2
  30.3 2.6 %attention_far.3.far_ref = bf16[384,768]{1,0:T(8,128)(2,1)S(1)} custom-call(bf16[768,768]{1,0:T(8,128)(2,1)S(1)} %get-tuple-element.84.q_ref, bf16[768,768]{1,0:T(8,128)(2,1)S(1)} %get-tuple-element.85.k_ref, bf16[768,768]{1,0:T(8,128)(2,1)S(1)} %get-tuple-element.86.v_ref, s32[3,256]{1,0:T(4,128)S(1)} %copy-done, s32[1,3]{1,0:T(1,128)S(1)} %bitcast.13), custom_call_target="tpu_custom_call" | custom-call | flops 2000000000 | bytes 6000000 | tf_op jit(solution)/shard_map/attention_far/pallas_call | solution.py:527
  32.9 33.0 %turn.1 = (f32[768,768]{1,0:T(8,128)S(1)}, bf16[384,768]{1,0:T(8,128)(2,1)S(1)}, bf16[384,768]{1,0:T(8,128)(2,1)S(1)}, f32[1056,768]{1,0:T(8,128)S(1)}, f32[1056...) custom-call(s32[3,256]{1,0:T(4,128)S(1)} %copy-done, ...), custom_call_target="tpu_custom_call" | custom-call | flops 16307453952 | bytes 24000000 | tf_op jit(solution)/shard_map/turn/pallas_call | solution.py:527
  66.1 4.8 %back_far.2 = (bf16[768,768]{1,0:T(8,128)(2,1)S(1)}, f32[768,768]{1,0:T(8,128)S(1)}, f32[768,768]{1,0:T(8,128)S(1)}) custom-call(s32[3,256]{1,0:T(4,128)S(1)} %copy-done, s32[1,3]{1,0:T(1,128)S(1)} %bitcast.15, bf16[768,768]{1,0:T(8,128)(2,1)S(1)} %get-tuple-element.84.q_ref, bf16[768,768]{1,0:T(8,128)(2,1)S(1)} %get-tuple-element.85.k_ref, ...), custom_call_target="tpu_custom_call" | custom-call | flops 4000000000 | bytes 16000000 | tf_op jit(solution)/shard_map/back_far/pallas_call | solution.py:527
  70.8 24.2 %back.1 = (f32[768,768]{1,0:T(8,128)S(1)}, bf16[384,768]{1,0:T(8,128)(2,1)S(1)}, bf16[384,768]{1,0:T(8,128)(2,1)S(1)}, f32[1056,768]{1,0:T(8,128)S(1)}, f32[1056...) custom-call(s32[3,256]{1,0:T(4,128)S(1)} %copy-done, ...), custom_call_target="tpu_custom_call" | custom-call | flops 10871635968 | bytes 24000000 | tf_op jit(solution)/shard_map/back/pallas_call | solution.py:527
  95.0 0.5 collective-permute-start.4
  95.5 4.7 %back_far.3 = (bf16[768,768]{1,0:T(8,128)(2,1)S(1)}, f32[768,768]{1,0:T(8,128)S(1)}, f32[768,768]{1,0:T(8,128)S(1)}) custom-call(s32[3,256]{1,0:T(4,128)S(1)} %copy-done, s32[1,3]{1,0:T(1,128)S(1)} %bitcast.17, bf16[768,768]{1,0:T(8,128)(2,1)S(1)} %get-tuple-element.113.q_ref, bf16[768,768]{1,0:T(8,128)(2,1)S(1)} %get-tuple-element.114.k_ref, ...), custom_call_target="tpu_custom_call" | custom-call | flops 4000000000 | bytes 16000000 | tf_op jit(solution)/shard_map/back_far/pallas_call | solution.py:527
  100.3 3.2 %adapter_back.1 = (bf16[768,768]{1,0:T(8,128)(2,1)S(1)}, bf16[768,768]{1,0:T(8,128)(2,1)S(1)}, bf16[768,16]{1,0:T(8,128)(2,1)S(1)}, bf16[768,2304]{1,0:T(8,128)(...) custom-call(bf16[768,768]{1,0:T(8,128)(2,1)S(1)} %get-tuple-element., ...), custom_call_target="tpu_custom_call" | custom-call | flops 500000000 | bytes 12000000 | tf_op jit(solution)/shard_map/adapter_back/pallas_call | solution.py:527
  103.5 0.2 collective-permute-start.5
  103.7 1.2 collective-permute-done.5
  104.9 2.7 %collective-permute-start.6 = (bf16[32,768]{1,0:T(8,128)(2,1)S(1)}, bf16[32,768]{1,0:T(8,128)(2,1)S(1)}, u32[]{:S(2)}, u32[]{:S(2)}) collective-permute-start(bf16[32,768]{1,0:T(8,128)(2,1)S(1)} %get-tuple-element.152), channel_id=1, source_target_pairs={{0,1},{1,0},{2,3},{3,2},{4,5},{5,4},{6,7},{7,6},{8,9},{9,8},{10,11... | collective-permute-start | bytes 147464 | tf_op jit(solution)/shard_map/ppermute | solution.py:961
  107.6 1.5 %collective-permute-start.7 = (bf16[32,768]{1,0:T(8,128)(2,1)S(1)}, bf16[32,768]{1,0:T(8,128)(2,1)S(1)}, u32[]{:S(2)}, u32[]{:S(2)}) collective-permute-start(bf16[32,768]{1,0:T(8,128)(2,1)S(1)} %get-tuple-element.152), channel_id=1, source_target_pairs={{0,2},{1,3},{2,0},{3,1},{4,6},{5,7},{6,4},{7,5},{8,10},{9,11},{10,... | collective-permute-start | bytes 147464 | tf_op jit(solution)/shard_map/ppermute | solution.py:961
  109.2 4.5 %project_back.1 = f32[768,768]{1,0:T(8,128)} custom-call(f32[768,768]{1,0:T(8,128)S(1)} %get-tuple-element.130.datt_ref, bf16[768,768]{1,0:T(8,128)(2,1)S(1)} %get-tuple-element.121.dq_ref, bf16[768,768]{1,0:T(8,128)(2,1)S(1)} %get-tuple-element.131.dk_ref, bf16[768,768]{1,0:T(8,128)(2,1)S(1)} %get-tuple-element.132.dv_ref, ...), custom_call_target="tpu_custom_call" | custom-call | flops 2717908992 | bytes 4000000 | tf_op jit(solution)/shard_map/project_back/pallas_call | solution.py:527
  113.7 0.4 collective-permute-done.8
  114.1 3.7 %collective-permute-start.11 = (bf16[32,768]{1,0:T(8,128)(2,1)S(1)}, bf16[32,768]{1,0:T(8,128)(2,1)S(1)}, u32[]{:S(2)}, u32[]{:S(2)}) collective-permute-start(bf16[32,768]{1,0:T(8,128)(2,1)S(1)} %fusion), channel_id=1, source_target_pairs={{0,12},{1,13},{2,14},{3,15},{4,8},{5,9},{6,10},{7,11},{8,4},{9,5},... | collective-permute-start | bytes 147464 | tf_op jit(solution)/shard_map/ppermute | solution.py:961
  117.8 0.7 collective-permute-start.9
  118.6 2.1 %collective-permute-done.11 = bf16[32,768]{1,0:T(8,128)(2,1)S(1)} collective-permute-done((bf16[32,768]{1,0:T(8,128)(2,1)S(1)}, bf16[32,768]{1,0:T(8,128)(2,1)S(1)}, u32[]{:S(2)}, u32[]{:S(2)}) %collective-permute-start.11) | collective-permute-done | bytes 49184 | tf_op jit(solution)/shard_map/ppermute | solution.py:961
  120.7 2.2 %collective-permute-done.10 = bf16[32,768]{1,0:T(8,128)(2,1)S(1)} collective-permute-done((bf16[32,768]{1,0:T(8,128)(2,1)S(1)}, bf16[32,768]{1,0:T(8,128)(2,1)S(1)}, u32[]{:S(2)}, u32[]{:S(2)}) %collective-permute-start.10) | collective-permute-done | bytes 49184 | tf_op jit(solution)/shard_map/ppermute | solution.py:961
  123.1 1.2 collective-permute-done.12.theirs_ref
  124.3 1.1 adam.1
  (23 shorter events, 0.6 us)
Async XLA Ops:
  0.6 7.1 %copy-start = (s32[3,256]{1,0:T(4,128)S(1)}, s32[3,256]{1,0:T(4,128)}, u32[]{:S(2)}) copy-start(s32[3,256]{1,0:T(4,128)} %own_ref.13) | copy-start | bytes 9220
  0.6 7.2 %copy-start.1 = (s32[3]{0:T(128)S(1)}, s32[3]{0:T(128)}, u32[]{:S(2)}) copy-start(s32[3]{0:T(128)} %param.20) | copy-start | bytes 40
  7.2 3.2 %collective-permute-start.1 = (bf16[2,288,768]{2,1,0:T(8,128)(2,1)S(1)}, bf16[2,288,768]{2,1,0:T(8,128)(2,1)S(1)}, u32[]{:S(2)}, u32[]{:S(2)}) collective-permute-start(bf16[2,288,768]{2,1,0:T(8,128)(2,1)S(1)} %get-tuple-element.83), channel_id=1, source_target_pairs={{0,16},{16,0},{1,17},{17,1},{2,18},{18,2},{3,19},{19,3},{4,20},{20... | collective-permute-start | bytes 2654216 | tf_op jit(solution)/shard_map/ppermute | solution.py:1006
  7.7 2.6 %collective-permute-start = (s32[3,256]{1,0:T(4,128)S(1)}, s32[3,256]{1,0:T(4,128)S(1)}, u32[]{:S(2)}, u32[]{:S(2)}) collective-permute-start(s32[3,256]{1,0:T(4,128)S(1)} %copy-done), channel_id=1, source_target_pairs={{0,16},{16,0},{1,17},{17,1},{2,18},{18,2},{3,19},{19,3},{4,20},{20... | collective-permute-start | bytes 9224 | tf_op jit(solution)/shard_map/ppermute | solution.py:1000
  29.8 3.1 %collective-permute-start.2 = (bf16[2,288,768]{2,1,0:T(8,128)(2,1)S(1)}, bf16[2,288,768]{2,1,0:T(8,128)(2,1)S(1)}, u32[]{:S(2)}, u32[]{:S(2)}) collective-permute-start(bf16[2,288,768]{2,1,0:T(8,128)(2,1)S(1)} %get-tuple-element.87), channel_id=1, source_target_pairs={{0,16},{16,0},{1,17},{17,1},{2,18},{18,2},{3,19},{19,3},{4,20},{20... | collective-permute-start | bytes 2654216 | tf_op jit(solution)/shard_map/ppermute | solution.py:1010
  65.9 4.9 %collective-permute-start.3 = (bf16[2,288,768]{2,1,0:T(8,128)(2,1)S(1)}, bf16[2,288,768]{2,1,0:T(8,128)(2,1)S(1)}, u32[]{:S(2)}, u32[]{:S(2)}) collective-permute-start(bf16[2,288,768]{2,1,0:T(8,128)(2,1)S(1)} %get-tuple-element.98), channel_id=1, source_target_pairs={{0,16},{16,0},{1,17},{17,1},{2,18},{18,2},{3,19},{19,3},{4,20},{20... | collective-permute-start | bytes 2654216 | tf_op jit(solution)/shard_map/ppermute | solution.py:1015
  95.0 5.3 %collective-permute-start.4 = (bf16[2,288,768]{2,1,0:T(8,128)(2,1)S(1)}, bf16[2,288,768]{2,1,0:T(8,128)(2,1)S(1)}, u32[]{:S(2)}, u32[]{:S(2)}) collective-permute-start(bf16[2,288,768]{2,1,0:T(8,128)(2,1)S(1)} %get-tuple-element.124), channel_id=1, source_target_pairs={{0,16},{16,0},{1,17},{17,1},{2,18},{18,2},{3,19},{19,3},{4,20},{20... | collective-permute-start | bytes 2654216 | tf_op jit(solution)/shard_map/ppermute | solution.py:1019
  103.5 1.4 %collective-permute-start.5 = (f32[32,768]{1,0:T(8,128)S(1)}, f32[32,768]{1,0:T(8,128)S(1)}, u32[]{:S(2)}, u32[]{:S(2)}) collective-permute-start(f32[32,768]{1,0:T(8,128)S(1)} %get-tuple-element.128), channel_id=1, source_target_pairs={{0,16},{16,0},{1,17},{17,1},{2,18},{18,2},{3,19},{19,3},{4,20},{20... | collective-permute-start | bytes 294920 | tf_op jit(solution)/shard_map/ppermute | solution.py:956
  104.9 8.8 %collective-permute-start.6 = (bf16[32,768]{1,0:T(8,128)(2,1)S(1)}, bf16[32,768]{1,0:T(8,128)(2,1)S(1)}, u32[]{:S(2)}, u32[]{:S(2)}) collective-permute-start(bf16[32,768]{1,0:T(8,128)(2,1)S(1)} %get-tuple-element.152), channel_id=1, source_target_pairs={{0,1},{1,0},{2,3},{3,2},{4,5},{5,4},{6,7},{7,6},{8,9},{9,8},{10,11... | collective-permute-start | bytes 147464 | tf_op jit(solution)/shard_map/ppermute | solution.py:961
  107.6 6.0 %collective-permute-start.7 = (bf16[32,768]{1,0:T(8,128)(2,1)S(1)}, bf16[32,768]{1,0:T(8,128)(2,1)S(1)}, u32[]{:S(2)}, u32[]{:S(2)}) collective-permute-start(bf16[32,768]{1,0:T(8,128)(2,1)S(1)} %get-tuple-element.152), channel_id=1, source_target_pairs={{0,2},{1,3},{2,0},{3,1},{4,6},{5,7},{6,4},{7,5},{8,10},{9,11},{10,... | collective-permute-start | bytes 147464 | tf_op jit(solution)/shard_map/ppermute | solution.py:961
  109.1 5.0 %collective-permute-start.8 = (bf16[32,768]{1,0:T(8,128)(2,1)S(1)}, bf16[32,768]{1,0:T(8,128)(2,1)S(1)}, u32[]{:S(2)}, u32[]{:S(2)}) collective-permute-start(bf16[32,768]{1,0:T(8,128)(2,1)S(1)} %get-tuple-element.152), channel_id=1, source_target_pairs={{0,3},{1,2},{2,1},{3,0},{4,7},{5,6},{6,5},{7,4},{8,11},{9,10},{10,... | collective-permute-start | bytes 147464 | tf_op jit(solution)/shard_map/ppermute | solution.py:961
  109.1 13.8 %copy-start.2 = (s32[2,2,2]{2,1,0:T(2,128)S(1)}, s32[2,2,2]{2,1,0:T(2,128)}, u32[]{:S(2)}) copy-start(s32[2,2,2]{2,1,0:T(2,128)} %param.21) | copy-start | bytes 100
  114.1 6.5 %collective-permute-start.11 = (bf16[32,768]{1,0:T(8,128)(2,1)S(1)}, bf16[32,768]{1,0:T(8,128)(2,1)S(1)}, u32[]{:S(2)}, u32[]{:S(2)}) collective-permute-start(bf16[32,768]{1,0:T(8,128)(2,1)S(1)} %fusion), channel_id=1, source_target_pairs={{0,12},{1,13},{2,14},{3,15},{4,8},{5,9},{6,10},{7,11},{8,4},{9,5},... | collective-permute-start | bytes 147464 | tf_op jit(solution)/shard_map/ppermute | solution.py:961
  117.8 5.0 %collective-permute-start.10 = (bf16[32,768]{1,0:T(8,128)(2,1)S(1)}, bf16[32,768]{1,0:T(8,128)(2,1)S(1)}, u32[]{:S(2)}, u32[]{:S(2)}) collective-permute-start(bf16[32,768]{1,0:T(8,128)(2,1)S(1)} %fusion), channel_id=1, source_target_pairs={{0,8},{1,9},{2,10},{3,11},{4,12},{5,13},{6,14},{7,15},{8,0},{9,1},... | collective-permute-start | bytes 147464 | tf_op jit(solution)/shard_map/ppermute | solution.py:961
  117.8 5.0 %collective-permute-start.9 = (bf16[32,768]{1,0:T(8,128)(2,1)S(1)}, bf16[32,768]{1,0:T(8,128)(2,1)S(1)}, u32[]{:S(2)}, u32[]{:S(2)}) collective-permute-start(bf16[32,768]{1,0:T(8,128)(2,1)S(1)} %fusion), channel_id=1, source_target_pairs={{0,4},{1,5},{2,6},{3,7},{4,0},{5,1},{6,2},{7,3},{8,12},{9,13},{10,... | collective-permute-start | bytes 147464 | tf_op jit(solution)/shard_map/ppermute | solution.py:961
  122.9 1.4 %collective-permute-start.12 = (f32[32,768]{1,0:T(8,128)S(1)}, f32[32,768]{1,0:T(8,128)S(1)}, u32[]{:S(2)}, u32[]{:S(2)}) collective-permute-start(f32[32,768]{1,0:T(8,128)S(1)} %add_add_fusion.mine_ref), channel_id=1, source_target_pairs={{0,16},{16,0},{1,17},{17,1},{2,18},{18,2},{3,19},{19,3},{4,20},{20... | collective-permute-start | bytes 294920 | tf_op jit(solution)/shard_map/ppermute | solution.py:970

commit v6 on v5

--- a/solution.py
+++ b/solution.py
@@ -429,19 +429,16 @@
         datt_ref[rows, :] = dot_nt(gate_ref[rows, :], wu_ref[...])
 
     def first(s):
-        rows = rows_at(s * length, length, length)
+        rows = slice(s * length, (s + 1) * length)
         att = norm_backward(datt_ref[rows, :] + two_ref[rows, :], n1_ref[rows, :].astype(F32),
                             r1_ref[rows, 0:1], vec[4:5])
         datt_ref[rows, :] = att
-        low_ref[rows, :] = att.astype(BF16)
-
-    def mixture(i):
-        rows = rows_at(i * tall, tall, 128)
-        low_ref[rows, :] = dot_nt(low_ref[rows, :], wo_ref[...]).astype(BF16)
+        att = att.astype(BF16)
+        yield True
+        low_ref[rows, :] = dot_nt(att, wo_ref[...]).astype(BF16)
 
     loop(2, up)
-    loop(sequences, first)
-    loop(2, mixture)
+    pipelined(first(s) for s in range(sequences))
 
 
 def near_backward(near, sequences, length, q_ref, nk_ref, nv_ref, dmix_ref, mix_ref,

time: 126 us -> 124 us (0.984)
  Pallas kernels: 107 us -> 105 us
    pallas_call x11, Pallas kernels: 107 us -> 105 us  [call(): pl.pallas_call(kernel, name=name, out_shape=tuple((space(shape, dtype) fo...]
where the time goes in v6:
time: 124 us
  Pallas kernels  105 us (85%)
  starting transfers between devices  10.7 us (9%)
  waiting for transfers between devices  7.12 us (6%)
    pallas_call x11, Pallas kernels, call(): pl.pallas_call(kernel, name=name, out_shape=tuple((space(shape, dtype) fo...  105 us
    ppermute x6, starting transfers between devices, sum_while(): lax.ppermute(given, 'batch', [(i, i ^ step * d) for i in range(batch)])  8.71 us
    ppermute x6, waiting for transfers between devices, sum_while(): lax.ppermute(given, 'batch', [(i, i ^ step * d) for i in range(batch)])  4.69 us
  transfers between devices with their start and end apart: 13, of which 5 were waited for; matrix products, arithmetic and copies ran while one was open for 0% of the time, Pallas kernels for 15%

profile of v6, /device:TPU:0, one launch (start us, length us, event | category | flops | bytes accessed | tf_op | source)
XLA Modules:
  0.0 124.1 jit_solution(2677949981037343593)
XLA Ops:
  0.7 6.5 %project_in.1 = (bf16[768,768]{1,0:T(8,128)(2,1)S(1)}, bf16[768,768]{1,0:T(8,128)(2,1)S(1)}, bf16[768,768]{1,0:T(8,128)(2,1)S(1)}, bf16[2,288,768]{2,1,0:T(8,128)(2,1)S(1)}, bf16[768,16]{1,0:T(8,128)(2,1)}) custom-call(bf16[768,768]{1,0:T(8,128)(2,1)} %bitcast.19, bf16[2,768,2304]{2,1,0:T(8,128)(2,1)} %w_hbm.7, f32[2,2,8,768]{3,2,1,0:T(8,128)} %rest_0_.1, ...), custom_call_target="tpu_custom_call" | custom-call | flops 2717908992 | bytes 12000000 | tf_op jit(solution)/shard_map/project_in/pallas_call | solution.py:524
  7.2 0.5 collective-permute-start.1
  7.8 2.5 %attention_far.2.far_ref = bf16[384,768]{1,0:T(8,128)(2,1)S(1)} custom-call(bf16[768,768]{1,0:T(8,128)(2,1)S(1)} %get-tuple-element.80.q_ref, bf16[768,768]{1,0:T(8,128)(2,1)S(1)} %get-tuple-element.81.k_ref, bf16[768,768]{1,0:T(8,128)(2,1)S(1)} %get-tuple-element.82.v_ref, s32[3,256]{1,0:T(4,128)S(1)} %copy-done, s32[1,3]{1,0:T(1,128)S(1)} %bitcast.11), custom_call_target="tpu_custom_call" | custom-call | flops 2000000000 | bytes 6000000 | tf_op jit(solution)/shard_map/attention_far/pallas_call | solution.py:524
  10.4 19.5 %middle.1 = (bf16[768,768]{1,0:T(8,128)(2,1)S(1)}, bf16[768,768]{1,0:T(8,128)(2,1)S(1)}, bf16[768,768]{1,0:T(8,128)(2,1)S(1)}, bf16[2,288,768]{2,1,0:T(8,128)(2,...) custom-call(s32[3,256]{1,0:T(4,128)S(1)} %copy-done, ...), custom_call_target="tpu_custom_call" | custom-call | flops 10871635968 | bytes 24000000 | tf_op jit(solution)/shard_map/middle/pallas_call | solution.py:524
  29.8 0.5 collective-permute-start.2
  30.3 2.6 %attention_far.3.far_ref = bf16[384,768]{1,0:T(8,128)(2,1)S(1)} custom-call(bf16[768,768]{1,0:T(8,128)(2,1)S(1)} %get-tuple-element.84.q_ref, bf16[768,768]{1,0:T(8,128)(2,1)S(1)} %get-tuple-element.85.k_ref, bf16[768,768]{1,0:T(8,128)(2,1)S(1)} %get-tuple-element.86.v_ref, s32[3,256]{1,0:T(4,128)S(1)} %copy-done, s32[1,3]{1,0:T(1,128)S(1)} %bitcast.13), custom_call_target="tpu_custom_call" | custom-call | flops 2000000000 | bytes 6000000 | tf_op jit(solution)/shard_map/attention_far/pallas_call | solution.py:524
  32.9 32.1 %turn.1 = (f32[768,768]{1,0:T(8,128)S(1)}, bf16[384,768]{1,0:T(8,128)(2,1)S(1)}, bf16[384,768]{1,0:T(8,128)(2,1)S(1)}, f32[1056,768]{1,0:T(8,128)S(1)}, f32[1056...) custom-call(s32[3,256]{1,0:T(4,128)S(1)} %copy-done, ...), custom_call_target="tpu_custom_call" | custom-call | flops 16307453952 | bytes 24000000 | tf_op jit(solution)/shard_map/turn/pallas_call | solution.py:524
  65.1 0.1 collective-permute-start.3
  65.2 4.8 %back_far.2 = (bf16[768,768]{1,0:T(8,128)(2,1)S(1)}, f32[768,768]{1,0:T(8,128)S(1)}, f32[768,768]{1,0:T(8,128)S(1)}) custom-call(s32[3,256]{1,0:T(4,128)S(1)} %copy-done, s32[1,3]{1,0:T(1,128)S(1)} %bitcast.15, bf16[768,768]{1,0:T(8,128)(2,1)S(1)} %get-tuple-element.84.q_ref, bf16[768,768]{1,0:T(8,128)(2,1)S(1)} %get-tuple-element.85.k_ref, ...), custom_call_target="tpu_custom_call" | custom-call | flops 4000000000 | bytes 16000000 | tf_op jit(solution)/shard_map/back_far/pallas_call | solution.py:524
  70.0 23.6 %back.1 = (f32[768,768]{1,0:T(8,128)S(1)}, bf16[384,768]{1,0:T(8,128)(2,1)S(1)}, bf16[384,768]{1,0:T(8,128)(2,1)S(1)}, f32[1056,768]{1,0:T(8,128)S(1)}, f32[1056...) custom-call(s32[3,256]{1,0:T(4,128)S(1)} %copy-done, ...), custom_call_target="tpu_custom_call" | custom-call | flops 10871635968 | bytes 24000000 | tf_op jit(solution)/shard_map/back/pallas_call | solution.py:524
  93.6 0.5 collective-permute-start.4
  94.1 4.8 %back_far.3 = (bf16[768,768]{1,0:T(8,128)(2,1)S(1)}, f32[768,768]{1,0:T(8,128)S(1)}, f32[768,768]{1,0:T(8,128)S(1)}) custom-call(s32[3,256]{1,0:T(4,128)S(1)} %copy-done, s32[1,3]{1,0:T(1,128)S(1)} %bitcast.17, bf16[768,768]{1,0:T(8,128)(2,1)S(1)} %get-tuple-element.113.q_ref, bf16[768,768]{1,0:T(8,128)(2,1)S(1)} %get-tuple-element.114.k_ref, ...), custom_call_target="tpu_custom_call" | custom-call | flops 4000000000 | bytes 16000000 | tf_op jit(solution)/shard_map/back_far/pallas_call | solution.py:524
  98.9 3.2 %adapter_back.1 = (bf16[768,768]{1,0:T(8,128)(2,1)S(1)}, bf16[768,768]{1,0:T(8,128)(2,1)S(1)}, bf16[768,16]{1,0:T(8,128)(2,1)S(1)}, bf16[768,2304]{1,0:T(8,128)(...) custom-call(bf16[768,768]{1,0:T(8,128)(2,1)S(1)} %get-tuple-element., ...), custom_call_target="tpu_custom_call" | custom-call | flops 500000000 | bytes 12000000 | tf_op jit(solution)/shard_map/adapter_back/pallas_call | solution.py:524
  102.2 1.2 collective-permute-done.5
  103.5 2.7 %collective-permute-start.6 = (bf16[32,768]{1,0:T(8,128)(2,1)S(1)}, bf16[32,768]{1,0:T(8,128)(2,1)S(1)}, u32[]{:S(2)}, u32[]{:S(2)}) collective-permute-start(bf16[32,768]{1,0:T(8,128)(2,1)S(1)} %get-tuple-element.152), channel_id=1, source_target_pairs={{0,1},{1,0},{2,3},{3,2},{4,5},{5,4},{6,7},{7,6},{8,9},{9,8},{10,11... | collective-permute-start | bytes 147464 | tf_op jit(solution)/shard_map/ppermute | solution.py:958
  106.2 1.5 %collective-permute-start.7 = (bf16[32,768]{1,0:T(8,128)(2,1)S(1)}, bf16[32,768]{1,0:T(8,128)(2,1)S(1)}, u32[]{:S(2)}, u32[]{:S(2)}) collective-permute-start(bf16[32,768]{1,0:T(8,128)(2,1)S(1)} %get-tuple-element.152), channel_id=1, source_target_pairs={{0,2},{1,3},{2,0},{3,1},{4,6},{5,7},{6,4},{7,5},{8,10},{9,11},{10,... | collective-permute-start | bytes 147464 | tf_op jit(solution)/shard_map/ppermute | solution.py:958
  107.7 4.5 %project_back.1 = f32[768,768]{1,0:T(8,128)} custom-call(f32[768,768]{1,0:T(8,128)S(1)} %get-tuple-element.130.datt_ref, bf16[768,768]{1,0:T(8,128)(2,1)S(1)} %get-tuple-element.121.dq_ref, bf16[768,768]{1,0:T(8,128)(2,1)S(1)} %get-tuple-element.131.dk_ref, bf16[768,768]{1,0:T(8,128)(2,1)S(1)} %get-tuple-element.132.dv_ref, ...), custom_call_target="tpu_custom_call" | custom-call | flops 2717908992 | bytes 4000000 | tf_op jit(solution)/shard_map/project_back/pallas_call | solution.py:524
  112.2 0.4 collective-permute-done.8
  112.7 3.7 %collective-permute-start.11 = (bf16[32,768]{1,0:T(8,128)(2,1)S(1)}, bf16[32,768]{1,0:T(8,128)(2,1)S(1)}, u32[]{:S(2)}, u32[]{:S(2)}) collective-permute-start(bf16[32,768]{1,0:T(8,128)(2,1)S(1)} %fusion), channel_id=1, source_target_pairs={{0,12},{1,13},{2,14},{3,15},{4,8},{5,9},{6,10},{7,11},{8,4},{9,5},... | collective-permute-start | bytes 147464 | tf_op jit(solution)/shard_map/ppermute | solution.py:958
  116.4 0.7 collective-permute-start.9
  117.1 2.1 %collective-permute-done.11 = bf16[32,768]{1,0:T(8,128)(2,1)S(1)} collective-permute-done((bf16[32,768]{1,0:T(8,128)(2,1)S(1)}, bf16[32,768]{1,0:T(8,128)(2,1)S(1)}, u32[]{:S(2)}, u32[]{:S(2)}) %collective-permute-start.11) | collective-permute-done | bytes 49184 | tf_op jit(solution)/shard_map/ppermute | solution.py:958
  119.2 2.2 %collective-permute-done.10 = bf16[32,768]{1,0:T(8,128)(2,1)S(1)} collective-permute-done((bf16[32,768]{1,0:T(8,128)(2,1)S(1)}, bf16[32,768]{1,0:T(8,128)(2,1)S(1)}, u32[]{:S(2)}, u32[]{:S(2)}) %collective-permute-start.10) | collective-permute-done | bytes 49184 | tf_op jit(solution)/shard_map/ppermute | solution.py:958
  121.6 1.2 collective-permute-done.12.theirs_ref
  122.8 1.1 adam.1
  (23 shorter events, 0.6 us)
Async XLA Ops:
  0.6 7.1 %copy-start = (s32[3,256]{1,0:T(4,128)S(1)}, s32[3,256]{1,0:T(4,128)}, u32[]{:S(2)}) copy-start(s32[3,256]{1,0:T(4,128)} %own_ref.13) | copy-start | bytes 9220
  0.6 7.2 %copy-start.1 = (s32[3]{0:T(128)S(1)}, s32[3]{0:T(128)}, u32[]{:S(2)}) copy-start(s32[3]{0:T(128)} %param.20) | copy-start | bytes 40
  7.2 3.2 %collective-permute-start.1 = (bf16[2,288,768]{2,1,0:T(8,128)(2,1)S(1)}, bf16[2,288,768]{2,1,0:T(8,128)(2,1)S(1)}, u32[]{:S(2)}, u32[]{:S(2)}) collective-permute-start(bf16[2,288,768]{2,1,0:T(8,128)(2,1)S(1)} %get-tuple-element.83), channel_id=1, source_target_pairs={{0,16},{16,0},{1,17},{17,1},{2,18},{18,2},{3,19},{19,3},{4,20},{20... | collective-permute-start | bytes 2654216 | tf_op jit(solution)/shard_map/ppermute | solution.py:1003
  7.7 2.6 %collective-permute-start = (s32[3,256]{1,0:T(4,128)S(1)}, s32[3,256]{1,0:T(4,128)S(1)}, u32[]{:S(2)}, u32[]{:S(2)}) collective-permute-start(s32[3,256]{1,0:T(4,128)S(1)} %copy-done), channel_id=1, source_target_pairs={{0,16},{16,0},{1,17},{17,1},{2,18},{18,2},{3,19},{19,3},{4,20},{20... | collective-permute-start | bytes 9224 | tf_op jit(solution)/shard_map/ppermute | solution.py:997
  29.8 3.1 %collective-permute-start.2 = (bf16[2,288,768]{2,1,0:T(8,128)(2,1)S(1)}, bf16[2,288,768]{2,1,0:T(8,128)(2,1)S(1)}, u32[]{:S(2)}, u32[]{:S(2)}) collective-permute-start(bf16[2,288,768]{2,1,0:T(8,128)(2,1)S(1)} %get-tuple-element.87), channel_id=1, source_target_pairs={{0,16},{16,0},{1,17},{17,1},{2,18},{18,2},{3,19},{19,3},{4,20},{20... | collective-permute-start | bytes 2654216 | tf_op jit(solution)/shard_map/ppermute | solution.py:1007
  65.1 4.9 %collective-permute-start.3 = (bf16[2,288,768]{2,1,0:T(8,128)(2,1)S(1)}, bf16[2,288,768]{2,1,0:T(8,128)(2,1)S(1)}, u32[]{:S(2)}, u32[]{:S(2)}) collective-permute-start(bf16[2,288,768]{2,1,0:T(8,128)(2,1)S(1)} %get-tuple-element.98), channel_id=1, source_target_pairs={{0,16},{16,0},{1,17},{17,1},{2,18},{18,2},{3,19},{19,3},{4,20},{20... | collective-permute-start | bytes 2654216 | tf_op jit(solution)/shard_map/ppermute | solution.py:1012
  93.6 5.3 %collective-permute-start.4 = (bf16[2,288,768]{2,1,0:T(8,128)(2,1)S(1)}, bf16[2,288,768]{2,1,0:T(8,128)(2,1)S(1)}, u32[]{:S(2)}, u32[]{:S(2)}) collective-permute-start(bf16[2,288,768]{2,1,0:T(8,128)(2,1)S(1)} %get-tuple-element.124), channel_id=1, source_target_pairs={{0,16},{16,0},{1,17},{17,1},{2,18},{18,2},{3,19},{19,3},{4,20},{20... | collective-permute-start | bytes 2654216 | tf_op jit(solution)/shard_map/ppermute | solution.py:1016
  102.1 1.4 %collective-permute-start.5 = (f32[32,768]{1,0:T(8,128)S(1)}, f32[32,768]{1,0:T(8,128)S(1)}, u32[]{:S(2)}, u32[]{:S(2)}) collective-permute-start(f32[32,768]{1,0:T(8,128)S(1)} %get-tuple-element.128), channel_id=1, source_target_pairs={{0,16},{16,0},{1,17},{17,1},{2,18},{18,2},{3,19},{19,3},{4,20},{20... | collective-permute-start | bytes 294920 | tf_op jit(solution)/shard_map/ppermute | solution.py:953
  103.5 8.8 %collective-permute-start.6 = (bf16[32,768]{1,0:T(8,128)(2,1)S(1)}, bf16[32,768]{1,0:T(8,128)(2,1)S(1)}, u32[]{:S(2)}, u32[]{:S(2)}) collective-permute-start(bf16[32,768]{1,0:T(8,128)(2,1)S(1)} %get-tuple-element.152), channel_id=1, source_target_pairs={{0,1},{1,0},{2,3},{3,2},{4,5},{5,4},{6,7},{7,6},{8,9},{9,8},{10,11... | collective-permute-start | bytes 147464 | tf_op jit(solution)/shard_map/ppermute | solution.py:958
  106.2 6.0 %collective-permute-start.7 = (bf16[32,768]{1,0:T(8,128)(2,1)S(1)}, bf16[32,768]{1,0:T(8,128)(2,1)S(1)}, u32[]{:S(2)}, u32[]{:S(2)}) collective-permute-start(bf16[32,768]{1,0:T(8,128)(2,1)S(1)} %get-tuple-element.152), channel_id=1, source_target_pairs={{0,2},{1,3},{2,0},{3,1},{4,6},{5,7},{6,4},{7,5},{8,10},{9,11},{10,... | collective-permute-start | bytes 147464 | tf_op jit(solution)/shard_map/ppermute | solution.py:958
  107.7 5.0 %collective-permute-start.8 = (bf16[32,768]{1,0:T(8,128)(2,1)S(1)}, bf16[32,768]{1,0:T(8,128)(2,1)S(1)}, u32[]{:S(2)}, u32[]{:S(2)}) collective-permute-start(bf16[32,768]{1,0:T(8,128)(2,1)S(1)} %get-tuple-element.152), channel_id=1, source_target_pairs={{0,3},{1,2},{2,1},{3,0},{4,7},{5,6},{6,5},{7,4},{8,11},{9,10},{10,... | collective-permute-start | bytes 147464 | tf_op jit(solution)/shard_map/ppermute | solution.py:958
  107.7 13.8 %copy-start.2 = (s32[2,2,2]{2,1,0:T(2,128)S(1)}, s32[2,2,2]{2,1,0:T(2,128)}, u32[]{:S(2)}) copy-start(s32[2,2,2]{2,1,0:T(2,128)} %param.21) | copy-start | bytes 100
  112.7 6.5 %collective-permute-start.11 = (bf16[32,768]{1,0:T(8,128)(2,1)S(1)}, bf16[32,768]{1,0:T(8,128)(2,1)S(1)}, u32[]{:S(2)}, u32[]{:S(2)}) collective-permute-start(bf16[32,768]{1,0:T(8,128)(2,1)S(1)} %fusion), channel_id=1, source_target_pairs={{0,12},{1,13},{2,14},{3,15},{4,8},{5,9},{6,10},{7,11},{8,4},{9,5},... | collective-permute-start | bytes 147464 | tf_op jit(solution)/shard_map/ppermute | solution.py:958
  116.4 5.0 %collective-permute-start.10 = (bf16[32,768]{1,0:T(8,128)(2,1)S(1)}, bf16[32,768]{1,0:T(8,128)(2,1)S(1)}, u32[]{:S(2)}, u32[]{:S(2)}) collective-permute-start(bf16[32,768]{1,0:T(8,128)(2,1)S(1)} %fusion), channel_id=1, source_target_pairs={{0,8},{1,9},{2,10},{3,11},{4,12},{5,13},{6,14},{7,15},{8,0},{9,1},... | collective-permute-start | bytes 147464 | tf_op jit(solution)/shard_map/ppermute | solution.py:958
  116.4 5.0 %collective-permute-start.9 = (bf16[32,768]{1,0:T(8,128)(2,1)S(1)}, bf16[32,768]{1,0:T(8,128)(2,1)S(1)}, u32[]{:S(2)}, u32[]{:S(2)}) collective-permute-start(bf16[32,768]{1,0:T(8,128)(2,1)S(1)} %fusion), channel_id=1, source_target_pairs={{0,4},{1,5},{2,6},{3,7},{4,0},{5,1},{6,2},{7,3},{8,12},{9,13},{10,... | collective-permute-start | bytes 147464 | tf_op jit(solution)/shard_map/ppermute | solution.py:958
  121.5 1.4 %collective-permute-start.12 = (f32[32,768]{1,0:T(8,128)S(1)}, f32[32,768]{1,0:T(8,128)S(1)}, u32[]{:S(2)}, u32[]{:S(2)}) collective-permute-start(f32[32,768]{1,0:T(8,128)S(1)} %add_add_fusion.mine_ref), channel_id=1, source_target_pairs={{0,16},{16,0},{1,17},{17,1},{2,18},{18,2},{3,19},{19,3},{4,20},{20... | collective-permute-start | bytes 294920 | tf_op jit(solution)/shard_map/ppermute | solution.py:967

commit v7 on v6

--- a/solution.py
+++ b/solution.py
@@ -957,7 +957,7 @@
         given = mine.astype(BF16)
         come = [lax.ppermute(given, "batch", [(i, i ^ (step * d)) for i in range(batch)])
                 for d in range(1, ways)]
-        if work:
+        if work and step * ways >= batch:
             done = work.pop(0)(mine, done)
             *come, done = together(*come, done)
         mine = mine + sum(item.astype(F32) for item in come)

time: 124 us -> 125 us (level)
  transfers between devices with their start and end apart: 13 -> 13, of which waited for: 5 -> 6; matrix products, arithmetic and copies ran while one was open for 0% -> 0% of each run, Pallas kernels for 15% -> 15%
where the time goes in v7:
time: 125 us
  Pallas kernels  105 us (84%)
  starting transfers between devices  10.7 us (9%)
  waiting for transfers between devices  7.55 us (6%)
    pallas_call x11, Pallas kernels, call(): pl.pallas_call(kernel, name=name, out_shape=tuple((space(shape, dtype) fo...  105 us
    ppermute x6, starting transfers between devices, sum_while(): lax.ppermute(given, 'batch', [(i, i ^ step * d) for i in range(batch)])  8.74 us
    ppermute x6, waiting for transfers between devices, sum_while(): lax.ppermute(given, 'batch', [(i, i ^ step * d) for i in range(batch)])  5.12 us
  transfers between devices with their start and end apart: 13, of which 6 were waited for; matrix products, arithmetic and copies ran while one was open for 0% of the time, Pallas kernels for 15%

profile of v7, /device:TPU:0, one launch (start us, length us, event | category | flops | bytes accessed | tf_op | source)
XLA Modules:
  0.0 124.5 jit_solution(12363957311544903767)
XLA Ops:
  0.7 6.5 %project_in.1 = (bf16[768,768]{1,0:T(8,128)(2,1)S(1)}, bf16[768,768]{1,0:T(8,128)(2,1)S(1)}, bf16[768,768]{1,0:T(8,128)(2,1)S(1)}, bf16[2,288,768]{2,1,0:T(8,128)(2,1)S(1)}, bf16[768,16]{1,0:T(8,128)(2,1)}) custom-call(bf16[768,768]{1,0:T(8,128)(2,1)} %bitcast.19, bf16[2,768,2304]{2,1,0:T(8,128)(2,1)} %w_hbm.7, f32[2,2,8,768]{3,2,1,0:T(8,128)} %rest_0_.1, ...), custom_call_target="tpu_custom_call" | custom-call | flops 2717908992 | bytes 12000000 | tf_op jit(solution)/shard_map/project_in/pallas_call | solution.py:524
  7.2 0.5 collective-permute-start.1
  7.8 2.5 %attention_far.2.far_ref = bf16[384,768]{1,0:T(8,128)(2,1)S(1)} custom-call(bf16[768,768]{1,0:T(8,128)(2,1)S(1)} %get-tuple-element.80.q_ref, bf16[768,768]{1,0:T(8,128)(2,1)S(1)} %get-tuple-element.81.k_ref, bf16[768,768]{1,0:T(8,128)(2,1)S(1)} %get-tuple-element.82.v_ref, s32[3,256]{1,0:T(4,128)S(1)} %copy-done, s32[1,3]{1,0:T(1,128)S(1)} %bitcast.11), custom_call_target="tpu_custom_call" | custom-call | flops 2000000000 | bytes 6000000 | tf_op jit(solution)/shard_map/attention_far/pallas_call | solution.py:524
  10.4 19.5 %middle.1 = (bf16[768,768]{1,0:T(8,128)(2,1)S(1)}, bf16[768,768]{1,0:T(8,128)(2,1)S(1)}, bf16[768,768]{1,0:T(8,128)(2,1)S(1)}, bf16[2,288,768]{2,1,0:T(8,128)(2,...) custom-call(s32[3,256]{1,0:T(4,128)S(1)} %copy-done, ...), custom_call_target="tpu_custom_call" | custom-call | flops 10871635968 | bytes 24000000 | tf_op jit(solution)/shard_map/middle/pallas_call | solution.py:524
  29.8 0.5 collective-permute-start.2
  30.3 2.6 %attention_far.3.far_ref = bf16[384,768]{1,0:T(8,128)(2,1)S(1)} custom-call(bf16[768,768]{1,0:T(8,128)(2,1)S(1)} %get-tuple-element.84.q_ref, bf16[768,768]{1,0:T(8,128)(2,1)S(1)} %get-tuple-element.85.k_ref, bf16[768,768]{1,0:T(8,128)(2,1)S(1)} %get-tuple-element.86.v_ref, s32[3,256]{1,0:T(4,128)S(1)} %copy-done, s32[1,3]{1,0:T(1,128)S(1)} %bitcast.13), custom_call_target="tpu_custom_call" | custom-call | flops 2000000000 | bytes 6000000 | tf_op jit(solution)/shard_map/attention_far/pallas_call | solution.py:524
  32.9 32.1 %turn.1 = (f32[768,768]{1,0:T(8,128)S(1)}, bf16[384,768]{1,0:T(8,128)(2,1)S(1)}, bf16[384,768]{1,0:T(8,128)(2,1)S(1)}, f32[1056,768]{1,0:T(8,128)S(1)}, f32[1056...) custom-call(s32[3,256]{1,0:T(4,128)S(1)} %copy-done, ...), custom_call_target="tpu_custom_call" | custom-call | flops 16307453952 | bytes 24000000 | tf_op jit(solution)/shard_map/turn/pallas_call | solution.py:524
  65.2 4.8 %back_far.2 = (bf16[768,768]{1,0:T(8,128)(2,1)S(1)}, f32[768,768]{1,0:T(8,128)S(1)}, f32[768,768]{1,0:T(8,128)S(1)}) custom-call(s32[3,256]{1,0:T(4,128)S(1)} %copy-done, s32[1,3]{1,0:T(1,128)S(1)} %bitcast.15, bf16[768,768]{1,0:T(8,128)(2,1)S(1)} %get-tuple-element.84.q_ref, bf16[768,768]{1,0:T(8,128)(2,1)S(1)} %get-tuple-element.85.k_ref, ...), custom_call_target="tpu_custom_call" | custom-call | flops 4000000000 | bytes 16000000 | tf_op jit(solution)/shard_map/back_far/pallas_call | solution.py:524
  70.0 23.6 %back.1 = (f32[768,768]{1,0:T(8,128)S(1)}, bf16[384,768]{1,0:T(8,128)(2,1)S(1)}, bf16[384,768]{1,0:T(8,128)(2,1)S(1)}, f32[1056,768]{1,0:T(8,128)S(1)}, f32[1056...) custom-call(s32[3,256]{1,0:T(4,128)S(1)} %copy-done, ...), custom_call_target="tpu_custom_call" | custom-call | flops 10871635968 | bytes 24000000 | tf_op jit(solution)/shard_map/back/pallas_call | solution.py:524
  93.6 0.5 collective-permute-start.4
  94.1 4.8 %back_far.3 = (bf16[768,768]{1,0:T(8,128)(2,1)S(1)}, f32[768,768]{1,0:T(8,128)S(1)}, f32[768,768]{1,0:T(8,128)S(1)}) custom-call(s32[3,256]{1,0:T(4,128)S(1)} %copy-done, s32[1,3]{1,0:T(1,128)S(1)} %bitcast.17, bf16[768,768]{1,0:T(8,128)(2,1)S(1)} %get-tuple-element.113.q_ref, bf16[768,768]{1,0:T(8,128)(2,1)S(1)} %get-tuple-element.114.k_ref, ...), custom_call_target="tpu_custom_call" | custom-call | flops 4000000000 | bytes 16000000 | tf_op jit(solution)/shard_map/back_far/pallas_call | solution.py:524
  98.9 3.2 %adapter_back.1 = (bf16[768,768]{1,0:T(8,128)(2,1)S(1)}, bf16[768,768]{1,0:T(8,128)(2,1)S(1)}, bf16[768,16]{1,0:T(8,128)(2,1)S(1)}, bf16[768,2304]{1,0:T(8,128)(...) custom-call(bf16[768,768]{1,0:T(8,128)(2,1)S(1)} %get-tuple-element., ...), custom_call_target="tpu_custom_call" | custom-call | flops 500000000 | bytes 12000000 | tf_op jit(solution)/shard_map/adapter_back/pallas_call | solution.py:524
  102.2 1.2 collective-permute-done.5
  103.5 3.6 %collective-permute-start.8 = (bf16[32,768]{1,0:T(8,128)(2,1)S(1)}, bf16[32,768]{1,0:T(8,128)(2,1)S(1)}, u32[]{:S(2)}, u32[]{:S(2)}) collective-permute-start(bf16[32,768]{1,0:T(8,128)(2,1)S(1)} %get-tuple-element.154), channel_id=1, source_target_pairs={{0,3},{1,2},{2,1},{3,0},{4,7},{5,6},{6,5},{7,4},{8,11},{9,10},{10,... | collective-permute-start | bytes 147464 | tf_op jit(solution)/shard_map/ppermute | solution.py:958
  107.1 0.5 collective-permute-start.7
  107.8 1.6 %collective-permute-done.8 = bf16[32,768]{1,0:T(8,128)(2,1)S(1)} collective-permute-done((bf16[32,768]{1,0:T(8,128)(2,1)S(1)}, bf16[32,768]{1,0:T(8,128)(2,1)S(1)}, u32[]{:S(2)}, u32[]{:S(2)}) %collective-permute-start.8) | collective-permute-done | bytes 49184 | tf_op jit(solution)/shard_map/ppermute | solution.py:958
  109.4 1.8 %collective-permute-done.7 = bf16[32,768]{1,0:T(8,128)(2,1)S(1)} collective-permute-done((bf16[32,768]{1,0:T(8,128)(2,1)S(1)}, bf16[32,768]{1,0:T(8,128)(2,1)S(1)}, u32[]{:S(2)}, u32[]{:S(2)}) %collective-permute-start.7) | collective-permute-done | bytes 49184 | tf_op jit(solution)/shard_map/ppermute | solution.py:958
  111.2 0.5 collective-permute-done.6
  111.8 1.6 %collective-permute-start.9 = (bf16[32,768]{1,0:T(8,128)(2,1)S(1)}, bf16[32,768]{1,0:T(8,128)(2,1)S(1)}, u32[]{:S(2)}, u32[]{:S(2)}) collective-permute-start(bf16[32,768]{1,0:T(8,128)(2,1)S(1)} %get-tuple-element.152), channel_id=1, source_target_pairs={{0,4},{1,5},{2,6},{3,7},{4,0},{5,1},{6,2},{7,3},{8,12},{9,13},{10,... | collective-permute-start | bytes 147464 | tf_op jit(solution)/shard_map/ppermute | solution.py:958
  113.4 2.6 %collective-permute-start.10 = (bf16[32,768]{1,0:T(8,128)(2,1)S(1)}, bf16[32,768]{1,0:T(8,128)(2,1)S(1)}, u32[]{:S(2)}, u32[]{:S(2)}) collective-permute-start(bf16[32,768]{1,0:T(8,128)(2,1)S(1)} %get-tuple-element.152), channel_id=1, source_target_pairs={{0,8},{1,9},{2,10},{3,11},{4,12},{5,13},{6,14},{7,15},{8,0},{9,1},... | collective-permute-start | bytes 147464 | tf_op jit(solution)/shard_map/ppermute | solution.py:958
  116.2 4.5 %project_back.1 = f32[768,768]{1,0:T(8,128)} custom-call(f32[768,768]{1,0:T(8,128)S(1)} %get-tuple-element.130.datt_ref, bf16[768,768]{1,0:T(8,128)(2,1)S(1)} %get-tuple-element.121.dq_ref, bf16[768,768]{1,0:T(8,128)(2,1)S(1)} %get-tuple-element.131.dk_ref, bf16[768,768]{1,0:T(8,128)(2,1)S(1)} %get-tuple-element.132.dv_ref, ...), custom_call_target="tpu_custom_call" | custom-call | flops 2717908992 | bytes 4000000 | tf_op jit(solution)/shard_map/project_back/pallas_call | solution.py:524
  120.7 1.1 collective-permute-done.11
  122.1 1.2 collective-permute-done.12.theirs_ref
  123.3 1.1 adam.1
  (23 shorter events, 1.0 us)
Async XLA Ops:
  0.6 7.1 %copy-start = (s32[3,256]{1,0:T(4,128)S(1)}, s32[3,256]{1,0:T(4,128)}, u32[]{:S(2)}) copy-start(s32[3,256]{1,0:T(4,128)} %own_ref.13) | copy-start | bytes 9220
  0.6 7.2 %copy-start.1 = (s32[3]{0:T(128)S(1)}, s32[3]{0:T(128)}, u32[]{:S(2)}) copy-start(s32[3]{0:T(128)} %param.20) | copy-start | bytes 40
  7.2 3.2 %collective-permute-start.1 = (bf16[2,288,768]{2,1,0:T(8,128)(2,1)S(1)}, bf16[2,288,768]{2,1,0:T(8,128)(2,1)S(1)}, u32[]{:S(2)}, u32[]{:S(2)}) collective-permute-start(bf16[2,288,768]{2,1,0:T(8,128)(2,1)S(1)} %get-tuple-element.83), channel_id=1, source_target_pairs={{0,16},{16,0},{1,17},{17,1},{2,18},{18,2},{3,19},{19,3},{4,20},{20... | collective-permute-start | bytes 2654216 | tf_op jit(solution)/shard_map/ppermute | solution.py:1003
  7.7 2.6 %collective-permute-start = (s32[3,256]{1,0:T(4,128)S(1)}, s32[3,256]{1,0:T(4,128)S(1)}, u32[]{:S(2)}, u32[]{:S(2)}) collective-permute-start(s32[3,256]{1,0:T(4,128)S(1)} %copy-done), channel_id=1, source_target_pairs={{0,16},{16,0},{1,17},{17,1},{2,18},{18,2},{3,19},{19,3},{4,20},{20... | collective-permute-start | bytes 9224 | tf_op jit(solution)/shard_map/ppermute | solution.py:997
  29.8 3.1 %collective-permute-start.2 = (bf16[2,288,768]{2,1,0:T(8,128)(2,1)S(1)}, bf16[2,288,768]{2,1,0:T(8,128)(2,1)S(1)}, u32[]{:S(2)}, u32[]{:S(2)}) collective-permute-start(bf16[2,288,768]{2,1,0:T(8,128)(2,1)S(1)} %get-tuple-element.87), channel_id=1, source_target_pairs={{0,16},{16,0},{1,17},{17,1},{2,18},{18,2},{3,19},{19,3},{4,20},{20... | collective-permute-start | bytes 2654216 | tf_op jit(solution)/shard_map/ppermute | solution.py:1007
  65.1 4.9 %collective-permute-start.3 = (bf16[2,288,768]{2,1,0:T(8,128)(2,1)S(1)}, bf16[2,288,768]{2,1,0:T(8,128)(2,1)S(1)}, u32[]{:S(2)}, u32[]{:S(2)}) collective-permute-start(bf16[2,288,768]{2,1,0:T(8,128)(2,1)S(1)} %get-tuple-element.98), channel_id=1, source_target_pairs={{0,16},{16,0},{1,17},{17,1},{2,18},{18,2},{3,19},{19,3},{4,20},{20... | collective-permute-start | bytes 2654216 | tf_op jit(solution)/shard_map/ppermute | solution.py:1012
  93.6 5.3 %collective-permute-start.4 = (bf16[2,288,768]{2,1,0:T(8,128)(2,1)S(1)}, bf16[2,288,768]{2,1,0:T(8,128)(2,1)S(1)}, u32[]{:S(2)}, u32[]{:S(2)}) collective-permute-start(bf16[2,288,768]{2,1,0:T(8,128)(2,1)S(1)} %get-tuple-element.124), channel_id=1, source_target_pairs={{0,16},{16,0},{1,17},{17,1},{2,18},{18,2},{3,19},{19,3},{4,20},{20... | collective-permute-start | bytes 2654216 | tf_op jit(solution)/shard_map/ppermute | solution.py:1016
  102.1 1.4 %collective-permute-start.5 = (f32[32,768]{1,0:T(8,128)S(1)}, f32[32,768]{1,0:T(8,128)S(1)}, u32[]{:S(2)}, u32[]{:S(2)}) collective-permute-start(f32[32,768]{1,0:T(8,128)S(1)} %get-tuple-element.128), channel_id=1, source_target_pairs={{0,16},{16,0},{1,17},{17,1},{2,18},{18,2},{3,19},{19,3},{4,20},{20... | collective-permute-start | bytes 294920 | tf_op jit(solution)/shard_map/ppermute | solution.py:953
  103.5 5.9 %collective-permute-start.8 = (bf16[32,768]{1,0:T(8,128)(2,1)S(1)}, bf16[32,768]{1,0:T(8,128)(2,1)S(1)}, u32[]{:S(2)}, u32[]{:S(2)}) collective-permute-start(bf16[32,768]{1,0:T(8,128)(2,1)S(1)} %get-tuple-element.154), channel_id=1, source_target_pairs={{0,3},{1,2},{2,1},{3,0},{4,7},{5,6},{6,5},{7,4},{8,11},{9,10},{10,... | collective-permute-start | bytes 147464 | tf_op jit(solution)/shard_map/ppermute | solution.py:958
  107.1 4.1 %collective-permute-start.7 = (bf16[32,768]{1,0:T(8,128)(2,1)S(1)}, bf16[32,768]{1,0:T(8,128)(2,1)S(1)}, u32[]{:S(2)}, u32[]{:S(2)}) collective-permute-start(bf16[32,768]{1,0:T(8,128)(2,1)S(1)} %get-tuple-element.154), channel_id=1, source_target_pairs={{0,2},{1,3},{2,0},{3,1},{4,6},{5,7},{6,4},{7,5},{8,10},{9,11},{10,... | collective-permute-start | bytes 147464 | tf_op jit(solution)/shard_map/ppermute | solution.py:958
  107.6 4.1 %collective-permute-start.6 = (bf16[32,768]{1,0:T(8,128)(2,1)S(1)}, bf16[32,768]{1,0:T(8,128)(2,1)S(1)}, u32[]{:S(2)}, u32[]{:S(2)}) collective-permute-start(bf16[32,768]{1,0:T(8,128)(2,1)S(1)} %get-tuple-element.154), channel_id=1, source_target_pairs={{0,1},{1,0},{2,3},{3,2},{4,5},{5,4},{6,7},{7,6},{8,9},{9,8},{10,11... | collective-permute-start | bytes 147464 | tf_op jit(solution)/shard_map/ppermute | solution.py:958
  111.8 8.9 %collective-permute-start.9 = (bf16[32,768]{1,0:T(8,128)(2,1)S(1)}, bf16[32,768]{1,0:T(8,128)(2,1)S(1)}, u32[]{:S(2)}, u32[]{:S(2)}) collective-permute-start(bf16[32,768]{1,0:T(8,128)(2,1)S(1)} %get-tuple-element.152), channel_id=1, source_target_pairs={{0,4},{1,5},{2,6},{3,7},{4,0},{5,1},{6,2},{7,3},{8,12},{9,13},{10,... | collective-permute-start | bytes 147464 | tf_op jit(solution)/shard_map/ppermute | solution.py:958
  113.4 7.3 %collective-permute-start.10 = (bf16[32,768]{1,0:T(8,128)(2,1)S(1)}, bf16[32,768]{1,0:T(8,128)(2,1)S(1)}, u32[]{:S(2)}, u32[]{:S(2)}) collective-permute-start(bf16[32,768]{1,0:T(8,128)(2,1)S(1)} %get-tuple-element.152), channel_id=1, source_target_pairs={{0,8},{1,9},{2,10},{3,11},{4,12},{5,13},{6,14},{7,15},{8,0},{9,1},... | collective-permute-start | bytes 147464 | tf_op jit(solution)/shard_map/ppermute | solution.py:958
  116.0 5.9 %collective-permute-start.11 = (bf16[32,768]{1,0:T(8,128)(2,1)S(1)}, bf16[32,768]{1,0:T(8,128)(2,1)S(1)}, u32[]{:S(2)}, u32[]{:S(2)}) collective-permute-start(bf16[32,768]{1,0:T(8,128)(2,1)S(1)} %get-tuple-element.152), channel_id=1, source_target_pairs={{0,12},{1,13},{2,14},{3,15},{4,8},{5,9},{6,10},{7,11},{8,4},{9,5},... | collective-permute-start | bytes 147464 | tf_op jit(solution)/shard_map/ppermute | solution.py:958
  116.2 5.8 %copy-start.2 = (s32[2,2,2]{2,1,0:T(2,128)S(1)}, s32[2,2,2]{2,1,0:T(2,128)}, u32[]{:S(2)}) copy-start(s32[2,2,2]{2,1,0:T(2,128)} %param.21) | copy-start | bytes 100
  121.9 1.4 %collective-permute-start.12 = (f32[32,768]{1,0:T(8,128)S(1)}, f32[32,768]{1,0:T(8,128)S(1)}, u32[]{:S(2)}, u32[]{:S(2)}) collective-permute-start(f32[32,768]{1,0:T(8,128)S(1)} %add_add_fusion.mine_ref), channel_id=1, source_target_pairs={{0,16},{16,0},{1,17},{17,1},{2,18},{18,2},{3,19},{19,3},{4,20},{20... | collective-permute-start | bytes 294920 | tf_op jit(solution)/shard_map/ppermute | solution.py:967
